TPU v7x, 512 devices: a whole 4x8x8 slice. The times are simulated.
512 devices in a mesh: sec: 2 (over core), lat: 4 (over z_hi), lon: 64 (over x, y, z_lo).
Axes of the slice: x: 4, y: 8, z: 8 (z_hi: 4, z_lo: 2; z = z_hi * 2 + z_lo), core: 2. Of those that a mesh axis runs over, the one named last changes fastest.
Arguments:
- adjoint: float32 [2, 4, 4, 128, 8192], P('sec', None, None, 'lat', 'lon'), may hold values from -6 to 6
- diffusivity: float32 [2, 4, 128, 8192], P('sec', None, 'lat', 'lon'), may hold values from 0.02 to 0.2
- velocity: float32 [2, 2, 4, 128, 8192], P('sec', None, None, 'lat', 'lon'), may hold values from -0.4 to 0.4
- sensitivity: float32 [2, 4, 4], P('sec'), may hold values from -3 to 3
- sea_mask: int32 [2, 128, 8192], P('sec', 'lat', 'lon'), may hold values 0 or 1
- coast_distance: int32 [2, 128, 8192], P('sec', 'lat', 'lon'), may hold values from 0 to 31
- send_cells: int32 [2, 4, 192, 1024], P('sec', 'lat', 'lon'), may hold values from 0 to 4095
- recv_slots: int32 [2, 4, 128, 8192], P('sec', None, 'lat', 'lon'), may hold values from 0 to 3071
- regrid_weight: float32 [2, 4, 128, 8192], P('sec', None, 'lat', 'lon'), may hold values from 0.1 to 0.5
Outputs:
- adjoint_out: float32 [2, 4, 4, 128, 8192], P('sec', None, None, 'lat', 'lon')
Inputs may be any that keep to these rules, and one draw needn't show every extreme that they name: `send_cells`: a cell number of the sending tile. `recv_slots`: an entry of the 3072 received entries, source tile major, west source first.
All inputs are finite; a program needn't handle non-finite values. No bound on the sum of `sea_mask` on one device may be relied on, other than what follows from the above.
Results may differ from a plain program's by a relative error of at most 0.0003.
Values sent between devices are 32-bit elements; how exact they have to be, the bound alone decides.
No kernel may reach another device: no remote copies, remote signals or barrier semaphores. Data moves between devices by JAX's collectives and lax.ppermute only.
A program may use at most 64 MiB of HBM per device.

v0:
```python
import jax
import jax.numpy as jnp
from jax import lax
from jax.sharding import PartitionSpec as P

COMP = 4
TERMS = 4
STEPS = 2


def padded_2(block, sides, width, periodic):
    for axis, dim in sides:
        count = lax.axis_size(axis)
        forward = [(i, i + 1) for i in range(count - 1)]
        if periodic:
            forward.append((count - 1, 0))
        backward = [(target, source) for source, target in forward]
        low = lax.ppermute(
            lax.slice_in_dim(block, block.shape[dim] - width, None, axis=dim), axis, forward
        )
        high = lax.ppermute(lax.slice_in_dim(block, 0, width, axis=dim), axis, backward)
        block = jnp.concatenate([low, block, high], axis=dim)
    return block


def shifted(value, axis, steps):
    count = lax.axis_size(axis)
    pairs = [(source, (source + steps) % count) for source in range(count)]
    return lax.ppermute(value, axis, pairs)


def partner(block, axis, stride):
    count = lax.axis_size(axis)
    route = []
    for low in range(count):
        high = low | 1 << stride
        if high != low and high < count:
            route += [(low, high), (high, low)]
    return lax.ppermute(block, axis, route)


def widen_rims(array):
    across = padded_2(array, (("lon", 3),), 1, True)
    return padded_2(across, (("lat", 2),), 1, False)


def sweep_once(field, coef_padded):
    padded = widen_rims(field)
    diffused = coef_padded[0:1] * padded
    carried_x = coef_padded[1:2] * padded
    carried_y = coef_padded[2:3] * padded
    centre = diffused[..., 1:-1, 1:-1]
    laplace = (
        diffused[..., 2:, 1:-1]
        + diffused[..., :-2, 1:-1]
        + diffused[..., 1:-1, 2:]
        + diffused[..., 1:-1, :-2]
        - 4.0 * centre
    )
    advect = 0.5 * (carried_x[..., 1:-1, 2:] - carried_x[..., 1:-1, :-2]) + 0.5 * (
        carried_y[..., 2:, 1:-1] - carried_y[..., :-2, 1:-1]
    )
    return field + laplace + advect


def couple(field, sensitivity, weight_sea, send_list, slot_list, weight_list):
    surface = field[:, 0]
    fluxes = []
    for which in range(COMP):
        total = jnp.zeros(surface.shape[1:], jnp.float32)
        for other in range(COMP):
            total = total + sensitivity[which, other] * surface[other]
        fluxes.append(weight_sea * total)
    flux = jnp.stack(fluxes, axis=0).reshape(COMP, -1)
    peers = send_list.shape[0]
    packed = jnp.take(flux, send_list.reshape(-1), axis=1).reshape(COMP, peers, send_list.shape[1])
    arrived = []
    for offset in (1, -1):
        arrived.append(shifted(packed[:, 1 + offset], "lon", offset))
    routed = jnp.stack([arrived[0], packed[:, 1], arrived[1]], axis=1)
    received = partner(routed, "sec", 0).reshape(COMP, -1)
    cells = slot_list.shape[1]
    picked_all = jnp.take(received, slot_list.reshape(-1), axis=1).reshape(COMP, TERMS, cells)
    total = jnp.zeros((COMP, cells), jnp.float32)
    for which in range(TERMS):
        total = total + weight_list[which][None, :] * picked_all[:, which]
    return total.reshape(surface.shape)


def on_device(
    adjoint,
    diffusivity,
    velocity,
    sensitivity,
    sea_mask,
    coast_distance,
    send_cells,
    recv_slots,
    regrid_weight,
):
    field = adjoint[0]
    distance = coast_distance[0].astype(jnp.float32)
    blend = (distance + 1.0) / (distance + 9.0)
    weight_sea = sea_mask[0].astype(jnp.float32) * blend
    coefficients = jnp.concatenate([diffusivity[0][None], velocity[0]], axis=0)
    coef_padded = widen_rims(coefficients)
    send_list = send_cells[0, 0]
    slot_list = recv_slots[0].reshape(TERMS, -1)
    weight_list = regrid_weight[0].reshape(TERMS, -1)
    for step_index in range(STEPS):
        coupled = couple(field, sensitivity[0], weight_sea, send_list, slot_list, weight_list)
        field = sweep_once(field, coef_padded)
        field = field.at[:, 0].add(coupled)
    return field[None]


def solution(mesh):
    placed = (
        P("sec", None, None, "lat", "lon"),
        P("sec", None, "lat", "lon"),
        P("sec", None, None, "lat", "lon"),
        P("sec", None, None),
        P("sec", "lat", "lon"),
        P("sec", "lat", "lon"),
        P("sec", "lat", "lon", None),
        P("sec", None, "lat", "lon"),
        P("sec", None, "lat", "lon"),
    )
    return jax.shard_map(
        on_device,
        mesh=mesh,
        in_specs=placed,
        out_specs=P("sec", None, None, "lat", "lon"),
        check_vma=False,
    )
```

profile of v0, /device:TPU:1, one launch (start us, length us, event | category | flops | bytes accessed | tf_op | source)
XLA Modules:
  0.0 306.0 jit_solution(5409013942232679152)
XLA Ops:
  0.0 0.7 fusion.13
  0.7 0.7 compare_and_fusion.1
  1.4 2.0 fusion.20
  3.4 3.4 %bitcast_multiply_fusion.7 = (f32[1,32,128]{2,1,0:T(8,128)S(1)}, f32[1,32,128]{2,1,0:T(8,128)S(1)}) fusion(f32[4,4,32,128]{3,2,1,0:T(8,128)} %bitcast.99, f32[]{:T(128)} %bitcast.12, f32[]{:T(128)} %bitcast.11, f32[]{:T(128)} %bitcast.10, f32[]{:T(128)} %bitcast.9, s32[1,32,128]{2,1,0:T(8,128)} %param.22, s32[1,32,128]{2,1,0:T(8,128)} %param.21), kind=kLoop, calls=%fused_computation.69 | loop fusion | flops 57344 | bytes 131088 | tf_op jit(solution)/shard_map/mul | solution.py:73
  6.8 3.3 %bitcast_multiply_fusion.5 = f32[1,32,128]{2,1,0:T(8,128)S(1)} fusion(f32[1,32,128]{2,1,0:T(8,128)S(1)} %get-tuple-element.34, f32[4,4,32,128]{3,2,1,0:T(8,128)} %bitcast.100, f32[]{:T(128)} %bitcast.24, f32[]{:T(128)} %bitcast.23, f32[]{:T(128)} %bitcast.22, f32[]{:T(128)} %bitcast.21), kind=kLoop, calls=%fused_computation.67 | loop fusion | flops 32768 | bytes 98320 | tf_op jit(solution)/shard_map/mul | solution.py:73
  10.1 5.6 %bitcast_multiply_fusion.6 = (f32[1,32,128]{2,1,0:T(8,128)S(1)}, f32[1,32,128]{2,1,0:T(8,128)S(1)}) fusion(f32[1,32,128]{2,1,0:T(8,128)S(1)} %get-tuple-element.34, f32[4,4,32,128]{3,2,1,0:T(8,128)} %bitcast.101, f32[]{:T(128)} %bitcast.18, f32[]{:T(128)} %bitcast.17, f32[]{:T(128)} %bitcast.16, f32[]{:T(128)} %bitcast.15, f32[]{:T(128)} %bitcast.30, ...), kind=kLoop, calls=%fused_computation.68 | loop fusion | flops 65536 | bytes 114720 | tf_op jit(solution)/shard_map/mul | solution.py:73
  15.8 0.6 copy.46
  16.5 10.9 %gather_fusion = f32[3072,4]{1,0:T(8,128)} fusion(f32[4,4096]{0,1:T(8,128)S(1)} %copy.46, s32[3072]{0:T(1024)S(1)} %fusion.13), kind=kCustom, calls=%fused_computation.clone | custom fusion | bytes 110592 | tf_op jit(solution)/shard_map/jit(_take)/gather | solution.py:76
  27.4 2.7 broadcast_select_fusion.3
  30.4 4.8 %collective-permute-start.8 = (f32[4,1024]{1,0:T(4,128)S(1)}, f32[4,1024]{1,0:T(4,128)S(1)}, u32[]{:S(2)}, u32[]{:S(2)}) collective-permute-start(f32[4,1024]{1,0:T(4,128)S(1)} %bitcast.134), channel_id=1, source_target_pairs={{0,1},{1,2},{2,3},{3,4},{4,5},{5,6},{6,7},{7,8},{8,9},{9,10},{10,1... | collective-permute-start | bytes 49160 | tf_op jit(solution)/shard_map/ppermute | solution.py:29
  35.4 7.0 %collective-permute-start.9 = (f32[4,1024]{1,0:T(4,128)S(1)}, f32[4,1024]{1,0:T(4,128)S(1)}, u32[]{:S(2)}, u32[]{:S(2)}) collective-permute-start(f32[4,1024]{1,0:T(4,128)S(1)} %bitcast.135), channel_id=1, source_target_pairs={{0,63},{1,0},{2,1},{3,2},{4,3},{5,4},{6,5},{7,6},{8,7},{9,8},{10,9... | collective-permute-start | bytes 49160 | tf_op jit(solution)/shard_map/ppermute | solution.py:29
  42.6 1.9 collective-permute-start
  44.5 7.6 %collective-permute-start.1 = (f32[3,4,32,1]{3,2,1,0:T(8,128)S(1)}, f32[3,4,32,1]{3,2,1,0:T(8,128)S(1)}, u32[]{:S(2)}, u32[]{:S(2)}) collective-permute-start(f32[3,4,32,1]{3,2,1,0:T(8,128)S(1)} %get-tuple-element.71), channel_id=1, source_target_pairs={{1,0},{2,1},{3,2},{4,3},{5,4},{6,5},{7,6},{8,7},{9,8},{10,9},{11,1... | collective-permute-start | bytes 4616 | tf_op jit(solution)/shard_map/ppermute | solution.py:21
  52.3 1.9 collective-permute-start.4
  54.5 7.6 %collective-permute-start.5 = (f32[4,4,32,1]{3,2,1,0:T(8,128)S(1)}, f32[4,4,32,1]{3,2,1,0:T(8,128)S(1)}, u32[]{:S(2)}, u32[]{:S(2)}) collective-permute-start(f32[4,4,32,1]{3,2,1,0:T(8,128)S(1)} %get-tuple-element.69), channel_id=1, source_target_pairs={{1,0},{2,1},{3,2},{4,3},{5,4},{6,5},{7,6},{8,7},{9,8},{10,9},{11,1... | collective-permute-start | bytes 6152 | tf_op jit(solution)/shard_map/ppermute | solution.py:21
  62.2 5.8 %collective-permute-start.2 = (f32[3,4,1,130]{3,2,1,0:T(1,128)S(1)}, f32[3,4,1,130]{3,2,1,0:T(1,128)S(1)}, u32[]{:S(2)}, u32[]{:S(2)}) collective-permute-start(f32[3,4,1,130]{3,2,1,0:T(1,128)S(1)} %get-tuple-element.59), channel_id=1, source_target_pairs={{0,64},{64,128},{128,192},{1,65},{65,129},{129,193},{2,66},{66,130... | collective-permute-start | bytes 18728 | tf_op jit(solution)/shard_map/ppermute | solution.py:18
  68.1 1.3 collective-permute-start.3
  69.6 6.7 %collective-permute-start.6 = (f32[4,4,1,130]{3,2,1,0:T(1,128)S(1)}, f32[4,4,1,130]{3,2,1,0:T(1,128)S(1)}, u32[]{:S(2)}, u32[]{:S(2)}) collective-permute-start(f32[4,4,1,130]{3,2,1,0:T(1,128)S(1)} %get-tuple-element.57), channel_id=1, source_target_pairs={{0,64},{64,128},{128,192},{1,65},{65,129},{129,193},{2,66},{66,130... | collective-permute-start | bytes 24968 | tf_op jit(solution)/shard_map/ppermute | solution.py:18
  76.3 1.3 collective-permute-start.7
  77.9 5.0 %collective-permute-done.7 = f32[4,4,1,130]{3,2,1,0:T(1,128)S(1)} collective-permute-done((f32[4,4,1,130]{3,2,1,0:T(1,128)S(1)}, f32[4,4,1,130]{3,2,1,0:T(1,128)S(1)}, u32[]{:S(2)}, u32[]{:S(2)}) %collective-permute-start.7) | collective-permute-done | bytes 8352 | tf_op jit(solution)/shard_map/ppermute | solution.py:21
  83.4 5.7 %collective-permute-start.10 = (f32[4,3,1024]{2,0,1:T(4,128)S(1)}, f32[4,3,1024]{2,0,1:T(4,128)S(1)}, u32[]{:S(2)}, u32[]{:S(2)}) collective-permute-start(f32[4,3,1024]{2,0,1:T(4,128)S(1)} %pad_maximum_fusion.6), channel_id=1, source_target_pairs={{0,256},{256,0},{1,257},{257,1},{2,258},{258,2},{3,259},{259,3},{4... | collective-permute-start | bytes 147464 | tf_op jit(solution)/shard_map/ppermute | solution.py:39
  90.4 54.8 %gather_fusion.1 = f32[16384,4]{1,0:T(8,128)} fusion(f32[4,3072]{0,1:T(8,128)S(1)} %bitcast.106, s32[16384]{0:T(1024)S(1)} %fusion.12), kind=kCustom, calls=%fused_computation.1.clone | custom fusion | bytes 589824 | tf_op jit(solution)/shard_map/jit(_take)/gather | solution.py:83
  145.2 11.8 %broadcast_select_fusion.1 = f32[16384,4]{1,0:T(8,128)S(1)} fusion(f32[16384,4]{1,0:T(8,128)} %gather_fusion.1, pred[16384]{0:T(1024)(128)(4,1)S(1)} %compare_and_fusion), kind=kLoop, calls=%fused_computation.5 | loop fusion | flops 65536 | bytes 540672 | tf_op jit(solution)/shard_map/jit(_take)/select_n | solution.py:83
  157.0 2.8 fusion.15
  159.7 2.2 copy.65
  161.9 2.2 copy.66
  164.2 2.2 copy.67
  167.1 5.1 %bitcast_multiply_fusion.3 = (f32[1,32,128]{2,1,0:T(8,128)S(1)}, f32[1,32,128]{2,1,0:T(8,128)S(1)}) fusion(f32[1,32,128]{2,1,0:T(8,128)S(1)} %get-tuple-element.34, f32[4,1,32,128]{3,2,1,0:T(8,128)S(1)} %get-tuple-element.32, f32[]{:T(128)} %bitcast.12, f32[]{:T(128)} %bitcast.11, f32[]{:T(128)} %bitcast.10, f32[]{:T(128)} %bitcast.9, f32[]{:T(128)} %bitcast.24, ...), kind=kLoop, calls=%fused_computation.65 | loop fusion | flops 65536 | bytes 114720 | tf_op jit(solution)/shard_map/mul | solution.py:73
  172.2 4.9 %bitcast_multiply_fusion.2 = (f32[1,32,128]{2,1,0:T(8,128)S(1)}, f32[1,32,128]{2,1,0:T(8,128)S(1)}) fusion(f32[1,32,128]{2,1,0:T(8,128)S(1)} %get-tuple-element.34, f32[4,1,32,128]{3,2,1,0:T(8,128)S(1)} %get-tuple-element.32, f32[]{:T(128)} %bitcast.18, f32[]{:T(128)} %bitcast.17, f32[]{:T(128)} %bitcast.16, f32[]{:T(128)} %bitcast.15, f32[]{:T(128)} %bitcast.30, ...), kind=kLoop, calls=%fused_computation.64 | loop fusion | flops 65536 | bytes 114720 | tf_op jit(solution)/shard_map/mul | solution.py:73
  177.8 10.9 %gather_fusion.2 = f32[3072,4]{1,0:T(8,128)} fusion(f32[4,4096]{0,1:T(8,128)S(1)} %copy.55, s32[3072]{0:T(1024)S(1)} %fusion.13), kind=kCustom, calls=%fused_computation.2.clone | custom fusion | bytes 110592 | tf_op jit(solution)/shard_map/jit(_take)/gather | solution.py:76
  188.8 1.9 collective-permute-start.11
  190.7 7.6 %collective-permute-start.12 = (f32[4,4,32,1]{3,2,1,0:T(8,128)S(1)}, f32[4,4,32,1]{3,2,1,0:T(8,128)S(1)}, u32[]{:S(2)}, u32[]{:S(2)}) collective-permute-start(f32[4,4,32,1]{3,2,1,0:T(8,128)S(1)} %get-tuple-element.67), channel_id=1, source_target_pairs={{1,0},{2,1},{3,2},{4,3},{5,4},{6,5},{7,6},{8,7},{9,8},{10,9},{11,1... | collective-permute-start | bytes 6152 | tf_op jit(solution)/shard_map/ppermute | solution.py:21
  198.3 2.7 broadcast_select_fusion.2
  201.0 1.5 collective-permute-done.11
  202.5 1.1 collective-permute-done.12
  203.8 5.7 %collective-permute-start.13 = (f32[4,4,1,130]{3,2,1,0:T(1,128)S(1)}, f32[4,4,1,130]{3,2,1,0:T(1,128)S(1)}, u32[]{:S(2)}, u32[]{:S(2)}) collective-permute-start(f32[4,4,1,130]{3,2,1,0:T(1,128)S(1)} %get-tuple-element.55), channel_id=1, source_target_pairs={{0,64},{64,128},{128,192},{1,65},{65,129},{129,193},{2,66},{66,130... | collective-permute-start | bytes 24968 | tf_op jit(solution)/shard_map/ppermute | solution.py:18
  209.6 1.3 collective-permute-start.14
  211.2 2.5 collective-permute-start.15
  213.8 7.5 %collective-permute-start.16 = (f32[4,1024]{1,0:T(4,128)S(1)}, f32[4,1024]{1,0:T(4,128)S(1)}, u32[]{:S(2)}, u32[]{:S(2)}) collective-permute-start(f32[4,1024]{1,0:T(4,128)S(1)} %bitcast.137), channel_id=1, source_target_pairs={{0,63},{1,0},{2,1},{3,2},{4,3},{5,4},{6,5},{7,6},{8,7},{9,8},{10,9... | collective-permute-start | bytes 49160 | tf_op jit(solution)/shard_map/ppermute | solution.py:29
  222.2 4.8 %collective-permute-start.17 = (f32[4,3,1024]{2,0,1:T(4,128)S(1)}, f32[4,3,1024]{2,0,1:T(4,128)S(1)}, u32[]{:S(2)}, u32[]{:S(2)}) collective-permute-start(f32[4,3,1024]{2,0,1:T(4,128)S(1)} %pad_maximum_fusion.7), channel_id=1, source_target_pairs={{0,256},{256,0},{1,257},{257,1},{2,258},{258,2},{3,259},{259,3},{4... | collective-permute-start | bytes 147464 | tf_op jit(solution)/shard_map/ppermute | solution.py:39
  227.5 0.7 copy.80
  228.7 54.8 %gather_fusion.3 = f32[16384,4]{1,0:T(8,128)} fusion(f32[4,3072]{0,1:T(8,128)S(1)} %bitcast.105, s32[16384]{0:T(1024)S(1)} %fusion.12), kind=kCustom, calls=%fused_computation.3.clone | custom fusion | bytes 589824 | tf_op jit(solution)/shard_map/jit(_take)/gather | solution.py:83
  283.5 11.8 %broadcast_select_fusion = f32[16384,4]{1,0:T(8,128)S(1)} fusion(f32[16384,4]{1,0:T(8,128)} %gather_fusion.3, pred[16384]{0:T(1024)(128)(4,1)S(1)} %compare_and_fusion), kind=kLoop, calls=%fused_computation.4 | loop fusion | flops 65536 | bytes 540672 | tf_op jit(solution)/shard_map/jit(_take)/select_n | solution.py:83
  295.2 2.8 fusion.14
  298.0 2.2 copy.69
  300.2 2.2 copy.70
  302.4 2.2 copy.71
  305.3 0.7 fusion.11
  (58 shorter events, 8.1 us)
Async XLA Ops:
  30.1 12.4 %copy-start.1 = (f32[1,2,4,32,128]{4,3,2,1,0:T(8,128)S(1)}, f32[1,2,4,32,128]{4,3,2,1,0:T(8,128)}, u32[]{:S(2)}) copy-start(f32[1,2,4,32,128]{4,3,2,1,0:T(8,128)} %param.19) | copy-start | bytes 393220
  30.1 12.4 %copy-start.2 = (f32[1,4,32,128]{3,2,1,0:T(8,128)S(1)}, f32[1,4,32,128]{3,2,1,0:T(8,128)}, u32[]{:S(2)}) copy-start(f32[1,4,32,128]{3,2,1,0:T(8,128)} %param.18) | copy-start | bytes 196612
  30.1 22.0 %copy-start = (f32[1,4,4,32,128]{4,3,2,1,0:T(8,128)S(1)}, f32[1,4,4,32,128]{4,3,2,1,0:T(8,128)}, u32[]{:S(2)}) copy-start(f32[1,4,4,32,128]{4,3,2,1,0:T(8,128)} %param.17) | copy-start | bytes 786436
  30.2 24.0 %copy-start.3 = (s32[1,4,32,128]{3,2,1,0:T(8,128)S(1)}, s32[1,4,32,128]{3,2,1,0:T(8,128)}, u32[]{:S(2)}) copy-start(s32[1,4,32,128]{3,2,1,0:T(8,128)} %param.24) | copy-start | bytes 196612
  30.2 24.1 %copy-start.4 = (f32[1,4,32,128]{3,2,1,0:T(8,128)S(1)}, f32[1,4,32,128]{3,2,1,0:T(8,128)}, u32[]{:S(2)}) copy-start(f32[1,4,32,128]{3,2,1,0:T(8,128)} %param.25) | copy-start | bytes 196612
  30.4 52.9 %collective-permute-start.8 = (f32[4,1024]{1,0:T(4,128)S(1)}, f32[4,1024]{1,0:T(4,128)S(1)}, u32[]{:S(2)}, u32[]{:S(2)}) collective-permute-start(f32[4,1024]{1,0:T(4,128)S(1)} %bitcast.134), channel_id=1, source_target_pairs={{0,1},{1,2},{2,3},{3,4},{4,5},{5,6},{6,7},{7,8},{8,9},{9,10},{10,1... | collective-permute-start | bytes 49160 | tf_op jit(solution)/shard_map/ppermute | solution.py:29
  35.4 47.9 %collective-permute-start.9 = (f32[4,1024]{1,0:T(4,128)S(1)}, f32[4,1024]{1,0:T(4,128)S(1)}, u32[]{:S(2)}, u32[]{:S(2)}) collective-permute-start(f32[4,1024]{1,0:T(4,128)S(1)} %bitcast.135), channel_id=1, source_target_pairs={{0,63},{1,0},{2,1},{3,2},{4,3},{5,4},{6,5},{7,6},{8,7},{9,8},{10,9... | collective-permute-start | bytes 49160 | tf_op jit(solution)/shard_map/ppermute | solution.py:29
  42.6 11.9 %collective-permute-start = (f32[3,4,32,1]{3,2,1,0:T(8,128)S(1)}, f32[3,4,32,1]{3,2,1,0:T(8,128)S(1)}, u32[]{:S(2)}, u32[]{:S(2)}) collective-permute-start(f32[3,4,32,1]{3,2,1,0:T(8,128)S(1)} %get-tuple-element.70), channel_id=1, source_target_pairs={{0,1},{1,2},{2,3},{3,4},{4,5},{5,6},{6,7},{7,8},{8,9},{9,10},{10,1... | collective-permute-start | bytes 4616 | tf_op jit(solution)/shard_map/ppermute | solution.py:18
  44.5 17.5 %collective-permute-start.1 = (f32[3,4,32,1]{3,2,1,0:T(8,128)S(1)}, f32[3,4,32,1]{3,2,1,0:T(8,128)S(1)}, u32[]{:S(2)}, u32[]{:S(2)}) collective-permute-start(f32[3,4,32,1]{3,2,1,0:T(8,128)S(1)} %get-tuple-element.71), channel_id=1, source_target_pairs={{1,0},{2,1},{3,2},{4,3},{5,4},{6,5},{7,6},{8,7},{9,8},{10,9},{11,1... | collective-permute-start | bytes 4616 | tf_op jit(solution)/shard_map/ppermute | solution.py:21
  52.3 15.8 %collective-permute-start.4 = (f32[4,4,32,1]{3,2,1,0:T(8,128)S(1)}, f32[4,4,32,1]{3,2,1,0:T(8,128)S(1)}, u32[]{:S(2)}, u32[]{:S(2)}) collective-permute-start(f32[4,4,32,1]{3,2,1,0:T(8,128)S(1)} %get-tuple-element.68), channel_id=1, source_target_pairs={{0,1},{1,2},{2,3},{3,4},{4,5},{5,6},{6,7},{7,8},{8,9},{9,10},{10,1... | collective-permute-start | bytes 6152 | tf_op jit(solution)/shard_map/ppermute | solution.py:18
  54.5 14.9 %collective-permute-start.5 = (f32[4,4,32,1]{3,2,1,0:T(8,128)S(1)}, f32[4,4,32,1]{3,2,1,0:T(8,128)S(1)}, u32[]{:S(2)}, u32[]{:S(2)}) collective-permute-start(f32[4,4,32,1]{3,2,1,0:T(8,128)S(1)} %get-tuple-element.69), channel_id=1, source_target_pairs={{1,0},{2,1},{3,2},{4,3},{5,4},{6,5},{7,6},{8,7},{9,8},{10,9},{11,1... | collective-permute-start | bytes 6152 | tf_op jit(solution)/shard_map/ppermute | solution.py:21
  62.2 14.1 %collective-permute-start.2 = (f32[3,4,1,130]{3,2,1,0:T(1,128)S(1)}, f32[3,4,1,130]{3,2,1,0:T(1,128)S(1)}, u32[]{:S(2)}, u32[]{:S(2)}) collective-permute-start(f32[3,4,1,130]{3,2,1,0:T(1,128)S(1)} %get-tuple-element.59), channel_id=1, source_target_pairs={{0,64},{64,128},{128,192},{1,65},{65,129},{129,193},{2,66},{66,130... | collective-permute-start | bytes 18728 | tf_op jit(solution)/shard_map/ppermute | solution.py:18
  68.1 9.6 %collective-permute-start.3 = (f32[3,4,1,130]{3,2,1,0:T(1,128)S(1)}, f32[3,4,1,130]{3,2,1,0:T(1,128)S(1)}, u32[]{:S(2)}, u32[]{:S(2)}) collective-permute-start(f32[3,4,1,130]{3,2,1,0:T(1,128)S(1)} %get-tuple-element.60), channel_id=1, source_target_pairs={{64,0},{128,64},{192,128},{65,1},{129,65},{193,129},{66,2},{130,66... | collective-permute-start | bytes 18728 | tf_op jit(solution)/shard_map/ppermute | solution.py:21
  69.6 8.4 %collective-permute-start.6 = (f32[4,4,1,130]{3,2,1,0:T(1,128)S(1)}, f32[4,4,1,130]{3,2,1,0:T(1,128)S(1)}, u32[]{:S(2)}, u32[]{:S(2)}) collective-permute-start(f32[4,4,1,130]{3,2,1,0:T(1,128)S(1)} %get-tuple-element.57), channel_id=1, source_target_pairs={{0,64},{64,128},{128,192},{1,65},{65,129},{129,193},{2,66},{66,130... | collective-permute-start | bytes 24968 | tf_op jit(solution)/shard_map/ppermute | solution.py:18
  76.3 6.6 %collective-permute-start.7 = (f32[4,4,1,130]{3,2,1,0:T(1,128)S(1)}, f32[4,4,1,130]{3,2,1,0:T(1,128)S(1)}, u32[]{:S(2)}, u32[]{:S(2)}) collective-permute-start(f32[4,4,1,130]{3,2,1,0:T(1,128)S(1)} %get-tuple-element.58), channel_id=1, source_target_pairs={{64,0},{128,64},{192,128},{65,1},{129,65},{193,129},{66,2},{130,66... | collective-permute-start | bytes 24968 | tf_op jit(solution)/shard_map/ppermute | solution.py:21
  83.4 6.6 %collective-permute-start.10 = (f32[4,3,1024]{2,0,1:T(4,128)S(1)}, f32[4,3,1024]{2,0,1:T(4,128)S(1)}, u32[]{:S(2)}, u32[]{:S(2)}) collective-permute-start(f32[4,3,1024]{2,0,1:T(4,128)S(1)} %pad_maximum_fusion.6), channel_id=1, source_target_pairs={{0,256},{256,0},{1,257},{257,1},{2,258},{258,2},{3,259},{259,3},{4... | collective-permute-start | bytes 147464 | tf_op jit(solution)/shard_map/ppermute | solution.py:39
  188.8 13.7 %collective-permute-start.11 = (f32[4,4,32,1]{3,2,1,0:T(8,128)S(1)}, f32[4,4,32,1]{3,2,1,0:T(8,128)S(1)}, u32[]{:S(2)}, u32[]{:S(2)}) collective-permute-start(f32[4,4,32,1]{3,2,1,0:T(8,128)S(1)} %get-tuple-element.66), channel_id=1, source_target_pairs={{0,1},{1,2},{2,3},{3,4},{4,5},{5,6},{6,7},{7,8},{8,9},{9,10},{10,1... | collective-permute-start | bytes 6152 | tf_op jit(solution)/shard_map/ppermute | solution.py:18
  190.7 12.9 %collective-permute-start.12 = (f32[4,4,32,1]{3,2,1,0:T(8,128)S(1)}, f32[4,4,32,1]{3,2,1,0:T(8,128)S(1)}, u32[]{:S(2)}, u32[]{:S(2)}) collective-permute-start(f32[4,4,32,1]{3,2,1,0:T(8,128)S(1)} %get-tuple-element.67), channel_id=1, source_target_pairs={{1,0},{2,1},{3,2},{4,3},{5,4},{6,5},{7,6},{8,7},{9,8},{10,9},{11,1... | collective-permute-start | bytes 6152 | tf_op jit(solution)/shard_map/ppermute | solution.py:21
  203.8 17.7 %collective-permute-start.13 = (f32[4,4,1,130]{3,2,1,0:T(1,128)S(1)}, f32[4,4,1,130]{3,2,1,0:T(1,128)S(1)}, u32[]{:S(2)}, u32[]{:S(2)}) collective-permute-start(f32[4,4,1,130]{3,2,1,0:T(1,128)S(1)} %get-tuple-element.55), channel_id=1, source_target_pairs={{0,64},{64,128},{128,192},{1,65},{65,129},{129,193},{2,66},{66,130... | collective-permute-start | bytes 24968 | tf_op jit(solution)/shard_map/ppermute | solution.py:18
  209.6 11.9 %collective-permute-start.14 = (f32[4,4,1,130]{3,2,1,0:T(1,128)S(1)}, f32[4,4,1,130]{3,2,1,0:T(1,128)S(1)}, u32[]{:S(2)}, u32[]{:S(2)}) collective-permute-start(f32[4,4,1,130]{3,2,1,0:T(1,128)S(1)} %get-tuple-element.56), channel_id=1, source_target_pairs={{64,0},{128,64},{192,128},{65,1},{129,65},{193,129},{66,2},{130,66... | collective-permute-start | bytes 24968 | tf_op jit(solution)/shard_map/ppermute | solution.py:21
  211.2 10.8 %collective-permute-start.15 = (f32[4,1024]{1,0:T(4,128)S(1)}, f32[4,1024]{1,0:T(4,128)S(1)}, u32[]{:S(2)}, u32[]{:S(2)}) collective-permute-start(f32[4,1024]{1,0:T(4,128)S(1)} %bitcast.136), channel_id=1, source_target_pairs={{0,1},{1,2},{2,3},{3,4},{4,5},{5,6},{6,7},{7,8},{8,9},{9,10},{10,1... | collective-permute-start | bytes 49160 | tf_op jit(solution)/shard_map/ppermute | solution.py:29
  213.8 8.3 %collective-permute-start.16 = (f32[4,1024]{1,0:T(4,128)S(1)}, f32[4,1024]{1,0:T(4,128)S(1)}, u32[]{:S(2)}, u32[]{:S(2)}) collective-permute-start(f32[4,1024]{1,0:T(4,128)S(1)} %bitcast.137), channel_id=1, source_target_pairs={{0,63},{1,0},{2,1},{3,2},{4,3},{5,4},{6,5},{7,6},{8,7},{9,8},{10,9... | collective-permute-start | bytes 49160 | tf_op jit(solution)/shard_map/ppermute | solution.py:29
  222.2 6.0 %collective-permute-start.17 = (f32[4,3,1024]{2,0,1:T(4,128)S(1)}, f32[4,3,1024]{2,0,1:T(4,128)S(1)}, u32[]{:S(2)}, u32[]{:S(2)}) collective-permute-start(f32[4,3,1024]{2,0,1:T(4,128)S(1)} %pad_maximum_fusion.7), channel_id=1, source_target_pairs={{0,256},{256,0},{1,257},{257,1},{2,258},{258,2},{3,259},{259,3},{4... | collective-permute-start | bytes 147464 | tf_op jit(solution)/shard_map/ppermute | solution.py:39
where the time goes:
time: 308 us; the launch traced here: 306 us
  local copies, waits for them, and re-layouts  158 us (51%)
  starting transfers between devices  82.9 us (27%)
  other arithmetic  56.3 us (18%)
  waiting for transfers between devices  8.13 us (3%)
    gather x2, local copies, waits for them, and re-layouts, couple(): jnp.take(received, slot_list.reshape(-1), axis=1)  110 us
    ppermute x6, starting transfers between devices, padded_2(): lax.ppermute(lax.slice_in_dim(block, 0, width, axis=dim), axis, backward)  26.6 us
    ppermute x6, starting transfers between devices, padded_2(): lax.ppermute(lax.slice_in_dim(block, block.shape[dim] - width, None, axis...  24.1 us
    select_n x2, other arithmetic, couple(): jnp.take(received, slot_list.reshape(-1), axis=1)  23.5 us
    mul x5, other arithmetic, couple(): fluxes.append(weight_sea * total)  22.3 us
    gather x2, local copies, waits for them, and re-layouts, couple(): jnp.take(flux, send_list.reshape(-1), axis=1)  21.8 us
    ppermute x4, starting transfers between devices, shifted(): return lax.ppermute(value, axis, pairs)  21.8 us
    squeeze x8, local copies, waits for them, and re-layouts, couple(): total = total + weight_list[which][None, :] * picked_all[:, which]  14.6 us
  transfers between devices with their start and end apart: 18, of which 5 were waited for; matrix products, arithmetic and copies ran while one was open for 2% of the time, Pallas kernels for 0%

commit v1 on v0

v1 whole, which is shorter than its diff:
```python
import functools

import jax
import jax.numpy as jnp
from jax import lax
from jax.experimental import pallas as pl
from jax.experimental.pallas import tpu as pltpu
from jax.sharding import PartitionSpec as P

COMP = 4
LEV = 4
TERMS = 4
ROWS = 32
LANES = 128
BLOCKS = ROWS // 8
PEERS = 3
PLANES = COMP * LEV

LIST = 8 * COMP
SIDE = LIST + 8
KEEP = SIDE + PLANES
GIVE = KEEP + LIST


def lookup(rows, high, low):
    found = [jnp.zeros((8, LANES), jnp.float32) for _ in rows]
    for at in range(len(rows[0])):
        here = high == at
        for k in range(len(rows)):
            row = jnp.broadcast_to(rows[k][at](), (8, LANES))
            got = jnp.take_along_axis(row, low, axis=1, mode="promise_in_bounds")
            found[k] = jnp.where(here, got, found[k])
    return found


def outgoing(core, field, dif_ref, vel_ref, sens_ref, sea_ref, dist_ref, send_ref, flux_ref, keep_ref, give_ref):
    distance = dist_ref[...].astype(jnp.float32)
    blend = (distance + 1.0) / (distance + 9.0)
    weight = sea_ref[...].astype(jnp.float32) * blend
    surface = [field(k, 0) for k in range(COMP)]
    for k in range(COMP):
        total = sens_ref[k, 0] * surface[0]
        for j in range(1, COMP):
            total = total + sens_ref[k, j] * surface[j]
        flux_ref[k] = weight * total

    first = core == 0
    cells = []
    for d in range(PEERS):
        pieces = [send_ref[d : d + 1, LANES * i : LANES * (i + 1)] for i in range(8)]
        cells.append(jnp.concatenate(pieces, axis=0))
    east_west = (jnp.where(first, cells[2], cells[0]), jnp.where(first, cells[0], cells[2]), cells[1])
    table = [[functools.partial(lambda k, r: flux_ref[k, r : r + 1, :], k, r) for r in range(ROWS)] for k in range(COMP)]
    for which, cell in enumerate(east_west):
        found = lookup(table, cell >> 7, cell & (LANES - 1))
        for k in range(COMP):
            if which == 0:
                keep_ref[8 * k : 8 * k + 8, :] = found[k]
            elif which == 1:
                give_ref[8 * k : 8 * k + 8, :] = found[k]
            else:
                give_ref[KEEP + 8 * k : KEEP + 8 * k + 8, :] = found[k]

    lane = lax.broadcasted_iota(jnp.int32, (8, LANES), 1)
    east = jnp.zeros((8, LANES), jnp.float32)
    west = jnp.zeros((8, LANES), jnp.float32)
    for level in range(LEV):
        dif = dif_ref[level]
        half_u = 0.5 * vel_ref[0, level]
        half_v = 0.5 * vel_ref[1, level]
        for k in range(COMP):
            plane = field(k, level)
            at = LEV * k + level
            to_east = (dif - half_u) * plane
            to_west = (dif + half_u) * plane
            for b in range(BLOCKS):
                here = lane == PLANES * b + at
                rows = slice(8 * b, 8 * b + 8)
                east = jnp.where(here, jnp.broadcast_to(to_east[rows, LANES - 1 :], (8, LANES)), east)
                west = jnp.where(here, jnp.broadcast_to(to_west[rows, :1], (8, LANES)), west)
            to_north = ((dif[24:] - half_v[24:]) * plane[24:])[7:8]
            to_south = ((dif[:8] + half_v[:8]) * plane[:8])[0:1]
            keep_ref[SIDE + at : SIDE + at + 1, :] = jnp.where(first, to_north, to_south)
            give_ref[SIDE + at : SIDE + at + 1, :] = jnp.where(first, to_south, to_north)
    keep_ref[LIST:SIDE, :] = jnp.where(first, east, west)
    give_ref[LIST:SIDE, :] = jnp.where(first, west, east)


def advance(core, field_ref, dif_ref, vel_ref, slot_ref, weight_ref, lon_ref, lat_ref, near_ref, back_ref, out_ref):
    first = core == 0
    def row_of(k, r):
        if r < 8:
            return lambda: lon_ref[SIDE + 8 * k + r : SIDE + 8 * k + r + 1, :]
        if r < 16:
            return lambda: near_ref[KEEP + 8 * k + r - 8 : KEEP + 8 * k + r - 7, :]
        return lambda: back_ref[8 * k + r - 16 : 8 * k + r - 15, :]

    table = [[row_of(k, r) for r in range(8 * PEERS)] for k in range(COMP)]
    kept_side = lon_ref[LIST:SIDE, :]
    passed_side = back_ref[LIST:SIDE, :]
    from_west = jnp.where(first, kept_side, passed_side)
    from_east = jnp.where(first, passed_side, kept_side)
    lane = lax.broadcasted_iota(jnp.int32, (8, LANES), 1)
    row = lax.broadcasted_iota(jnp.int32, (ROWS, LANES), 0)

    for level in range(LEV):
        dif = dif_ref[level]
        half_u = 0.5 * vel_ref[0, level]
        half_v = 0.5 * vel_ref[1, level]
        for k in range(COMP):
            at = LEV * k + level
            plane = field_ref[k, level]
            kept_row = lat_ref[at : at + 1, :]
            passed_row = back_ref[SIDE + at : SIDE + at + 1, :]
            south_row = jnp.where(first, kept_row, passed_row)
            north_row = jnp.where(first, passed_row, kept_row)
            east = pltpu.roll((dif + half_u) * plane, LANES - 1, 1)
            west = pltpu.roll((dif - half_u) * plane, 1, 1)
            north = pltpu.roll((dif + half_v) * plane, ROWS - 1, 0)
            south = pltpu.roll((dif - half_v) * plane, 1, 0)
            north = jnp.where(row == ROWS - 1, jnp.broadcast_to(north_row, (ROWS, LANES)), north)
            south = jnp.where(row == 0, jnp.broadcast_to(south_row, (ROWS, LANES)), south)
            centre = plane - 4.0 * (dif * plane) + (north + south)
            for b in range(BLOCKS):
                rows = slice(8 * b, 8 * b + 8)
                j = PLANES * b + at
                edge_east = jnp.broadcast_to(from_east[:, j : j + 1], (8, LANES))
                edge_west = jnp.broadcast_to(from_west[:, j : j + 1], (8, LANES))
                across = jnp.where(lane == LANES - 1, edge_east, east[rows]) + jnp.where(lane == 0, edge_west, west[rows])
                out_ref[k, level, rows, :] = centre[rows] + across

    for b in range(BLOCKS):
        rows = slice(8 * b, 8 * b + 8)
        total = [jnp.zeros((8, LANES), jnp.float32) for _ in range(COMP)]
        for t in range(TERMS):
            slot = slot_ref[t, rows, :]
            source = slot >> 10
            source = jnp.where(first, source, 2 - source)
            high = source * 8 + ((slot >> 7) & 7)
            found = lookup(table, high, slot & (LANES - 1))
            for k in range(COMP):
                total[k] = total[k] + weight_ref[t, rows, :] * found[k]
        for k in range(COMP):
            out_ref[k, 0, rows, :] = out_ref[k, 0, rows, :] + total[k]


def start_kernel(core_ref, sens_ref, field_ref, dif_ref, vel_ref, sea_ref, dist_ref, send_ref, keep_ref, give_ref, flux_ref):
    outgoing(
        core_ref[0], lambda k, l: field_ref[k, l], dif_ref, vel_ref, sens_ref, sea_ref, dist_ref, send_ref, flux_ref, keep_ref, give_ref
    )


def middle_kernel(
    core_ref, sens_ref, field_ref, dif_ref, vel_ref, sea_ref, dist_ref, send_ref, slot_ref, weight_ref,
    lon_ref, lat_ref, near_ref, back_ref, out_ref, keep_ref, give_ref, flux_ref,
):
    core = core_ref[0]
    advance(core, field_ref, dif_ref, vel_ref, slot_ref, weight_ref, lon_ref, lat_ref, near_ref, back_ref, out_ref)
    outgoing(
        core, lambda k, l: out_ref[k, l], dif_ref, vel_ref, sens_ref, sea_ref, dist_ref, send_ref, flux_ref, keep_ref, give_ref
    )


def last_kernel(
    core_ref, field_ref, dif_ref, vel_ref, slot_ref, weight_ref, lon_ref, lat_ref, near_ref, back_ref, out_ref
):
    advance(core_ref[0], field_ref, dif_ref, vel_ref, slot_ref, weight_ref, lon_ref, lat_ref, near_ref, back_ref, out_ref)


def call(kernel, scalars, arrays, outs, scratch=()):
    in_vmem = pl.BlockSpec(memory_space=pltpu.VMEM)
    in_smem = pl.BlockSpec(memory_space=pltpu.SMEM)
    return pl.pallas_call(
        kernel,
        out_shape=[jax.ShapeDtypeStruct(shape, jnp.float32) for shape in outs],
        in_specs=[in_smem] * len(scalars) + [in_vmem] * len(arrays),
        out_specs=[in_vmem] * len(outs),
        scratch_shapes=[pltpu.VMEM(shape, jnp.float32) for shape in scratch],
        compiler_params=pltpu.CompilerParams(vmem_limit_bytes=8 << 20),
    )(*scalars, *arrays)


def routes(axis):
    count = lax.axis_size(axis)
    periodic = axis == "lon"
    pairs = []
    for i in range(count):
        if periodic or i + 1 < count:
            pairs.append((i, (i + 1) % count))
        if periodic or i > 0:
            pairs.append((count + i, count + (i - 1) % count))
    return pairs


def exchange(keep, give):
    near = lax.ppermute(give, "sec", [(0, 1), (1, 0)])
    lon = jnp.concatenate([keep[:SIDE], near[:SIDE]], axis=0)
    lat = jnp.concatenate([keep[SIDE:], near[SIDE:KEEP]], axis=0)
    lon = lax.ppermute(lon, ("sec", "lon"), routes("lon"))
    lat = lax.ppermute(lat, ("sec", "lat"), routes("lat"))
    back = jnp.concatenate([lon[:LIST], lon[SIDE + LIST :], lat[PLANES:]], axis=0)
    back = lax.ppermute(back, "sec", [(0, 1), (1, 0)])
    return lon, lat, near, back


def on_device(
    adjoint,
    diffusivity,
    velocity,
    sensitivity,
    sea_mask,
    coast_distance,
    send_cells,
    recv_slots,
    regrid_weight,
):
    core = lax.axis_index("sec").astype(jnp.int32).reshape(1)
    field = adjoint[0]
    sens = sensitivity[0]
    dif, vel = diffusivity[0], velocity[0]
    send = (sea_mask[0], coast_distance[0], send_cells[0, 0])
    take = (recv_slots[0], regrid_weight[0])
    shape = field.shape
    flux = [(COMP, ROWS, LANES)]
    messages = [(KEEP, LANES), (GIVE, LANES)]
    keep, give = call(start_kernel, (core, sens), (field, dif, vel, *send), messages, flux)
    arrived = exchange(keep, give)
    field, keep, give = call(
        middle_kernel, (core, sens), (field, dif, vel, *send, *take, *arrived), [shape] + messages, flux
    )
    arrived = exchange(keep, give)
    (field,) = call(last_kernel, (core,), (field, dif, vel, *take, *arrived), [shape])
    return field[None]


def solution(mesh):
    placed = (
        P("sec", None, None, "lat", "lon"),
        P("sec", None, "lat", "lon"),
        P("sec", None, None, "lat", "lon"),
        P("sec", None, None),
        P("sec", "lat", "lon"),
        P("sec", "lat", "lon"),
        P("sec", "lat", "lon", None),
        P("sec", None, "lat", "lon"),
        P("sec", None, "lat", "lon"),
    )
    return jax.shard_map(
        on_device,
        mesh=mesh,
        in_specs=placed,
        out_specs=P("sec", None, None, "lat", "lon"),
        check_vma=False,
    )
```

time: 308 us -> 53.6 us (0.17)
  local copies, waits for them, and re-layouts: 158 us -> 5.46 us
  starting transfers between devices: 82.9 us -> 23.9 us
  other arithmetic: 56.3 us -> 0.02 us
  waiting for transfers between devices: 8.13 us -> 15.8 us
  Pallas kernels: 0 us -> 7.6 us
    gather x4 -> x0, local copies, waits for them, and re-layouts: 131 us -> none  [the longest x2 110 us: couple(): jnp.take(received, slot_list.reshape(-1), axis=1)]
    ppermute x18 -> x8, starting transfers between devices: 82.9 us -> 23.9 us  [the longest x2 10.9 us: exchange(): near = lax.ppermute(give, 'sec', [(0, 1), (1, 0)])]
    select_n x4 -> x0, other arithmetic: 28.9 us -> none  [the longest x2 23.5 us: couple(): jnp.take(received, slot_list.reshape(-1), axis=1)]
    mul x7 -> x0, other arithmetic: 23.1 us -> none  [the longest x5 22.3 us: couple(): fluxes.append(weight_sea * total)]
    squeeze x8 -> x0, local copies, waits for them, and re-layouts: 14.6 us -> none  [couple(): total = total + weight_list[which][None, :] * picked_all[:, which]]
    ppermute x18 -> x8, waiting for transfers between devices: 8.13 us -> 15.8 us  [the longest x2 11.7 us: exchange(): lat = lax.ppermute(lat, ('sec', 'lat'), routes('lat'))]
    pallas_call x0 -> x3, Pallas kernels: none -> 7.6 us  [call(): pl.pallas_call(kernel, out_shape=[jax.ShapeDtypeStruct(shape, jnp.float32...]
    slice x7 -> x15, local copies, waits for them, and re-layouts: 7.97 us -> 0.72 us  [the longest x3 0.69 us: exchange(): lat[PLANES:]]
  transfers between devices with their start and end apart: 18 -> 8, of which waited for: 5 -> 6; matrix products, arithmetic and copies ran while one was open for 2% -> 0% of each run, Pallas kernels for 0% -> 0%
where the time goes in v1:
time: 53.6 us; the launch traced here: 53 us
  starting transfers between devices  23.9 us (45%)
  waiting for transfers between devices  15.8 us (29%)
  Pallas kernels  7.6 us (14%)
  local copies, waits for them, and re-layouts  5.46 us (10%)
    ppermute x2, waiting for transfers between devices, exchange(): lat = lax.ppermute(lat, ('sec', 'lat'), routes('lat'))  11.7 us
    ppermute x2, starting transfers between devices, exchange(): near = lax.ppermute(give, 'sec', [(0, 1), (1, 0)])  10.9 us
    pallas_call x3, Pallas kernels, call(): pl.pallas_call(kernel, out_shape=[jax.ShapeDtypeStruct(shape, jnp.float32...  7.6 us
    ppermute x2, starting transfers between devices, exchange(): lon = lax.ppermute(lon, ('sec', 'lon'), routes('lon'))  6.36 us
    unnamed x27, local copies, waits for them, and re-layouts  4.73 us
    ppermute x2, starting transfers between devices, exchange(): back = lax.ppermute(back, 'sec', [(0, 1), (1, 0)])  4.01 us
    ppermute x2, starting transfers between devices, exchange(): lat = lax.ppermute(lat, ('sec', 'lat'), routes('lat'))  2.72 us
    ppermute x2, waiting for transfers between devices, exchange(): back = lax.ppermute(back, 'sec', [(0, 1), (1, 0)])  2.29 us
  transfers between devices with their start and end apart: 8, of which 6 were waited for; matrix products, arithmetic and copies ran while one was open for 0% of the time, Pallas kernels for 0%

profile of v1, /device:TPU:1, one launch (start us, length us, event | category | flops | bytes accessed | tf_op | source)
XLA Modules:
  0.0 53.0 jit_solution(11548101656000474324)
XLA Ops:
  0.0 0.0 copy-start.8
  0.0 0.0 copy-start.9
  0.0 0.7 %copy.12 = s32[1,1,3,1024]{3,2,1,0:T(4,128)S(1)} copy(s32[1,1,3,1024]{3,1,2,0:T(1,128)} %param.15) | data formatting | bytes 24576
  0.7 0.0 copy-start.12
  0.7 0.0 copy-done.8
  0.7 0.0 copy-done.9
  0.8 0.7 %copy-done.12 = f32[1,4,4]{2,1,0:T(4,128)S(1)} copy-done((f32[1,4,4]{2,1,0:T(4,128)S(1)}, f32[1,4,4]{2,1,0:T(4,128)}, u32[]{:S(2)}) %copy-start.12) | copy-done | bytes 88
  1.4 0.0 copy-start
  1.4 0.9 %copy-done = f32[1,2,4,32,128]{4,3,2,1,0:T(8,128)S(1)} copy-done((f32[1,2,4,32,128]{4,3,2,1,0:T(8,128)S(1)}, f32[1,2,4,32,128]{4,3,2,1,0:T(8,128)}, u32[]{:S(2)}) %copy-start) | copy-done | bytes 131096
  2.3 0.0 copy-start.2
  2.3 0.9 %copy-done.2 = f32[1,4,4,32,128]{4,3,2,1,0:T(8,128)S(1)} copy-done((f32[1,4,4,32,128]{4,3,2,1,0:T(8,128)S(1)}, f32[1,4,4,32,128]{4,3,2,1,0:T(8,128)}, u32[]{:S(2)}) %copy-start.2) | copy-done | bytes 262168
  3.3 0.0 copy-start.4
  3.3 0.8 %copy-done.4 = f32[1,4,32,128]{3,2,1,0:T(8,128)S(1)} copy-done((f32[1,4,32,128]{3,2,1,0:T(8,128)S(1)}, f32[1,4,32,128]{3,2,1,0:T(8,128)}, u32[]{:S(2)}) %copy-start.4) | copy-done | bytes 65560
  4.1 0.0 copy-start.3
  4.1 1.3 %shard_map.91 = (f32[56,128]{1,0:T(8,128)S(1)}, f32[88,128]{1,0:T(8,128)S(1)}) custom-call(s32[1]{0:T(128)} %bitcast.core_ref, f32[4,4]{1,0:T(4,128)S(1)} %bitcast.31, f32[4,4,32,128]{3,2,1,0:T(8,128)S(1)} %bitcast.16, f32[4,32,128]{2,1,0:T(8,128)S(1)} %bitcast.18, f32[2,4,32,128]{3,2,1,0:T(8,128)S(1)} %bitcast.13, s32[32,128]{1,0:T(8,128)S(1)} %bitcast.27, ...), custom_call_target="tpu_custom_call" | custom-call | tf_op jit(solution)/shard_map/pallas_call | solution.py:173
  5.4 8.8 %collective-permute-start = (f32[88,128]{1,0:T(8,128)S(1)}, f32[88,128]{1,0:T(8,128)S(1)}, u32[]{:S(2)}, u32[]{:S(2)}) collective-permute-start(f32[88,128]{1,0:T(8,128)S(1)} %get-tuple-element.11), channel_id=1, source_target_pairs={{0,256},{256,0},{1,257},{257,1},{2,258},{258,2},{3,259},{259,3},{4... | collective-permute-start | bytes 135176 | tf_op jit(solution)/shard_map/ppermute | solution.py:196
  14.2 0.0 copy-start.7
  14.2 0.8 %collective-permute-done.near_ref = f32[88,128]{1,0:T(8,128)S(1)} collective-permute-done((f32[88,128]{1,0:T(8,128)S(1)}, f32[88,128]{1,0:T(8,128)S(1)}, u32[]{:S(2)}, u32[]{:S(2)}) %collective-permute-start) | collective-permute-done | bytes 45088 | tf_op jit(solution)/shard_map/ppermute | solution.py:196
  15.0 0.0 copy-start.6
  15.1 0.0 copy-start.1
  15.1 3.9 %collective-permute-start.1 = (f32[80,128]{1,0:T(8,128)S(1)}, f32[80,128]{1,0:T(8,128)S(1)}, u32[]{:S(2)}, u32[]{:S(2)}) collective-permute-start(f32[80,128]{1,0:T(8,128)S(1)} %pad_maximum_fusion), channel_id=1, source_target_pairs={{0,1},{256,319},{1,2},{257,256},{2,3},{258,257},{3,4},{259,258},{4... | collective-permute-start | bytes 122888 | tf_op jit(solution)/shard_map/ppermute | solution.py:199
  18.9 0.0 copy-start.5
  19.0 1.4 %collective-permute-start.2 = (f32[32,128]{1,0:T(8,128)S(1)}, f32[32,128]{1,0:T(8,128)S(1)}, u32[]{:S(2)}, u32[]{:S(2)}) collective-permute-start(f32[32,128]{1,0:T(8,128)S(1)} %pad_maximum_fusion.4), channel_id=1, source_target_pairs={{0,64},{64,128},{320,256},{128,192},{384,320},{448,384},{1,65},{65... | collective-permute-start | bytes 49160 | tf_op jit(solution)/shard_map/ppermute | solution.py:200
  20.4 5.6 %collective-permute-done.2.lat_ref = f32[32,128]{1,0:T(8,128)S(1)} collective-permute-done((f32[32,128]{1,0:T(8,128)S(1)}, f32[32,128]{1,0:T(8,128)S(1)}, u32[]{:S(2)}, u32[]{:S(2)}) %collective-permute-start.2) | collective-permute-done | bytes 16416 | tf_op jit(solution)/shard_map/ppermute | solution.py:200
  26.0 0.0 collective-permute-done.1.lon_ref
  26.0 1.9 %collective-permute-start.3 = (f32[56,128]{1,0:T(8,128)S(1)}, f32[56,128]{1,0:T(8,128)S(1)}, u32[]{:S(2)}, u32[]{:S(2)}) collective-permute-start(f32[56,128]{1,0:T(8,128)S(1)} %pad_maximum_fusion.2), channel_id=1, source_target_pairs={{0,256},{256,0},{1,257},{257,1},{2,258},{258,2},{3,259},{259,3},{4... | collective-permute-start | bytes 86024 | tf_op jit(solution)/shard_map/ppermute | solution.py:202
  28.0 1.2 %collective-permute-done.3.back_ref = f32[56,128]{1,0:T(8,128)S(1)} collective-permute-done((f32[56,128]{1,0:T(8,128)S(1)}, f32[56,128]{1,0:T(8,128)S(1)}, u32[]{:S(2)}, u32[]{:S(2)}) %collective-permute-start.3) | collective-permute-done | bytes 28704 | tf_op jit(solution)/shard_map/ppermute | solution.py:202
  29.1 0.0 copy-done.3
  29.1 0.0 copy-done.7
  29.2 0.0 copy-done.6
  29.2 0.0 copy-done.1
  29.2 0.0 copy-done.5
  29.2 3.4 %shard_map.92 = (f32[4,4,32,128]{3,2,1,0:T(8,128)S(1)}, f32[56,128]{1,0:T(8,128)S(1)}, f32[88,128]{1,0:T(8,128)S(1)}) custom-call(s32[1]{0:T(128)} %bitcast.core_ref, f32[4,4]{1,0:T(4,128)S(1)} %bitcast.32, f32[4,4,32,128]{3,2,1,0:T(8,128)S(1)} %bitcast.17, f32[4,32,128]{2,1,0:T(8,128)S(1)} %bitcast.19, f32[2,4,32,128]{3,2,1,0:T(8,128)S(1)} %bitcast.14, ...), custom_call_target="tpu_custom_call" | custom-call | tf_op jit(solution)/shard_map/pallas_call | solution.py:173
  32.6 2.1 %collective-permute-start.4 = (f32[88,128]{1,0:T(8,128)S(1)}, f32[88,128]{1,0:T(8,128)S(1)}, u32[]{:S(2)}, u32[]{:S(2)}) collective-permute-start(f32[88,128]{1,0:T(8,128)S(1)} %get-tuple-element.14), channel_id=1, source_target_pairs={{0,256},{256,0},{1,257},{257,1},{2,258},{258,2},{3,259},{259,3},{4... | collective-permute-start | bytes 135176 | tf_op jit(solution)/shard_map/ppermute | solution.py:196
  34.7 1.0 %collective-permute-done.4.near_ref = f32[88,128]{1,0:T(8,128)S(1)} collective-permute-done((f32[88,128]{1,0:T(8,128)S(1)}, f32[88,128]{1,0:T(8,128)S(1)}, u32[]{:S(2)}, u32[]{:S(2)}) %collective-permute-start.4) | collective-permute-done | bytes 45088 | tf_op jit(solution)/shard_map/ppermute | solution.py:196
  35.7 2.5 %collective-permute-start.5 = (f32[80,128]{1,0:T(8,128)S(1)}, f32[80,128]{1,0:T(8,128)S(1)}, u32[]{:S(2)}, u32[]{:S(2)}) collective-permute-start(f32[80,128]{1,0:T(8,128)S(1)} %pad_maximum_fusion.1), channel_id=1, source_target_pairs={{0,1},{256,319},{1,2},{257,256},{2,3},{258,257},{3,4},{259,258},{4... | collective-permute-start | bytes 122888 | tf_op jit(solution)/shard_map/ppermute | solution.py:199
  38.3 1.3 %collective-permute-start.6 = (f32[32,128]{1,0:T(8,128)S(1)}, f32[32,128]{1,0:T(8,128)S(1)}, u32[]{:S(2)}, u32[]{:S(2)}) collective-permute-start(f32[32,128]{1,0:T(8,128)S(1)} %pad_maximum_fusion.5), channel_id=1, source_target_pairs={{0,64},{64,128},{320,256},{128,192},{384,320},{448,384},{1,65},{65... | collective-permute-start | bytes 49160 | tf_op jit(solution)/shard_map/ppermute | solution.py:200
  39.6 6.0 %collective-permute-done.6.lat_ref = f32[32,128]{1,0:T(8,128)S(1)} collective-permute-done((f32[32,128]{1,0:T(8,128)S(1)}, f32[32,128]{1,0:T(8,128)S(1)}, u32[]{:S(2)}, u32[]{:S(2)}) %collective-permute-start.6) | collective-permute-done | bytes 16416 | tf_op jit(solution)/shard_map/ppermute | solution.py:200
  45.6 0.0 copy-start.10
  45.6 0.6 %copy-done.10 = f32[32,128]{1,0:T(8,128)} copy-done((f32[32,128]{1,0:T(8,128)}, f32[32,128]{1,0:T(8,128)S(1)}, u32[]{:S(2)}) %copy-start.10) | copy-done | bytes 16408
  46.2 0.0 collective-permute-done.5.lon_ref
  46.2 0.0 slice-start
  46.2 0.7 %slice-done = f32[16,128]{1,0:T(8,128)S(1)} async-done(((f32[32,128]{1,0:T(8,128)}), f32[16,128]{1,0:T(8,128)S(1)}, s32[]{:S(2)}) %slice-start) | async-done | bytes 8216 | tf_op jit(solution)/shard_map/slice | solution.py:201
  46.9 0.0 copy-start.11
  46.9 2.1 %collective-permute-start.7 = (f32[56,128]{1,0:T(8,128)S(1)}, f32[56,128]{1,0:T(8,128)S(1)}, u32[]{:S(2)}, u32[]{:S(2)}) collective-permute-start(f32[56,128]{1,0:T(8,128)S(1)} %pad_maximum_fusion.3), channel_id=1, source_target_pairs={{0,256},{256,0},{1,257},{257,1},{2,258},{258,2},{3,259},{259,3},{4... | collective-permute-start | bytes 86024 | tf_op jit(solution)/shard_map/ppermute | solution.py:202
  49.0 1.1 %collective-permute-done.7.back_ref = f32[56,128]{1,0:T(8,128)S(1)} collective-permute-done((f32[56,128]{1,0:T(8,128)S(1)}, f32[56,128]{1,0:T(8,128)S(1)}, u32[]{:S(2)}, u32[]{:S(2)}) %collective-permute-start.7) | collective-permute-done | bytes 28704 | tf_op jit(solution)/shard_map/ppermute | solution.py:202
  50.1 0.0 copy-done.11
  50.1 2.9 %shard_map.93 = f32[4,4,32,128]{3,2,1,0:T(8,128)} custom-call(s32[1]{0:T(128)} %bitcast.core_ref, f32[4,4,32,128]{3,2,1,0:T(8,128)S(1)} %get-tuple-element.12.field_ref, f32[4,32,128]{2,1,0:T(8,128)S(1)} %bitcast.20, f32[2,4,32,128]{3,2,1,0:T(8,128)S(1)} %bitcast.15, s32[4,32,128]{2,1,0:T(8,128)S(1)} %bitcast.22, f32[4,32,128]{2,1,0:T(8,128)S(1)} %bitcast.24, ...), custom_call_target="tpu_custom_call" | custom-call | tf_op jit(solution)/shard_map/pallas_call | solution.py:173
  (19 shorter events, 0.1 us)
Async XLA Ops:
  0.0 0.7 %copy-start.8 = (s32[1,32,128]{2,1,0:T(8,128)S(1)}, s32[1,32,128]{2,1,0:T(8,128)}, u32[]{:S(2)}) copy-start(s32[1,32,128]{2,1,0:T(8,128)} %param.13) | copy-start | bytes 49156
  0.0 0.7 %copy-start.9 = (s32[1,32,128]{2,1,0:T(8,128)S(1)}, s32[1,32,128]{2,1,0:T(8,128)}, u32[]{:S(2)}) copy-start(s32[1,32,128]{2,1,0:T(8,128)} %param.14) | copy-start | bytes 49156
  0.7 0.7 %copy-start.12 = (f32[1,4,4]{2,1,0:T(4,128)S(1)}, f32[1,4,4]{2,1,0:T(4,128)}, u32[]{:S(2)}) copy-start(f32[1,4,4]{2,1,0:T(4,128)} %param.12) | copy-start | bytes 196
  1.4 0.9 %copy-start = (f32[1,2,4,32,128]{4,3,2,1,0:T(8,128)S(1)}, f32[1,2,4,32,128]{4,3,2,1,0:T(8,128)}, u32[]{:S(2)}) copy-start(f32[1,2,4,32,128]{4,3,2,1,0:T(8,128)} %param.11) | copy-start | bytes 393220
  2.3 0.9 %copy-start.2 = (f32[1,4,4,32,128]{4,3,2,1,0:T(8,128)S(1)}, f32[1,4,4,32,128]{4,3,2,1,0:T(8,128)}, u32[]{:S(2)}) copy-start(f32[1,4,4,32,128]{4,3,2,1,0:T(8,128)} %param.9) | copy-start | bytes 786436
  3.3 0.8 %copy-start.4 = (f32[1,4,32,128]{3,2,1,0:T(8,128)S(1)}, f32[1,4,32,128]{3,2,1,0:T(8,128)}, u32[]{:S(2)}) copy-start(f32[1,4,32,128]{3,2,1,0:T(8,128)} %param.10) | copy-start | bytes 196612
  4.1 25.0 %copy-start.3 = (f32[1,4,4,32,128]{4,3,2,1,0:T(8,128)S(1)}, f32[1,4,4,32,128]{4,3,2,1,0:T(8,128)}, u32[]{:S(2)}) copy-start(f32[1,4,4,32,128]{4,3,2,1,0:T(8,128)} %param.9) | copy-start | bytes 786436
  5.4 9.6 %collective-permute-start = (f32[88,128]{1,0:T(8,128)S(1)}, f32[88,128]{1,0:T(8,128)S(1)}, u32[]{:S(2)}, u32[]{:S(2)}) collective-permute-start(f32[88,128]{1,0:T(8,128)S(1)} %get-tuple-element.11), channel_id=1, source_target_pairs={{0,256},{256,0},{1,257},{257,1},{2,258},{258,2},{3,259},{259,3},{4... | collective-permute-start | bytes 135176 | tf_op jit(solution)/shard_map/ppermute | solution.py:196
  14.2 14.9 %copy-start.7 = (f32[1,4,32,128]{3,2,1,0:T(8,128)S(1)}, f32[1,4,32,128]{3,2,1,0:T(8,128)}, u32[]{:S(2)}) copy-start(f32[1,4,32,128]{3,2,1,0:T(8,128)} %param.17) | copy-start | bytes 196612
  15.0 14.1 %copy-start.6 = (s32[1,4,32,128]{3,2,1,0:T(8,128)S(1)}, s32[1,4,32,128]{3,2,1,0:T(8,128)}, u32[]{:S(2)}) copy-start(s32[1,4,32,128]{3,2,1,0:T(8,128)} %param.16) | copy-start | bytes 196612
  15.1 14.1 %copy-start.1 = (f32[1,2,4,32,128]{4,3,2,1,0:T(8,128)S(1)}, f32[1,2,4,32,128]{4,3,2,1,0:T(8,128)}, u32[]{:S(2)}) copy-start(f32[1,2,4,32,128]{4,3,2,1,0:T(8,128)} %param.11) | copy-start | bytes 393220
  15.1 11.0 %collective-permute-start.1 = (f32[80,128]{1,0:T(8,128)S(1)}, f32[80,128]{1,0:T(8,128)S(1)}, u32[]{:S(2)}, u32[]{:S(2)}) collective-permute-start(f32[80,128]{1,0:T(8,128)S(1)} %pad_maximum_fusion), channel_id=1, source_target_pairs={{0,1},{256,319},{1,2},{257,256},{2,3},{258,257},{3,4},{259,258},{4... | collective-permute-start | bytes 122888 | tf_op jit(solution)/shard_map/ppermute | solution.py:199
  18.9 10.2 %copy-start.5 = (f32[1,4,32,128]{3,2,1,0:T(8,128)S(1)}, f32[1,4,32,128]{3,2,1,0:T(8,128)}, u32[]{:S(2)}) copy-start(f32[1,4,32,128]{3,2,1,0:T(8,128)} %param.10) | copy-start | bytes 196612
  19.0 7.1 %collective-permute-start.2 = (f32[32,128]{1,0:T(8,128)S(1)}, f32[32,128]{1,0:T(8,128)S(1)}, u32[]{:S(2)}, u32[]{:S(2)}) collective-permute-start(f32[32,128]{1,0:T(8,128)S(1)} %pad_maximum_fusion.4), channel_id=1, source_target_pairs={{0,64},{64,128},{320,256},{128,192},{384,320},{448,384},{1,65},{65... | collective-permute-start | bytes 49160 | tf_op jit(solution)/shard_map/ppermute | solution.py:200
  26.0 3.1 %collective-permute-start.3 = (f32[56,128]{1,0:T(8,128)S(1)}, f32[56,128]{1,0:T(8,128)S(1)}, u32[]{:S(2)}, u32[]{:S(2)}) collective-permute-start(f32[56,128]{1,0:T(8,128)S(1)} %pad_maximum_fusion.2), channel_id=1, source_target_pairs={{0,256},{256,0},{1,257},{257,1},{2,258},{258,2},{3,259},{259,3},{4... | collective-permute-start | bytes 86024 | tf_op jit(solution)/shard_map/ppermute | solution.py:202
  32.6 3.1 %collective-permute-start.4 = (f32[88,128]{1,0:T(8,128)S(1)}, f32[88,128]{1,0:T(8,128)S(1)}, u32[]{:S(2)}, u32[]{:S(2)}) collective-permute-start(f32[88,128]{1,0:T(8,128)S(1)} %get-tuple-element.14), channel_id=1, source_target_pairs={{0,256},{256,0},{1,257},{257,1},{2,258},{258,2},{3,259},{259,3},{4... | collective-permute-start | bytes 135176 | tf_op jit(solution)/shard_map/ppermute | solution.py:196
  35.7 10.5 %collective-permute-start.5 = (f32[80,128]{1,0:T(8,128)S(1)}, f32[80,128]{1,0:T(8,128)S(1)}, u32[]{:S(2)}, u32[]{:S(2)}) collective-permute-start(f32[80,128]{1,0:T(8,128)S(1)} %pad_maximum_fusion.1), channel_id=1, source_target_pairs={{0,1},{256,319},{1,2},{257,256},{2,3},{258,257},{3,4},{259,258},{4... | collective-permute-start | bytes 122888 | tf_op jit(solution)/shard_map/ppermute | solution.py:199
  38.3 7.3 %collective-permute-start.6 = (f32[32,128]{1,0:T(8,128)S(1)}, f32[32,128]{1,0:T(8,128)S(1)}, u32[]{:S(2)}, u32[]{:S(2)}) collective-permute-start(f32[32,128]{1,0:T(8,128)S(1)} %pad_maximum_fusion.5), channel_id=1, source_target_pairs={{0,64},{64,128},{320,256},{128,192},{384,320},{448,384},{1,65},{65... | collective-permute-start | bytes 49160 | tf_op jit(solution)/shard_map/ppermute | solution.py:200
  45.6 0.6 %copy-start.10 = (f32[32,128]{1,0:T(8,128)}, f32[32,128]{1,0:T(8,128)S(1)}, u32[]{:S(2)}) copy-start(f32[32,128]{1,0:T(8,128)S(1)} %collective-permute-done.6.lat_ref) | copy-start | bytes 49156
  46.2 0.7 %slice-start = ((f32[32,128]{1,0:T(8,128)}), f32[16,128]{1,0:T(8,128)S(1)}, s32[]{:S(2)}) async-start(f32[32,128]{1,0:T(8,128)} %copy-done.10), calls=%async_computation | async-start | bytes 16384 | tf_op jit(solution)/shard_map/slice | solution.py:201
  46.9 3.2 %copy-start.11 = (f32[32,128]{1,0:T(8,128)S(1)}, f32[32,128]{1,0:T(8,128)}, u32[]{:S(2)}) copy-start(f32[32,128]{1,0:T(8,128)} %copy-done.10) | copy-start | bytes 49156
  46.9 3.2 %collective-permute-start.7 = (f32[56,128]{1,0:T(8,128)S(1)}, f32[56,128]{1,0:T(8,128)S(1)}, u32[]{:S(2)}, u32[]{:S(2)}) collective-permute-start(f32[56,128]{1,0:T(8,128)S(1)} %pad_maximum_fusion.3), channel_id=1, source_target_pairs={{0,256},{256,0},{1,257},{257,1},{2,258},{258,2},{3,259},{259,3},{4... | collective-permute-start | bytes 86024 | tf_op jit(solution)/shard_map/ppermute | solution.py:202

commit v2 on v1

v2 whole, which is shorter than its diff:
```python
import jax
import jax.numpy as jnp
from jax import lax
from jax.experimental import pallas as pl
from jax.experimental.pallas import tpu as pltpu
from jax.sharding import PartitionSpec as P

COMP = 4
LEV = 4
TERMS = 4
ROWS = 32
LANES = 128
BLOCKS = ROWS // 8
PEERS = 3
PLANES = COMP * LEV

LIST = 8 * COMP
SIDE = LIST + 8
KEEP = SIDE + PLANES
GIVE = KEEP + LIST


def lookup(rows, high, low, first_row):
    found = [jnp.zeros((8, LANES), jnp.float32) for _ in range(COMP)]
    for r in range(len(rows[0])):
        here = high == first_row + r
        for k in range(COMP):
            row = jnp.broadcast_to(rows[k][r](), (8, LANES))
            got = jnp.take_along_axis(row, low, axis=1, mode="promise_in_bounds")
            found[k] = jnp.where(here, got, found[k])
    return found


def regrid(list_ref, offset, source, slot_ref, weight_ref, b):
    rows = slice(8 * b, 8 * b + 8)

    def row_of(k, r):
        at = offset + 8 * k + r
        return lambda: list_ref[at : at + 1, :]

    table = [[row_of(k, r) for r in range(8)] for k in range(COMP)]
    total = None
    for t in range(TERMS):
        slot = slot_ref[t, rows, :]
        found = lookup(table, slot >> 7, slot & (LANES - 1), 8 * source)
        found = [weight_ref[t, rows, :] * entry for entry in found]
        total = found if total is None else [a + b for a, b in zip(total, found)]
    return total


def outgoing(core, field, dif_ref, vel_ref, sens_ref, weight, cells, flux_ref, keep_ref, give_ref, ready):
    surface = [field(k, 0) for k in range(COMP)]
    for k in range(COMP):
        total = sens_ref[k : k + 1, 0:1] * surface[0]
        for j in range(1, COMP):
            total = total + sens_ref[k : k + 1, j : j + 1] * surface[j]
        flux_ref[k] = weight * total

    first = core == 0
    kept = jnp.where(first, cells[2], cells[0])
    given = jnp.where(first, cells[0], cells[2])

    def row_of(k, r):
        return lambda: flux_ref[k, r : r + 1, :]

    table = [[row_of(k, r) for r in range(ROWS)] for k in range(COMP)]
    for cell, ref, offset in ((kept, keep_ref, 0), (given, give_ref, 0), (cells[1], give_ref, KEEP)):
        found = lookup(table, cell >> 7, cell & (LANES - 1), 0)
        for k in range(COMP):
            ref[offset + 8 * k : offset + 8 * k + 8, :] = found[k]

    ready()
    lane = lax.broadcasted_iota(jnp.int32, (8, LANES), 1)
    east = jnp.zeros((8, LANES), jnp.float32)
    west = jnp.zeros((8, LANES), jnp.float32)
    for level in range(LEV):
        dif = dif_ref[level]
        half_u = 0.5 * vel_ref[0, level]
        half_v = 0.5 * vel_ref[1, level]
        for k in range(COMP):
            plane = field(k, level)
            at = LEV * k + level
            to_east = (dif - half_u) * plane
            to_west = (dif + half_u) * plane
            for b in range(BLOCKS):
                here = lane == PLANES * b + at
                rows = slice(8 * b, 8 * b + 8)
                east = jnp.where(here, jnp.broadcast_to(to_east[rows, LANES - 1 :], (8, LANES)), east)
                west = jnp.where(here, jnp.broadcast_to(to_west[rows, :1], (8, LANES)), west)
            to_north = ((dif[24:] - half_v[24:]) * plane[24:])[7:8]
            to_south = ((dif[:8] + half_v[:8]) * plane[:8])[0:1]
            keep_ref[SIDE + at : SIDE + at + 1, :] = jnp.where(first, to_north, to_south)
            give_ref[SIDE + at : SIDE + at + 1, :] = jnp.where(first, to_south, to_north)
    keep_ref[LIST:SIDE, :] = jnp.where(first, east, west)
    give_ref[LIST:SIDE, :] = jnp.where(first, west, east)


def weight_and_cells(sea_ref, dist_ref, send_ref):
    distance = dist_ref[...].astype(jnp.float32)
    blend = (distance + 1.0) / (distance + 9.0)
    return sea_ref[...].astype(jnp.float32) * blend, [send_ref[8 * d : 8 * d + 8, :] for d in range(PEERS)]


def start_kernel(
    sens_hbm, field_hbm, dif_hbm, vel_hbm, sea_hbm, dist_hbm, send_hbm,
    keep_ref, give_ref, flux_ref, sens_ref, field_ref, dif_ref, vel_ref, sea_ref, dist_ref, send_ref, sems,
):
    early = [(sens_hbm, sens_ref), (send_hbm, send_ref), (sea_hbm, sea_ref), (dist_hbm, dist_ref)]
    early += [(field_hbm.at[k, 0], field_ref.at[k, 0]) for k in range(COMP)]
    late = [(dif_hbm, dif_ref), (vel_hbm, vel_ref)]
    late += [(field_hbm.at[k, pl.ds(1, LEV - 1)], field_ref.at[k, pl.ds(1, LEV - 1)]) for k in range(COMP)]
    copies = [pltpu.make_async_copy(a, b, sems.at[i]) for i, (a, b) in enumerate(early + late)]
    for copy in copies:
        copy.start()
    for copy in copies[: len(early)]:
        copy.wait()

    def ready():
        for copy in copies[len(early) :]:
            copy.wait()

    weight, cells = weight_and_cells(sea_ref, dist_ref, send_ref)
    outgoing(
        lax.axis_index("sec"), lambda k, l: field_ref[k, l], dif_ref, vel_ref, sens_ref, weight, cells, flux_ref, keep_ref, give_ref, ready
    )


def inner_kernel(field_ref, dif_ref, vel_ref, slot_ref, weight_ref, near_ref, base_ref):
    lane = lax.broadcasted_iota(jnp.int32, (ROWS, LANES), 1)
    row = lax.broadcasted_iota(jnp.int32, (ROWS, LANES), 0)
    for level in range(LEV):
        dif = dif_ref[level]
        half_u = 0.5 * vel_ref[0, level]
        half_v = 0.5 * vel_ref[1, level]
        for k in range(COMP):
            plane = field_ref[k, level]
            east = jnp.where(lane == LANES - 1, 0.0, pltpu.roll((dif + half_u) * plane, LANES - 1, 1))
            west = jnp.where(lane == 0, 0.0, pltpu.roll((dif - half_u) * plane, 1, 1))
            north = jnp.where(row == ROWS - 1, 0.0, pltpu.roll((dif + half_v) * plane, ROWS - 1, 0))
            south = jnp.where(row == 0, 0.0, pltpu.roll((dif - half_v) * plane, 1, 0))
            base_ref[k, level] = plane - 4.0 * (dif * plane) + ((north + south) + (east + west))
    for b in range(BLOCKS):
        rows = slice(8 * b, 8 * b + 8)
        total = regrid(near_ref, KEEP, 1, slot_ref, weight_ref, b)
        for k in range(COMP):
            base_ref[k, 0, rows, :] = base_ref[k, 0, rows, :] + total[k]


def kept_kernel(slot_ref, weight_ref, lon_ref, part_ref):
    source = 2 * lax.axis_index("sec")
    for b in range(BLOCKS):
        total = regrid(lon_ref, SIDE, source, slot_ref, weight_ref, b)
        for k in range(COMP):
            part_ref[k, 8 * b : 8 * b + 8, :] = total[k]


def finish(core, base_ref, part_ref, slot_ref, weight_ref, edge_ref, back_ref, out_ref):
    first = core == 0
    kept_side = edge_ref[:8, :]
    passed_side = back_ref[LIST:SIDE, :]
    from_west = jnp.where(first, kept_side, passed_side)
    from_east = jnp.where(first, passed_side, kept_side)
    lane = lax.broadcasted_iota(jnp.int32, (8, LANES), 1)
    row = lax.broadcasted_iota(jnp.int32, (8, LANES), 0)
    for b in range(BLOCKS):
        rows = slice(8 * b, 8 * b + 8)
        total = regrid(back_ref, 0, 2 - 2 * core, slot_ref, weight_ref, b)
        for level in range(LEV):
            for k in range(COMP):
                at = LEV * k + level
                j = PLANES * b + at
                edge_east = jnp.broadcast_to(from_east[:, j : j + 1], (8, LANES))
                edge_west = jnp.broadcast_to(from_west[:, j : j + 1], (8, LANES))
                edge = jnp.where(lane == LANES - 1, edge_east, jnp.where(lane == 0, edge_west, 0.0))
                if b == 0 or b == BLOCKS - 1:
                    kept_row = edge_ref[8 + at : 9 + at, :]
                    passed_row = back_ref[SIDE + at : SIDE + at + 1, :]
                    pair = (kept_row, passed_row) if b == 0 else (passed_row, kept_row)
                    end = jnp.broadcast_to(jnp.where(first, *pair), (8, LANES))
                    edge = edge + jnp.where(row == (0 if b == 0 else 7), end, 0.0)
                value = base_ref[k, level, rows, :] + edge
                if level == 0:
                    value = value + (part_ref[k, rows, :] + total[k])
                out_ref[k, level, rows, :] = value


def middle_kernel(
    sens_ref, base_ref, part_ref, slot_ref, weight_ref, edge_ref, back_ref, dif_ref, vel_ref, sea_ref, dist_ref, send_ref,
    out_ref, keep_ref, give_ref, flux_ref,
):
    core = lax.axis_index("sec")
    finish(core, base_ref, part_ref, slot_ref, weight_ref, edge_ref, back_ref, out_ref)
    weight, cells = weight_and_cells(sea_ref, dist_ref, send_ref)
    outgoing(
        core, lambda k, l: out_ref[k, l], dif_ref, vel_ref, sens_ref, weight, cells, flux_ref, keep_ref, give_ref, lambda: None
    )


def last_kernel(base_ref, part_ref, slot_ref, weight_ref, edge_ref, back_ref, out_ref):
    finish(lax.axis_index("sec"), base_ref, part_ref, slot_ref, weight_ref, edge_ref, back_ref, out_ref)


def call(kernel, arrays, outs, scratch=(), space=pltpu.VMEM, cost=1 << 20):
    in_space = pl.BlockSpec(memory_space=space)
    in_vmem = pl.BlockSpec(memory_space=pltpu.VMEM)
    return pl.pallas_call(
        kernel,
        out_shape=[jax.ShapeDtypeStruct(shape, jnp.float32) for shape in outs],
        in_specs=[in_space] * len(arrays),
        out_specs=[in_vmem] * len(outs),
        scratch_shapes=list(scratch),
        compiler_params=pltpu.CompilerParams(vmem_limit_bytes=8 << 20),
        cost_estimate=pl.CostEstimate(flops=cost, transcendentals=0, bytes_accessed=cost),
    )(*arrays)


def routes(axis):
    count = lax.axis_size(axis)
    periodic = axis == "lon"
    pairs = []
    for i in range(count):
        if periodic or i + 1 < count:
            pairs.append((i, (i + 1) % count))
        if periodic or i > 0:
            pairs.append((count + i, count + (i - 1) % count))
    return pairs


def step(keep, give, field, dif, vel, take):
    near = lax.ppermute(give, "sec", [(0, 1), (1, 0)])
    lon = jnp.concatenate([keep[:SIDE], near[:SIDE]], axis=0)
    lat = jnp.concatenate([keep[SIDE:], near[SIDE:KEEP]], axis=0)
    lon = lax.ppermute(lon, ("sec", "lon"), routes("lon"))
    lat = lax.ppermute(lat, ("sec", "lat"), routes("lat"))
    (base,) = call(inner_kernel, (field, dif, vel, *take, near), [field.shape])
    back = jnp.concatenate([lon[:LIST], lon[SIDE + LIST :], lat[PLANES:]], axis=0)
    back = lax.ppermute(back, "sec", [(0, 1), (1, 0)])
    (part,) = call(kept_kernel, (*take, lon), [(COMP, ROWS, LANES)])
    edge = jnp.concatenate([lon[LIST:SIDE], lat[:PLANES]], axis=0)
    return base, part, *take, edge, back


def on_device(
    adjoint,
    diffusivity,
    velocity,
    sensitivity,
    sea_mask,
    coast_distance,
    send_cells,
    recv_slots,
    regrid_weight,
):
    field = adjoint[0]
    sens = sensitivity[0]
    dif, vel = diffusivity[0], velocity[0]
    send = (sea_mask[0], coast_distance[0], send_cells.reshape(8 * PEERS, LANES))
    take = (recv_slots[0], regrid_weight[0])
    messages = [(KEEP, LANES), (GIVE, LANES)]
    flux = pltpu.VMEM((COMP, ROWS, LANES), jnp.float32)
    held = [pltpu.VMEM(a.shape, a.dtype) for a in (sens, field, dif, vel, *send)]
    sems = pltpu.SemaphoreType.DMA((6 + 2 * COMP,))
    fresh = [pltpu.with_memory_space_constraint(a, pltpu.HBM) for a in (sens, field, dif, vel, *send)]
    keep, give = call(start_kernel, fresh, messages, [flux, *held, sems], pltpu.HBM)
    state = step(keep, give, field, dif, vel, take)
    field, keep, give = call(
        middle_kernel, (sens, *state, dif, vel, *send), [field.shape] + messages, [flux]
    )
    state = step(keep, give, field, dif, vel, take)
    (field,) = call(last_kernel, state, [field.shape])
    return field[None]


def solution(mesh):
    placed = (
        P("sec", None, None, "lat", "lon"),
        P("sec", None, "lat", "lon"),
        P("sec", None, None, "lat", "lon"),
        P("sec", None, None),
        P("sec", "lat", "lon"),
        P("sec", "lat", "lon"),
        P("sec", "lat", "lon", None),
        P("sec", None, "lat", "lon"),
        P("sec", None, "lat", "lon"),
    )
    return jax.shard_map(
        on_device,
        mesh=mesh,
        in_specs=placed,
        out_specs=P("sec", None, None, "lat", "lon"),
        check_vma=False,
    )
```

time: 53.6 us -> 53.2 us (level)
  starting transfers between devices: 23.9 us -> 40.9 us
  waiting for transfers between devices: 15.8 us -> 3.58 us
  local copies, waits for them, and re-layouts: 5.46 us -> 0.08 us
    ppermute x8, starting transfers between devices: 23.9 us -> 40.9 us  [the longest x2 19.8 us: step(): back = lax.ppermute(back, 'sec', [(0, 1), (1, 0)])]
    ppermute x8, waiting for transfers between devices: 15.8 us -> 3.58 us  [the longest x2 1.65 us: step(): near = lax.ppermute(give, 'sec', [(0, 1), (1, 0)])]
    unnamed x27 -> x18, local copies, waits for them, and re-layouts: 4.73 us -> 0.05 us
    slice x15 -> x14, local copies, waits for them, and re-layouts: 0.72 us -> 0.04 us  [the longest x4 0.01 us: step(): lon = jnp.concatenate([keep[:SIDE], near[:SIDE]], axis=0)]
    pallas_call x3 -> x7, Pallas kernels: 7.6 us -> 7.98 us  [call(): pl.pallas_call(kernel, out_shape=[jax.ShapeDtypeStruct(shape, jnp.float32...]
  transfers between devices with their start and end apart: 8 -> 8, of which waited for: 6 -> 6; matrix products, arithmetic and copies ran while one was open for 0% -> 0% of each run, Pallas kernels for 0% -> 6%
where the time goes in v2:
time: 53.2 us; the launch traced here: 52.8 us
  starting transfers between devices  40.9 us (77%)
  Pallas kernels  7.98 us (15%)
  waiting for transfers between devices  3.58 us (7%)
    ppermute x2, starting transfers between devices, step(): back = lax.ppermute(back, 'sec', [(0, 1), (1, 0)])  19.8 us
    ppermute x2, starting transfers between devices, step(): near = lax.ppermute(give, 'sec', [(0, 1), (1, 0)])  11 us
    pallas_call x7, Pallas kernels, call(): pl.pallas_call(kernel, out_shape=[jax.ShapeDtypeStruct(shape, jnp.float32...  7.98 us
    ppermute x2, starting transfers between devices, step(): lon = lax.ppermute(lon, ('sec', 'lon'), routes('lon'))  7.37 us
    ppermute x2, starting transfers between devices, step(): lat = lax.ppermute(lat, ('sec', 'lat'), routes('lat'))  2.7 us
    ppermute x2, waiting for transfers between devices, step(): near = lax.ppermute(give, 'sec', [(0, 1), (1, 0)])  1.65 us
    ppermute x2, waiting for transfers between devices, step(): lat = lax.ppermute(lat, ('sec', 'lat'), routes('lat'))  1.46 us
  transfers between devices with their start and end apart: 8, of which 6 were waited for; matrix products, arithmetic and copies ran while one was open for 0% of the time, Pallas kernels for 6%

profile of v2, /device:TPU:1, one launch (start us, length us, event | category | flops | bytes accessed | tf_op | source)
XLA Modules:
  0.0 52.8 jit_solution(247442150644173772)
XLA Ops:
  0.0 0.0 copy-start.2
  0.0 0.0 copy-start.3
  0.0 1.8 %shard_map.91 = (f32[56,128]{1,0:T(8,128)S(1)}, f32[88,128]{1,0:T(8,128)S(1)}) custom-call(f32[4,4]{1,0:T(4,128)} %bitcast.38, f32[4,4,32,128]{3,2,1,0:T(8,128)} %bitcast.26, f32[4,32,128]{2,1,0:T(8,128)} %bitcast.28, f32[2,4,32,128]{3,2,1,0:T(8,128)} %bitcast.22, s32[32,128]{1,0:T(8,128)} %bitcast.32, s32[32,128]{1,0:T(8,128)} %bitcast.34, s32[24,128]{1,0:T(8,128)} %bitcast.36), custom_call_target="tpu_custom_call" | custom-call | flops 1048576 | bytes 1048576 | tf_op jit(solution)/shard_map/pallas_call | solution.py:206
  1.8 8.8 %collective-permute-start = (f32[88,128]{1,0:T(8,128)S(1)}, f32[88,128]{1,0:T(8,128)S(1)}, u32[]{:S(2)}, u32[]{:S(2)}) collective-permute-start(f32[88,128]{1,0:T(8,128)S(1)} %get-tuple-element.10), channel_id=1, source_target_pairs={{0,256},{256,0},{1,257},{257,1},{2,258},{258,2},{3,259},{259,3},{4... | collective-permute-start | bytes 135176 | tf_op jit(solution)/shard_map/ppermute | solution.py:230
  10.6 0.0 copy-start.4
  10.7 0.8 %collective-permute-done.near_ref = f32[88,128]{1,0:T(8,128)S(1)} collective-permute-done((f32[88,128]{1,0:T(8,128)S(1)}, f32[88,128]{1,0:T(8,128)S(1)}, u32[]{:S(2)}, u32[]{:S(2)}) %collective-permute-start) | collective-permute-done | bytes 45088 | tf_op jit(solution)/shard_map/ppermute | solution.py:230
  11.5 0.0 copy-start.1
  11.5 0.0 copy-start
  11.5 1.4 %collective-permute-start.2 = (f32[32,128]{1,0:T(8,128)S(1)}, f32[32,128]{1,0:T(8,128)S(1)}, u32[]{:S(2)}, u32[]{:S(2)}) collective-permute-start(f32[32,128]{1,0:T(8,128)S(1)} %pad_maximum_fusion.4), channel_id=1, source_target_pairs={{0,64},{64,128},{320,256},{128,192},{384,320},{448,384},{1,65},{65... | collective-permute-start | bytes 49160 | tf_op jit(solution)/shard_map/ppermute | solution.py:234
  12.9 3.7 %collective-permute-start.1 = (f32[80,128]{1,0:T(8,128)S(1)}, f32[80,128]{1,0:T(8,128)S(1)}, u32[]{:S(2)}, u32[]{:S(2)}) collective-permute-start(f32[80,128]{1,0:T(8,128)S(1)} %pad_maximum_fusion), channel_id=1, source_target_pairs={{0,1},{256,319},{1,2},{257,256},{2,3},{258,257},{3,4},{259,258},{4... | collective-permute-start | bytes 122888 | tf_op jit(solution)/shard_map/ppermute | solution.py:233
  16.7 0.0 copy-done.2
  16.7 0.0 copy-done.3
  16.7 0.0 copy-done.4
  16.7 0.0 copy-done.1
  16.7 0.0 copy-done
  16.7 0.8 %shard_map.92.base_ref = f32[4,4,32,128]{3,2,1,0:T(8,128)S(1)} custom-call(f32[4,4,32,128]{3,2,1,0:T(8,128)S(1)} %bitcast.27, f32[4,32,128]{2,1,0:T(8,128)S(1)} %bitcast.29, f32[2,4,32,128]{3,2,1,0:T(8,128)S(1)} %bitcast.23, s32[4,32,128]{2,1,0:T(8,128)S(1)} %bitcast.10, f32[4,32,128]{2,1,0:T(8,128)S(1)} %bitcast.16, f32[88,128]{1,0:T(8,128)S(1)} %collective-permute-done.near_ref), custom_call_target="tpu_custom_call" | custom-call | flops 1048576 | bytes 1048576 | tf_op jit(solution)/shard_map/pallas_call | solution.py:206
  17.5 0.0 collective-permute-done.2
  17.6 0.2 collective-permute-done.1.lon_ref
  17.8 8.2 %collective-permute-start.3 = (f32[56,128]{1,0:T(8,128)S(1)}, f32[56,128]{1,0:T(8,128)S(1)}, u32[]{:S(2)}, u32[]{:S(2)}) collective-permute-start(f32[56,128]{1,0:T(8,128)S(1)} %pad_maximum_fusion.2), channel_id=1, source_target_pairs={{0,256},{256,0},{1,257},{257,1},{2,258},{258,2},{3,259},{259,3},{4... | collective-permute-start | bytes 86024 | tf_op jit(solution)/shard_map/ppermute | solution.py:237
  26.0 0.0 copy-start.5
  26.0 0.0 copy-start.6
  26.0 0.0 copy-start.7
  26.0 0.0 copy-start.8
  26.1 0.7 %shard_map.93.part_ref = f32[4,32,128]{2,1,0:T(8,128)S(1)} custom-call(s32[4,32,128]{2,1,0:T(8,128)S(1)} %bitcast.11, f32[4,32,128]{2,1,0:T(8,128)S(1)} %bitcast.17, f32[80,128]{1,0:T(8,128)S(1)} %collective-permute-done.1.lon_ref), custom_call_target="tpu_custom_call" | custom-call | flops 1048576 | bytes 1048576 | tf_op jit(solution)/shard_map/pallas_call | solution.py:206
  26.7 0.1 collective-permute-done.3.back_ref
  26.8 0.0 copy-done.5
  26.8 0.0 copy-done.6
  26.8 0.0 copy-done.7
  26.8 0.0 copy-done.8
  26.8 1.6 %shard_map.94 = (f32[4,4,32,128]{3,2,1,0:T(8,128)S(1)}, f32[56,128]{1,0:T(8,128)S(1)}, f32[88,128]{1,0:T(8,128)S(1)}) custom-call(f32[4,4]{1,0:T(4,128)S(1)} %bitcast.39, f32[4,4,32,128]{3,2,1,0:T(8,128)S(1)} %shard_map.92.base_ref, f32[4,32,128]{2,1,0:T(8,128)S(1)} %shard_map.93.part_ref, s32[4,32,128]{2,1,0:T(8,128)S(1)} %bitcast.12, ...), custom_call_target="tpu_custom_call" | custom-call | flops 1048576 | bytes 1048576 | tf_op jit(solution)/shard_map/pallas_call | solution.py:206
  28.5 2.3 %collective-permute-start.4 = (f32[88,128]{1,0:T(8,128)S(1)}, f32[88,128]{1,0:T(8,128)S(1)}, u32[]{:S(2)}, u32[]{:S(2)}) collective-permute-start(f32[88,128]{1,0:T(8,128)S(1)} %get-tuple-element.13), channel_id=1, source_target_pairs={{0,256},{256,0},{1,257},{257,1},{2,258},{258,2},{3,259},{259,3},{4... | collective-permute-start | bytes 135176 | tf_op jit(solution)/shard_map/ppermute | solution.py:230
  30.8 0.8 %collective-permute-done.4.near_ref = f32[88,128]{1,0:T(8,128)S(1)} collective-permute-done((f32[88,128]{1,0:T(8,128)S(1)}, f32[88,128]{1,0:T(8,128)S(1)}, u32[]{:S(2)}, u32[]{:S(2)}) %collective-permute-start.4) | collective-permute-done | bytes 45088 | tf_op jit(solution)/shard_map/ppermute | solution.py:230
  31.6 1.3 %collective-permute-start.6 = (f32[32,128]{1,0:T(8,128)S(1)}, f32[32,128]{1,0:T(8,128)S(1)}, u32[]{:S(2)}, u32[]{:S(2)}) collective-permute-start(f32[32,128]{1,0:T(8,128)S(1)} %pad_maximum_fusion.5), channel_id=1, source_target_pairs={{0,64},{64,128},{320,256},{128,192},{384,320},{448,384},{1,65},{65... | collective-permute-start | bytes 49160 | tf_op jit(solution)/shard_map/ppermute | solution.py:234
  32.9 3.6 %collective-permute-start.5 = (f32[80,128]{1,0:T(8,128)S(1)}, f32[80,128]{1,0:T(8,128)S(1)}, u32[]{:S(2)}, u32[]{:S(2)}) collective-permute-start(f32[80,128]{1,0:T(8,128)S(1)} %pad_maximum_fusion.1), channel_id=1, source_target_pairs={{0,1},{256,319},{1,2},{257,256},{2,3},{258,257},{3,4},{259,258},{4... | collective-permute-start | bytes 122888 | tf_op jit(solution)/shard_map/ppermute | solution.py:233
  36.6 0.8 %shard_map.95.base_ref = f32[4,4,32,128]{3,2,1,0:T(8,128)S(1)} custom-call(f32[4,4,32,128]{3,2,1,0:T(8,128)S(1)} %get-tuple-element.12.field_ref, f32[4,32,128]{2,1,0:T(8,128)S(1)} %bitcast.31, f32[2,4,32,128]{3,2,1,0:T(8,128)S(1)} %bitcast.25, s32[4,32,128]{2,1,0:T(8,128)S(1)} %bitcast.13, f32[4,32,128]{2,1,0:T(8,128)S(1)} %bitcast.19, ...), custom_call_target="tpu_custom_call" | custom-call | flops 1048576 | bytes 1048576 | tf_op jit(solution)/shard_map/pallas_call | solution.py:206
  37.4 1.5 %collective-permute-done.6 = f32[32,128]{1,0:T(8,128)S(1)} collective-permute-done((f32[32,128]{1,0:T(8,128)S(1)}, f32[32,128]{1,0:T(8,128)S(1)}, u32[]{:S(2)}, u32[]{:S(2)}) %collective-permute-start.6) | collective-permute-done | bytes 16416 | tf_op jit(solution)/shard_map/ppermute | solution.py:234
  38.9 0.0 collective-permute-done.5.lon_ref
  38.9 11.5 %collective-permute-start.7 = (f32[56,128]{1,0:T(8,128)S(1)}, f32[56,128]{1,0:T(8,128)S(1)}, u32[]{:S(2)}, u32[]{:S(2)}) collective-permute-start(f32[56,128]{1,0:T(8,128)S(1)} %pad_maximum_fusion.3), channel_id=1, source_target_pairs={{0,256},{256,0},{1,257},{257,1},{2,258},{258,2},{3,259},{259,3},{4... | collective-permute-start | bytes 86024 | tf_op jit(solution)/shard_map/ppermute | solution.py:237
  50.4 0.7 %shard_map.96.part_ref = f32[4,32,128]{2,1,0:T(8,128)S(1)} custom-call(s32[4,32,128]{2,1,0:T(8,128)S(1)} %bitcast.14, f32[4,32,128]{2,1,0:T(8,128)S(1)} %bitcast.20, f32[80,128]{1,0:T(8,128)S(1)} %collective-permute-done.5.lon_ref), custom_call_target="tpu_custom_call" | custom-call | flops 1048576 | bytes 1048576 | tf_op jit(solution)/shard_map/pallas_call | solution.py:206
  51.1 0.2 collective-permute-done.7.back_ref
  51.3 1.6 %shard_map.97 = f32[4,4,32,128]{3,2,1,0:T(8,128)} custom-call(f32[4,4,32,128]{3,2,1,0:T(8,128)S(1)} %shard_map.95.base_ref, f32[4,32,128]{2,1,0:T(8,128)S(1)} %shard_map.96.part_ref, s32[4,32,128]{2,1,0:T(8,128)S(1)} %bitcast.15, f32[4,32,128]{2,1,0:T(8,128)S(1)} %bitcast.21, f32[24,128]{1,0:T(8,128)S(1)} %pad_maximum_fusion.7.edge_ref, ...), custom_call_target="tpu_custom_call" | custom-call | flops 1048576 | bytes 1048576 | tf_op jit(solution)/shard_map/pallas_call | solution.py:206
  (22 shorter events, 0.1 us)
Async XLA Ops:
  0.0 16.7 %copy-start.2 = (f32[1,2,4,32,128]{4,3,2,1,0:T(8,128)S(1)}, f32[1,2,4,32,128]{4,3,2,1,0:T(8,128)}, u32[]{:S(2)}) copy-start(f32[1,2,4,32,128]{4,3,2,1,0:T(8,128)} %param.11) | copy-start | bytes 393220
  0.0 16.7 %copy-start.3 = (f32[1,4,4,32,128]{4,3,2,1,0:T(8,128)S(1)}, f32[1,4,4,32,128]{4,3,2,1,0:T(8,128)}, u32[]{:S(2)}) copy-start(f32[1,4,4,32,128]{4,3,2,1,0:T(8,128)} %param.9) | copy-start | bytes 786436
  1.8 9.6 %collective-permute-start = (f32[88,128]{1,0:T(8,128)S(1)}, f32[88,128]{1,0:T(8,128)S(1)}, u32[]{:S(2)}, u32[]{:S(2)}) collective-permute-start(f32[88,128]{1,0:T(8,128)S(1)} %get-tuple-element.10), channel_id=1, source_target_pairs={{0,256},{256,0},{1,257},{257,1},{2,258},{258,2},{3,259},{259,3},{4... | collective-permute-start | bytes 135176 | tf_op jit(solution)/shard_map/ppermute | solution.py:230
  10.6 6.1 %copy-start.4 = (f32[1,4,32,128]{3,2,1,0:T(8,128)S(1)}, f32[1,4,32,128]{3,2,1,0:T(8,128)}, u32[]{:S(2)}) copy-start(f32[1,4,32,128]{3,2,1,0:T(8,128)} %param.10) | copy-start | bytes 196612
  11.5 5.2 %copy-start.1 = (f32[1,4,32,128]{3,2,1,0:T(8,128)S(1)}, f32[1,4,32,128]{3,2,1,0:T(8,128)}, u32[]{:S(2)}) copy-start(f32[1,4,32,128]{3,2,1,0:T(8,128)} %param.17) | copy-start | bytes 196612
  11.5 5.2 %copy-start = (s32[1,4,32,128]{3,2,1,0:T(8,128)S(1)}, s32[1,4,32,128]{3,2,1,0:T(8,128)}, u32[]{:S(2)}) copy-start(s32[1,4,32,128]{3,2,1,0:T(8,128)} %param.16) | copy-start | bytes 196612
  11.5 6.1 %collective-permute-start.2 = (f32[32,128]{1,0:T(8,128)S(1)}, f32[32,128]{1,0:T(8,128)S(1)}, u32[]{:S(2)}, u32[]{:S(2)}) collective-permute-start(f32[32,128]{1,0:T(8,128)S(1)} %pad_maximum_fusion.4), channel_id=1, source_target_pairs={{0,64},{64,128},{320,256},{128,192},{384,320},{448,384},{1,65},{65... | collective-permute-start | bytes 49160 | tf_op jit(solution)/shard_map/ppermute | solution.py:234
  12.9 4.8 %collective-permute-start.1 = (f32[80,128]{1,0:T(8,128)S(1)}, f32[80,128]{1,0:T(8,128)S(1)}, u32[]{:S(2)}, u32[]{:S(2)}) collective-permute-start(f32[80,128]{1,0:T(8,128)S(1)} %pad_maximum_fusion), channel_id=1, source_target_pairs={{0,1},{256,319},{1,2},{257,256},{2,3},{258,257},{3,4},{259,258},{4... | collective-permute-start | bytes 122888 | tf_op jit(solution)/shard_map/ppermute | solution.py:233
  17.8 9.1 %collective-permute-start.3 = (f32[56,128]{1,0:T(8,128)S(1)}, f32[56,128]{1,0:T(8,128)S(1)}, u32[]{:S(2)}, u32[]{:S(2)}) collective-permute-start(f32[56,128]{1,0:T(8,128)S(1)} %pad_maximum_fusion.2), channel_id=1, source_target_pairs={{0,256},{256,0},{1,257},{257,1},{2,258},{258,2},{3,259},{259,3},{4... | collective-permute-start | bytes 86024 | tf_op jit(solution)/shard_map/ppermute | solution.py:237
  26.0 0.8 %copy-start.5 = (s32[1,32,128]{2,1,0:T(8,128)S(1)}, s32[1,32,128]{2,1,0:T(8,128)}, u32[]{:S(2)}) copy-start(s32[1,32,128]{2,1,0:T(8,128)} %param.13) | copy-start | bytes 49156
  26.0 0.8 %copy-start.6 = (s32[1,32,128]{2,1,0:T(8,128)S(1)}, s32[1,32,128]{2,1,0:T(8,128)}, u32[]{:S(2)}) copy-start(s32[1,32,128]{2,1,0:T(8,128)} %param.14) | copy-start | bytes 49156
  26.0 0.8 %copy-start.7 = (s32[1,1,3,1024]{3,1,2,0:T(1,128)S(1)}, s32[1,1,3,1024]{3,1,2,0:T(1,128)}, u32[]{:S(2)}) copy-start(s32[1,1,3,1024]{3,1,2,0:T(1,128)} %param.15) | copy-start | bytes 36868
  26.0 0.8 %copy-start.8 = (f32[1,4,4]{2,1,0:T(4,128)S(1)}, f32[1,4,4]{2,1,0:T(4,128)}, u32[]{:S(2)}) copy-start(f32[1,4,4]{2,1,0:T(4,128)} %param.12) | copy-start | bytes 196
  28.5 3.1 %collective-permute-start.4 = (f32[88,128]{1,0:T(8,128)S(1)}, f32[88,128]{1,0:T(8,128)S(1)}, u32[]{:S(2)}, u32[]{:S(2)}) collective-permute-start(f32[88,128]{1,0:T(8,128)S(1)} %get-tuple-element.13), channel_id=1, source_target_pairs={{0,256},{256,0},{1,257},{257,1},{2,258},{258,2},{3,259},{259,3},{4... | collective-permute-start | bytes 135176 | tf_op jit(solution)/shard_map/ppermute | solution.py:230
  31.6 7.2 %collective-permute-start.6 = (f32[32,128]{1,0:T(8,128)S(1)}, f32[32,128]{1,0:T(8,128)S(1)}, u32[]{:S(2)}, u32[]{:S(2)}) collective-permute-start(f32[32,128]{1,0:T(8,128)S(1)} %pad_maximum_fusion.5), channel_id=1, source_target_pairs={{0,64},{64,128},{320,256},{128,192},{384,320},{448,384},{1,65},{65... | collective-permute-start | bytes 49160 | tf_op jit(solution)/shard_map/ppermute | solution.py:234
  32.9 5.9 %collective-permute-start.5 = (f32[80,128]{1,0:T(8,128)S(1)}, f32[80,128]{1,0:T(8,128)S(1)}, u32[]{:S(2)}, u32[]{:S(2)}) collective-permute-start(f32[80,128]{1,0:T(8,128)S(1)} %pad_maximum_fusion.1), channel_id=1, source_target_pairs={{0,1},{256,319},{1,2},{257,256},{2,3},{258,257},{3,4},{259,258},{4... | collective-permute-start | bytes 122888 | tf_op jit(solution)/shard_map/ppermute | solution.py:233
  38.9 12.4 %collective-permute-start.7 = (f32[56,128]{1,0:T(8,128)S(1)}, f32[56,128]{1,0:T(8,128)S(1)}, u32[]{:S(2)}, u32[]{:S(2)}) collective-permute-start(f32[56,128]{1,0:T(8,128)S(1)} %pad_maximum_fusion.3), channel_id=1, source_target_pairs={{0,256},{256,0},{1,257},{257,1},{2,258},{258,2},{3,259},{259,3},{4... | collective-permute-start | bytes 86024 | tf_op jit(solution)/shard_map/ppermute | solution.py:237

commit v3 on v2

--- a/solution.py
+++ b/solution.py
@@ -229,11 +229,12 @@
 def step(keep, give, field, dif, vel, take):
     near = lax.ppermute(give, "sec", [(0, 1), (1, 0)])
     lon = jnp.concatenate([keep[:SIDE], near[:SIDE]], axis=0)
-    lat = jnp.concatenate([keep[SIDE:], near[SIDE:KEEP]], axis=0)
+    fill = jnp.zeros((2 * (SIDE - PLANES), LANES), jnp.float32)
+    lat = jnp.concatenate([keep[SIDE:], near[SIDE:KEEP], fill], axis=0)
     lon = lax.ppermute(lon, ("sec", "lon"), routes("lon"))
     lat = lax.ppermute(lat, ("sec", "lat"), routes("lat"))
     (base,) = call(inner_kernel, (field, dif, vel, *take, near), [field.shape])
-    back = jnp.concatenate([lon[:LIST], lon[SIDE + LIST :], lat[PLANES:]], axis=0)
+    back = jnp.concatenate([lon[:LIST], lon[SIDE + LIST :], lat[PLANES : 2 * PLANES]], axis=0)
     back = lax.ppermute(back, "sec", [(0, 1), (1, 0)])
     (part,) = call(kept_kernel, (*take, lon), [(COMP, ROWS, LANES)])
     edge = jnp.concatenate([lon[LIST:SIDE], lat[:PLANES]], axis=0)

time: 53.2 us -> 48 us (0.902)
  starting transfers between devices: 40.9 us -> 24.7 us
  waiting for transfers between devices: 3.58 us -> 11.5 us
  local copies, waits for them, and re-layouts: 0.08 us -> 2.81 us
    ppermute x2, starting transfers between devices: 19.8 us -> 4.96 us  [step(): back = lax.ppermute(back, 'sec', [(0, 1), (1, 0)])]
    ppermute x2, waiting for transfers between devices: 1.46 us -> 9.1 us  [step(): lat = lax.ppermute(lat, ('sec', 'lat'), routes('lat'))]
    slice x2 -> x4, local copies, waits for them, and re-layouts: 0.01 us -> 1.43 us  [step(): lon[:LIST]]
    unnamed x18 -> x26, local copies, waits for them, and re-layouts: 0.05 us -> 1.27 us
    ppermute x2, starting transfers between devices: 7.37 us -> 6.33 us  [step(): lon = lax.ppermute(lon, ('sec', 'lon'), routes('lon'))]
  transfers between devices with their start and end apart: 8 -> 8, of which waited for: 6 -> 7; matrix products, arithmetic and copies ran while one was open for 0% -> 1% of each run, Pallas kernels for 6% -> 6%
where the time goes in v3:
time: 48 us; the launch traced here: 47.4 us
  starting transfers between devices  24.7 us (51%)
  waiting for transfers between devices  11.5 us (24%)
  Pallas kernels  7.97 us (17%)
  local copies, waits for them, and re-layouts  2.81 us (6%)
    ppermute x2, starting transfers between devices, step(): near = lax.ppermute(give, 'sec', [(0, 1), (1, 0)])  10.9 us
    ppermute x2, waiting for transfers between devices, step(): lat = lax.ppermute(lat, ('sec', 'lat'), routes('lat'))  9.1 us
    pallas_call x7, Pallas kernels, call(): pl.pallas_call(kernel, out_shape=[jax.ShapeDtypeStruct(shape, jnp.float32...  7.97 us
    ppermute x2, starting transfers between devices, step(): lon = lax.ppermute(lon, ('sec', 'lon'), routes('lon'))  6.33 us
    ppermute x2, starting transfers between devices, step(): back = lax.ppermute(back, 'sec', [(0, 1), (1, 0)])  4.96 us
    ppermute x2, starting transfers between devices, step(): lat = lax.ppermute(lat, ('sec', 'lat'), routes('lat'))  2.57 us
    ppermute x2, waiting for transfers between devices, step(): near = lax.ppermute(give, 'sec', [(0, 1), (1, 0)])  1.76 us
    slice x4, local copies, waits for them, and re-layouts, step(): lon[:LIST]  1.43 us
  transfers between devices with their start and end apart: 8, of which 7 were waited for; matrix products, arithmetic and copies ran while one was open for 1% of the time, Pallas kernels for 6%

profile of v3, /device:TPU:1, one launch (start us, length us, event | category | flops | bytes accessed | tf_op | source)
XLA Modules:
  0.0 47.4 jit_solution(5951577366279494704)
XLA Ops:
  0.0 0.0 copy-start.3
  0.0 1.8 %shard_map.91 = (f32[56,128]{1,0:T(8,128)S(1)}, f32[88,128]{1,0:T(8,128)S(1)}) custom-call(f32[4,4]{1,0:T(4,128)} %bitcast.38, f32[4,4,32,128]{3,2,1,0:T(8,128)} %bitcast.26, f32[4,32,128]{2,1,0:T(8,128)} %bitcast.28, f32[2,4,32,128]{3,2,1,0:T(8,128)} %bitcast.22, s32[32,128]{1,0:T(8,128)} %bitcast.32, s32[32,128]{1,0:T(8,128)} %bitcast.34, s32[24,128]{1,0:T(8,128)} %bitcast.36), custom_call_target="tpu_custom_call" | custom-call | flops 1048576 | bytes 1048576 | tf_op jit(solution)/shard_map/pallas_call | solution.py:206
  1.8 8.8 %collective-permute-start = (f32[88,128]{1,0:T(8,128)S(1)}, f32[88,128]{1,0:T(8,128)S(1)}, u32[]{:S(2)}, u32[]{:S(2)}) collective-permute-start(f32[88,128]{1,0:T(8,128)S(1)} %get-tuple-element.10), channel_id=1, source_target_pairs={{0,256},{256,0},{1,257},{257,1},{2,258},{258,2},{3,259},{259,3},{4... | collective-permute-start | bytes 135176 | tf_op jit(solution)/shard_map/ppermute | solution.py:230
  10.6 0.0 copy-start.2
  10.7 0.1 pad.17.clone
  10.7 0.7 %collective-permute-done.near_ref = f32[88,128]{1,0:T(8,128)S(1)} collective-permute-done((f32[88,128]{1,0:T(8,128)S(1)}, f32[88,128]{1,0:T(8,128)S(1)}, u32[]{:S(2)}, u32[]{:S(2)}) %collective-permute-start) | collective-permute-done | bytes 45088 | tf_op jit(solution)/shard_map/ppermute | solution.py:230
  11.5 3.9 %collective-permute-start.1 = (f32[80,128]{1,0:T(8,128)S(1)}, f32[80,128]{1,0:T(8,128)S(1)}, u32[]{:S(2)}, u32[]{:S(2)}) collective-permute-start(f32[80,128]{1,0:T(8,128)S(1)} %pad_maximum_fusion), channel_id=1, source_target_pairs={{0,1},{256,319},{1,2},{257,256},{2,3},{258,257},{3,4},{259,258},{4... | collective-permute-start | bytes 122888 | tf_op jit(solution)/shard_map/ppermute | solution.py:234
  15.4 0.1 maximum_maximum_fusion
  15.4 1.3 %collective-permute-start.2 = (f32[80,128]{1,0:T(8,128)S(1)}, f32[80,128]{1,0:T(8,128)S(1)}, u32[]{:S(2)}, u32[]{:S(2)}) collective-permute-start(f32[80,128]{1,0:T(8,128)S(1)} %maximum_maximum_fusion), channel_id=1, source_target_pairs={{0,64},{64,128},{320,256},{128,192},{384,320},{448,384},{1,65},{65... | collective-permute-start | bytes 122888 | tf_op jit(solution)/shard_map/ppermute | solution.py:235
  16.7 0.0 copy-done.3
  16.7 0.0 copy-done.4
  16.8 0.0 copy-done.2
  16.8 0.0 copy-done
  16.8 0.0 copy-done.1
  16.8 0.8 %shard_map.92.base_ref = f32[4,4,32,128]{3,2,1,0:T(8,128)S(1)} custom-call(f32[4,4,32,128]{3,2,1,0:T(8,128)S(1)} %bitcast.27, f32[4,32,128]{2,1,0:T(8,128)S(1)} %bitcast.29, f32[2,4,32,128]{3,2,1,0:T(8,128)S(1)} %bitcast.23, s32[4,32,128]{2,1,0:T(8,128)S(1)} %bitcast.10, f32[4,32,128]{2,1,0:T(8,128)S(1)} %bitcast.16, f32[88,128]{1,0:T(8,128)S(1)} %collective-permute-done.near_ref), custom_call_target="tpu_custom_call" | custom-call | flops 1048576 | bytes 1048576 | tf_op jit(solution)/shard_map/pallas_call | solution.py:206
  17.6 0.0 collective-permute-done.1.lon_ref
  17.6 0.0 copy-start.7
  17.6 0.6 %copy-done.7 = f32[80,128]{1,0:T(8,128)} copy-done((f32[80,128]{1,0:T(8,128)}, f32[80,128]{1,0:T(8,128)S(1)}, u32[]{:S(2)}) %copy-start.7) | copy-done | bytes 40984
  18.2 4.4 %collective-permute-done.2 = f32[80,128]{1,0:T(8,128)S(1)} collective-permute-done((f32[80,128]{1,0:T(8,128)S(1)}, f32[80,128]{1,0:T(8,128)S(1)}, u32[]{:S(2)}, u32[]{:S(2)}) %collective-permute-start.2) | collective-permute-done | bytes 40992 | tf_op jit(solution)/shard_map/ppermute | solution.py:235
  22.6 0.7 %slice-done.1 = f32[32,128]{1,0:T(8,128)S(1)} async-done(((f32[80,128]{1,0:T(8,128)}), f32[32,128]{1,0:T(8,128)S(1)}, s32[]{:S(2)}) %slice-start.1) | async-done | bytes 16408 | tf_op jit(solution)/shard_map/slice | solution.py:237
  23.3 2.1 %collective-permute-start.3 = (f32[56,128]{1,0:T(8,128)S(1)}, f32[56,128]{1,0:T(8,128)S(1)}, u32[]{:S(2)}, u32[]{:S(2)}) collective-permute-start(f32[56,128]{1,0:T(8,128)S(1)} %pad_maximum_fusion.2), channel_id=1, source_target_pairs={{0,256},{256,0},{1,257},{257,1},{2,258},{258,2},{3,259},{259,3},{4... | collective-permute-start | bytes 86024 | tf_op jit(solution)/shard_map/ppermute | solution.py:238
  25.5 0.0 copy-done.8
  25.5 0.0 copy-start.9
  25.5 0.0 copy-start.10
  25.5 0.0 copy-start.11
  25.5 0.0 copy-start.12
  25.5 0.7 %shard_map.93.part_ref = f32[4,32,128]{2,1,0:T(8,128)S(1)} custom-call(s32[4,32,128]{2,1,0:T(8,128)S(1)} %bitcast.11, f32[4,32,128]{2,1,0:T(8,128)S(1)} %bitcast.17, f32[80,128]{1,0:T(8,128)S(1)} %copy-done.8), custom_call_target="tpu_custom_call" | custom-call | flops 1048576 | bytes 1048576 | tf_op jit(solution)/shard_map/pallas_call | solution.py:206
  26.2 0.4 collective-permute-done.3.back_ref
  26.6 0.0 copy-done.9
  26.6 0.0 copy-done.10
  26.6 0.0 copy-done.11
  26.6 0.0 copy-done.12
  26.6 1.6 %shard_map.94 = (f32[4,4,32,128]{3,2,1,0:T(8,128)S(1)}, f32[56,128]{1,0:T(8,128)S(1)}, f32[88,128]{1,0:T(8,128)S(1)}) custom-call(f32[4,4]{1,0:T(4,128)S(1)} %bitcast.39, f32[4,4,32,128]{3,2,1,0:T(8,128)S(1)} %shard_map.92.base_ref, f32[4,32,128]{2,1,0:T(8,128)S(1)} %shard_map.93.part_ref, s32[4,32,128]{2,1,0:T(8,128)S(1)} %bitcast.12, ...), custom_call_target="tpu_custom_call" | custom-call | flops 1048576 | bytes 1048576 | tf_op jit(solution)/shard_map/pallas_call | solution.py:206
  28.2 2.1 %collective-permute-start.4 = (f32[88,128]{1,0:T(8,128)S(1)}, f32[88,128]{1,0:T(8,128)S(1)}, u32[]{:S(2)}, u32[]{:S(2)}) collective-permute-start(f32[88,128]{1,0:T(8,128)S(1)} %get-tuple-element.13), channel_id=1, source_target_pairs={{0,256},{256,0},{1,257},{257,1},{2,258},{258,2},{3,259},{259,3},{4... | collective-permute-start | bytes 135176 | tf_op jit(solution)/shard_map/ppermute | solution.py:230
  30.3 1.0 %collective-permute-done.4.near_ref = f32[88,128]{1,0:T(8,128)S(1)} collective-permute-done((f32[88,128]{1,0:T(8,128)S(1)}, f32[88,128]{1,0:T(8,128)S(1)}, u32[]{:S(2)}, u32[]{:S(2)}) %collective-permute-start.4) | collective-permute-done | bytes 45088 | tf_op jit(solution)/shard_map/ppermute | solution.py:230
  31.3 2.5 %collective-permute-start.5 = (f32[80,128]{1,0:T(8,128)S(1)}, f32[80,128]{1,0:T(8,128)S(1)}, u32[]{:S(2)}, u32[]{:S(2)}) collective-permute-start(f32[80,128]{1,0:T(8,128)S(1)} %pad_maximum_fusion.1), channel_id=1, source_target_pairs={{0,1},{256,319},{1,2},{257,256},{2,3},{258,257},{3,4},{259,258},{4... | collective-permute-start | bytes 122888 | tf_op jit(solution)/shard_map/ppermute | solution.py:234
  33.8 0.1 maximum_maximum_fusion.1
  33.9 1.3 %collective-permute-start.6 = (f32[80,128]{1,0:T(8,128)S(1)}, f32[80,128]{1,0:T(8,128)S(1)}, u32[]{:S(2)}, u32[]{:S(2)}) collective-permute-start(f32[80,128]{1,0:T(8,128)S(1)} %maximum_maximum_fusion.1), channel_id=1, source_target_pairs={{0,64},{64,128},{320,256},{128,192},{384,320},{448,384},{1,65},{65... | collective-permute-start | bytes 122888 | tf_op jit(solution)/shard_map/ppermute | solution.py:235
  35.2 0.8 %shard_map.95.base_ref = f32[4,4,32,128]{3,2,1,0:T(8,128)S(1)} custom-call(f32[4,4,32,128]{3,2,1,0:T(8,128)S(1)} %get-tuple-element.12.field_ref, f32[4,32,128]{2,1,0:T(8,128)S(1)} %bitcast.31, f32[2,4,32,128]{3,2,1,0:T(8,128)S(1)} %bitcast.25, s32[4,32,128]{2,1,0:T(8,128)S(1)} %bitcast.13, f32[4,32,128]{2,1,0:T(8,128)S(1)} %bitcast.19, ...), custom_call_target="tpu_custom_call" | custom-call | flops 1048576 | bytes 1048576 | tf_op jit(solution)/shard_map/pallas_call | solution.py:206
  36.0 0.1 collective-permute-done.5.lon_ref
  36.1 0.6 %copy-done.5 = f32[80,128]{1,0:T(8,128)} copy-done((f32[80,128]{1,0:T(8,128)}, f32[80,128]{1,0:T(8,128)S(1)}, u32[]{:S(2)}) %copy-start.5) | copy-done | bytes 40984
  36.7 4.7 %collective-permute-done.6 = f32[80,128]{1,0:T(8,128)S(1)} collective-permute-done((f32[80,128]{1,0:T(8,128)S(1)}, f32[80,128]{1,0:T(8,128)S(1)}, u32[]{:S(2)}, u32[]{:S(2)}) %collective-permute-start.6) | collective-permute-done | bytes 40992 | tf_op jit(solution)/shard_map/ppermute | solution.py:235
  41.4 0.7 %slice-done = f32[32,128]{1,0:T(8,128)S(1)} async-done(((f32[80,128]{1,0:T(8,128)}), f32[32,128]{1,0:T(8,128)S(1)}, s32[]{:S(2)}) %slice-start) | async-done | bytes 16408 | tf_op jit(solution)/shard_map/slice | solution.py:237
  42.1 2.9 %collective-permute-start.7 = (f32[56,128]{1,0:T(8,128)S(1)}, f32[56,128]{1,0:T(8,128)S(1)}, u32[]{:S(2)}, u32[]{:S(2)}) collective-permute-start(f32[56,128]{1,0:T(8,128)S(1)} %pad_maximum_fusion.3), channel_id=1, source_target_pairs={{0,256},{256,0},{1,257},{257,1},{2,258},{258,2},{3,259},{259,3},{4... | collective-permute-start | bytes 86024 | tf_op jit(solution)/shard_map/ppermute | solution.py:238
  45.0 0.0 copy-done.6
  45.0 0.7 %shard_map.96.part_ref = f32[4,32,128]{2,1,0:T(8,128)S(1)} custom-call(s32[4,32,128]{2,1,0:T(8,128)S(1)} %bitcast.14, f32[4,32,128]{2,1,0:T(8,128)S(1)} %bitcast.20, f32[80,128]{1,0:T(8,128)S(1)} %copy-done.6), custom_call_target="tpu_custom_call" | custom-call | flops 1048576 | bytes 1048576 | tf_op jit(solution)/shard_map/pallas_call | solution.py:206
  45.7 0.1 collective-permute-done.7.back_ref
  45.8 1.6 %shard_map.97 = f32[4,4,32,128]{3,2,1,0:T(8,128)} custom-call(f32[4,4,32,128]{3,2,1,0:T(8,128)S(1)} %shard_map.95.base_ref, f32[4,32,128]{2,1,0:T(8,128)S(1)} %shard_map.96.part_ref, s32[4,32,128]{2,1,0:T(8,128)S(1)} %bitcast.15, f32[4,32,128]{2,1,0:T(8,128)S(1)} %bitcast.21, f32[24,128]{1,0:T(8,128)S(1)} %pad_maximum_fusion.5.edge_ref, ...), custom_call_target="tpu_custom_call" | custom-call | flops 1048576 | bytes 1048576 | tf_op jit(solution)/shard_map/pallas_call | solution.py:206
  (27 shorter events, 0.1 us)
Async XLA Ops:
  0.0 16.7 %copy-start.3 = (f32[1,4,4,32,128]{4,3,2,1,0:T(8,128)S(1)}, f32[1,4,4,32,128]{4,3,2,1,0:T(8,128)}, u32[]{:S(2)}) copy-start(f32[1,4,4,32,128]{4,3,2,1,0:T(8,128)} %param.9) | copy-start | bytes 786436
  0.0 16.7 %copy-start.4 = (f32[1,4,32,128]{3,2,1,0:T(8,128)S(1)}, f32[1,4,32,128]{3,2,1,0:T(8,128)}, u32[]{:S(2)}) copy-start(f32[1,4,32,128]{3,2,1,0:T(8,128)} %param.10) | copy-start | bytes 196612
  1.8 9.6 %collective-permute-start = (f32[88,128]{1,0:T(8,128)S(1)}, f32[88,128]{1,0:T(8,128)S(1)}, u32[]{:S(2)}, u32[]{:S(2)}) collective-permute-start(f32[88,128]{1,0:T(8,128)S(1)} %get-tuple-element.10), channel_id=1, source_target_pairs={{0,256},{256,0},{1,257},{257,1},{2,258},{258,2},{3,259},{259,3},{4... | collective-permute-start | bytes 135176 | tf_op jit(solution)/shard_map/ppermute | solution.py:230
  10.6 6.1 %copy-start.2 = (f32[1,2,4,32,128]{4,3,2,1,0:T(8,128)S(1)}, f32[1,2,4,32,128]{4,3,2,1,0:T(8,128)}, u32[]{:S(2)}) copy-start(f32[1,2,4,32,128]{4,3,2,1,0:T(8,128)} %param.11) | copy-start | bytes 393220
  11.5 5.3 %copy-start = (s32[1,4,32,128]{3,2,1,0:T(8,128)S(1)}, s32[1,4,32,128]{3,2,1,0:T(8,128)}, u32[]{:S(2)}) copy-start(s32[1,4,32,128]{3,2,1,0:T(8,128)} %param.16) | copy-start | bytes 196612
  11.5 5.3 %copy-start.1 = (f32[1,4,32,128]{3,2,1,0:T(8,128)S(1)}, f32[1,4,32,128]{3,2,1,0:T(8,128)}, u32[]{:S(2)}) copy-start(f32[1,4,32,128]{3,2,1,0:T(8,128)} %param.17) | copy-start | bytes 196612
  11.5 6.1 %collective-permute-start.1 = (f32[80,128]{1,0:T(8,128)S(1)}, f32[80,128]{1,0:T(8,128)S(1)}, u32[]{:S(2)}, u32[]{:S(2)}) collective-permute-start(f32[80,128]{1,0:T(8,128)S(1)} %pad_maximum_fusion), channel_id=1, source_target_pairs={{0,1},{256,319},{1,2},{257,256},{2,3},{258,257},{3,4},{259,258},{4... | collective-permute-start | bytes 122888 | tf_op jit(solution)/shard_map/ppermute | solution.py:234
  15.4 7.2 %collective-permute-start.2 = (f32[80,128]{1,0:T(8,128)S(1)}, f32[80,128]{1,0:T(8,128)S(1)}, u32[]{:S(2)}, u32[]{:S(2)}) collective-permute-start(f32[80,128]{1,0:T(8,128)S(1)} %maximum_maximum_fusion), channel_id=1, source_target_pairs={{0,64},{64,128},{320,256},{128,192},{384,320},{448,384},{1,65},{65... | collective-permute-start | bytes 122888 | tf_op jit(solution)/shard_map/ppermute | solution.py:235
  17.6 0.6 %copy-start.7 = (f32[80,128]{1,0:T(8,128)}, f32[80,128]{1,0:T(8,128)S(1)}, u32[]{:S(2)}) copy-start(f32[80,128]{1,0:T(8,128)S(1)} %collective-permute-done.1.lon_ref) | copy-start | bytes 122884
  22.6 0.7 %slice-start.1 = ((f32[80,128]{1,0:T(8,128)}), f32[32,128]{1,0:T(8,128)S(1)}, s32[]{:S(2)}) async-start(f32[80,128]{1,0:T(8,128)} %copy-done.7), calls=%async_computation.1 | async-start | bytes 32768 | tf_op jit(solution)/shard_map/slice | solution.py:237
  23.3 2.1 %copy-start.8 = (f32[80,128]{1,0:T(8,128)S(1)}, f32[80,128]{1,0:T(8,128)}, u32[]{:S(2)}) copy-start(f32[80,128]{1,0:T(8,128)} %copy-done.7) | copy-start | bytes 122884
  23.3 3.2 %collective-permute-start.3 = (f32[56,128]{1,0:T(8,128)S(1)}, f32[56,128]{1,0:T(8,128)S(1)}, u32[]{:S(2)}, u32[]{:S(2)}) collective-permute-start(f32[56,128]{1,0:T(8,128)S(1)} %pad_maximum_fusion.2), channel_id=1, source_target_pairs={{0,256},{256,0},{1,257},{257,1},{2,258},{258,2},{3,259},{259,3},{4... | collective-permute-start | bytes 86024 | tf_op jit(solution)/shard_map/ppermute | solution.py:238
  25.5 1.1 %copy-start.9 = (s32[1,32,128]{2,1,0:T(8,128)S(1)}, s32[1,32,128]{2,1,0:T(8,128)}, u32[]{:S(2)}) copy-start(s32[1,32,128]{2,1,0:T(8,128)} %param.13) | copy-start | bytes 49156
  25.5 1.1 %copy-start.10 = (s32[1,32,128]{2,1,0:T(8,128)S(1)}, s32[1,32,128]{2,1,0:T(8,128)}, u32[]{:S(2)}) copy-start(s32[1,32,128]{2,1,0:T(8,128)} %param.14) | copy-start | bytes 49156
  25.5 1.1 %copy-start.11 = (s32[1,1,3,1024]{3,1,2,0:T(1,128)S(1)}, s32[1,1,3,1024]{3,1,2,0:T(1,128)}, u32[]{:S(2)}) copy-start(s32[1,1,3,1024]{3,1,2,0:T(1,128)} %param.15) | copy-start | bytes 36868
  25.5 1.1 %copy-start.12 = (f32[1,4,4]{2,1,0:T(4,128)S(1)}, f32[1,4,4]{2,1,0:T(4,128)}, u32[]{:S(2)}) copy-start(f32[1,4,4]{2,1,0:T(4,128)} %param.12) | copy-start | bytes 196
  28.2 3.1 %collective-permute-start.4 = (f32[88,128]{1,0:T(8,128)S(1)}, f32[88,128]{1,0:T(8,128)S(1)}, u32[]{:S(2)}, u32[]{:S(2)}) collective-permute-start(f32[88,128]{1,0:T(8,128)S(1)} %get-tuple-element.13), channel_id=1, source_target_pairs={{0,256},{256,0},{1,257},{257,1},{2,258},{258,2},{3,259},{259,3},{4... | collective-permute-start | bytes 135176 | tf_op jit(solution)/shard_map/ppermute | solution.py:230
  31.3 4.7 %collective-permute-start.5 = (f32[80,128]{1,0:T(8,128)S(1)}, f32[80,128]{1,0:T(8,128)S(1)}, u32[]{:S(2)}, u32[]{:S(2)}) collective-permute-start(f32[80,128]{1,0:T(8,128)S(1)} %pad_maximum_fusion.1), channel_id=1, source_target_pairs={{0,1},{256,319},{1,2},{257,256},{2,3},{258,257},{3,4},{259,258},{4... | collective-permute-start | bytes 122888 | tf_op jit(solution)/shard_map/ppermute | solution.py:234
  33.9 7.5 %collective-permute-start.6 = (f32[80,128]{1,0:T(8,128)S(1)}, f32[80,128]{1,0:T(8,128)S(1)}, u32[]{:S(2)}, u32[]{:S(2)}) collective-permute-start(f32[80,128]{1,0:T(8,128)S(1)} %maximum_maximum_fusion.1), channel_id=1, source_target_pairs={{0,64},{64,128},{320,256},{128,192},{384,320},{448,384},{1,65},{65... | collective-permute-start | bytes 122888 | tf_op jit(solution)/shard_map/ppermute | solution.py:235
  36.1 0.6 %copy-start.5 = (f32[80,128]{1,0:T(8,128)}, f32[80,128]{1,0:T(8,128)S(1)}, u32[]{:S(2)}) copy-start(f32[80,128]{1,0:T(8,128)S(1)} %collective-permute-done.5.lon_ref) | copy-start | bytes 122884
  41.4 0.7 %slice-start = ((f32[80,128]{1,0:T(8,128)}), f32[32,128]{1,0:T(8,128)S(1)}, s32[]{:S(2)}) async-start(f32[80,128]{1,0:T(8,128)} %copy-done.5), calls=%async_computation | async-start | bytes 32768 | tf_op jit(solution)/shard_map/slice | solution.py:237
  42.1 2.9 %copy-start.6 = (f32[80,128]{1,0:T(8,128)S(1)}, f32[80,128]{1,0:T(8,128)}, u32[]{:S(2)}) copy-start(f32[80,128]{1,0:T(8,128)} %copy-done.5) | copy-start | bytes 122884
  42.1 3.7 %collective-permute-start.7 = (f32[56,128]{1,0:T(8,128)S(1)}, f32[56,128]{1,0:T(8,128)S(1)}, u32[]{:S(2)}, u32[]{:S(2)}) collective-permute-start(f32[56,128]{1,0:T(8,128)S(1)} %pad_maximum_fusion.3), channel_id=1, source_target_pairs={{0,256},{256,0},{1,257},{257,1},{2,258},{258,2},{3,259},{259,3},{4... | collective-permute-start | bytes 86024 | tf_op jit(solution)/shard_map/ppermute | solution.py:238

commit v4 on v2

v4 whole, which is shorter than its diff:
```python
import jax
import jax.numpy as jnp
from jax import lax
from jax.experimental import pallas as pl
from jax.experimental.pallas import tpu as pltpu
from jax.sharding import PartitionSpec as P

COMP = 4
LEV = 4
TERMS = 4
ROWS = 32
LANES = 128
BLOCKS = ROWS // 8
PEERS = 3
PLANES = COMP * LEV

LIST = 8 * COMP
SIDE = LIST + 8
KEEP = SIDE + PLANES
GIVE = KEEP + LIST


def lookup(rows, high, low, first_row):
    found = [jnp.zeros((8, LANES), jnp.float32) for _ in range(COMP)]
    for r in range(len(rows[0])):
        here = high == first_row + r
        for k in range(COMP):
            row = jnp.broadcast_to(rows[k][r](), (8, LANES))
            got = jnp.take_along_axis(row, low, axis=1, mode="promise_in_bounds")
            found[k] = jnp.where(here, got, found[k])
    return found


def regrid(list_ref, offset, source, slot_ref, weight_ref, b):
    rows = slice(8 * b, 8 * b + 8)

    def row_of(k, r):
        at = offset + 8 * k + r
        return lambda: list_ref[at : at + 1, :]

    table = [[row_of(k, r) for r in range(8)] for k in range(COMP)]
    total = None
    for t in range(TERMS):
        slot = slot_ref[t, rows, :]
        found = lookup(table, slot >> 7, slot & (LANES - 1), 8 * source)
        found = [weight_ref[t, rows, :] * entry for entry in found]
        total = found if total is None else [a + b for a, b in zip(total, found)]
    return total


def fluxes(surface, sens_ref, weight, flux_ref):
    for k in range(COMP):
        total = sens_ref[k : k + 1, 0:1] * surface[0]
        for j in range(1, COMP):
            total = total + sens_ref[k : k + 1, j : j + 1] * surface[j]
        flux_ref[k] = weight * total


def pick(flux_ref, cell, out_ref, offset):
    def row_of(k, r):
        return lambda: flux_ref[k, r : r + 1, :]

    table = [[row_of(k, r) for r in range(ROWS)] for k in range(COMP)]
    found = lookup(table, cell >> 7, cell & (LANES - 1), 0)
    for k in range(COMP):
        out_ref[offset + 8 * k : offset + 8 * k + 8, :] = found[k]


def edges(upward, field_ref, dif_ref, vel_ref, out_ref):
    half = jnp.where(upward, -0.5, 0.5).astype(jnp.float32)
    last = jnp.where(upward, ROWS - 1, 0)
    column = jnp.broadcast_to(jnp.where(upward, LANES - 1, 0), (8, LANES))
    lane = lax.broadcasted_iota(jnp.int32, (8, LANES), 1)
    side = jnp.zeros((8, LANES), jnp.float32)
    for level in range(LEV):
        across = dif_ref[level] + half * vel_ref[0, level]
        along = dif_ref[level, pl.ds(last, 1), :] + half * vel_ref[1, level, pl.ds(last, 1), :]
        for k in range(COMP):
            at = LEV * k + level
            product = across * field_ref[k, level]
            for b in range(BLOCKS):
                edge = jnp.take_along_axis(product[8 * b : 8 * b + 8], column, axis=1, mode="promise_in_bounds")
                side = jnp.where(lane == PLANES * b + at, edge, side)
            out_ref[SIDE + at : SIDE + at + 1, :] = along * field_ref[k, level, pl.ds(last, 1), :]
    out_ref[LIST:SIDE, :] = side


def given(core, flux_ref, send_ref, give_ref):
    pick(flux_ref, send_ref[pl.ds(pl.multiple_of(16 * core, 8), 8), :], give_ref, 0)
    pick(flux_ref, send_ref[8:16, :], give_ref, KEEP)


def keep_kernel(field_ref, dif_ref, vel_ref, send_ref, flux_ref, keep_ref):
    core = lax.axis_index("sec")
    pick(flux_ref, send_ref[pl.ds(pl.multiple_of(16 - 16 * core, 8), 8), :], keep_ref, 0)
    edges(core == 0, field_ref, dif_ref, vel_ref, keep_ref)


def sea_weight(sea_ref, dist_ref):
    distance = dist_ref[...].astype(jnp.float32)
    blend = (distance + 1.0) / (distance + 9.0)
    return sea_ref[...].astype(jnp.float32) * blend


def start_kernel(
    sens_hbm, field_hbm, dif_hbm, vel_hbm, sea_hbm, dist_hbm, send_hbm,
    give_ref, flux_ref, sens_ref, field_ref, dif_ref, vel_ref, sea_ref, dist_ref, send_ref, sems,
):
    early = [(sens_hbm, sens_ref), (send_hbm, send_ref), (sea_hbm, sea_ref), (dist_hbm, dist_ref)]
    early += [(field_hbm.at[k, 0], field_ref.at[k, 0]) for k in range(COMP)]
    late = [(dif_hbm, dif_ref), (vel_hbm, vel_ref)]
    late += [(field_hbm.at[k, pl.ds(1, LEV - 1)], field_ref.at[k, pl.ds(1, LEV - 1)]) for k in range(COMP)]
    copies = [pltpu.make_async_copy(a, b, sems.at[i]) for i, (a, b) in enumerate(early + late)]
    for copy in copies:
        copy.start()
    for copy in copies[: len(early)]:
        copy.wait()

    core = lax.axis_index("sec")
    fluxes([field_ref[k, 0] for k in range(COMP)], sens_ref, sea_weight(sea_ref, dist_ref), flux_ref)
    given(core, flux_ref, send_ref, give_ref)
    for copy in copies[len(early) :]:
        copy.wait()
    edges(core != 0, field_ref, dif_ref, vel_ref, give_ref)


def inner_kernel(field_ref, dif_ref, vel_ref, slot_ref, weight_ref, near_ref, base_ref):
    lane = lax.broadcasted_iota(jnp.int32, (ROWS, LANES), 1)
    row = lax.broadcasted_iota(jnp.int32, (ROWS, LANES), 0)
    for level in range(LEV):
        dif = dif_ref[level]
        half_u = 0.5 * vel_ref[0, level]
        half_v = 0.5 * vel_ref[1, level]
        for k in range(COMP):
            plane = field_ref[k, level]
            east = jnp.where(lane == LANES - 1, 0.0, pltpu.roll((dif + half_u) * plane, LANES - 1, 1))
            west = jnp.where(lane == 0, 0.0, pltpu.roll((dif - half_u) * plane, 1, 1))
            north = jnp.where(row == ROWS - 1, 0.0, pltpu.roll((dif + half_v) * plane, ROWS - 1, 0))
            south = jnp.where(row == 0, 0.0, pltpu.roll((dif - half_v) * plane, 1, 0))
            base_ref[k, level] = plane - 4.0 * (dif * plane) + ((north + south) + (east + west))
    for b in range(BLOCKS):
        rows = slice(8 * b, 8 * b + 8)
        total = regrid(near_ref, KEEP, 1, slot_ref, weight_ref, b)
        for k in range(COMP):
            base_ref[k, 0, rows, :] = base_ref[k, 0, rows, :] + total[k]


def send_kernel(keep_ref, near_ref, lon_ref, lat_ref):
    lon_ref[:SIDE, :] = keep_ref[:SIDE, :]
    lon_ref[SIDE:, :] = near_ref[:SIDE, :]
    lat_ref[:PLANES, :] = keep_ref[SIDE:, :]
    lat_ref[PLANES : 2 * PLANES, :] = near_ref[SIDE:KEEP, :]


def turn_kernel(lon_ref, lat_ref, base_ref, back_ref, edge_ref):
    back_ref[:LIST, :] = lon_ref[:LIST, :]
    back_ref[LIST:SIDE, :] = lon_ref[SIDE + LIST :, :]
    back_ref[SIDE:, :] = lat_ref[PLANES : 2 * PLANES, :]
    edge_ref[:8, :] = lon_ref[LIST:SIDE, :]
    edge_ref[8:, :] = lat_ref[:PLANES, :]


def kept_kernel(slot_ref, weight_ref, lon_ref, part_ref):
    source = 2 * lax.axis_index("sec")
    for b in range(BLOCKS):
        total = regrid(lon_ref, SIDE, source, slot_ref, weight_ref, b)
        for k in range(COMP):
            part_ref[k, 8 * b : 8 * b + 8, :] = total[k]


def finish(core, base_ref, part_ref, slot_ref, weight_ref, edge_ref, back_ref, out_ref, ready):
    first = core == 0
    kept_side = edge_ref[:8, :]
    passed_side = back_ref[LIST:SIDE, :]
    from_west = jnp.where(first, kept_side, passed_side)
    from_east = jnp.where(first, passed_side, kept_side)
    lane = lax.broadcasted_iota(jnp.int32, (8, LANES), 1)
    row = lax.broadcasted_iota(jnp.int32, (8, LANES), 0)

    def completed(k, level, b):
        at = LEV * k + level
        j = PLANES * b + at
        edge_east = jnp.broadcast_to(from_east[:, j : j + 1], (8, LANES))
        edge_west = jnp.broadcast_to(from_west[:, j : j + 1], (8, LANES))
        edge = jnp.where(lane == LANES - 1, edge_east, jnp.where(lane == 0, edge_west, 0.0))
        if b == 0 or b == BLOCKS - 1:
            kept_row = edge_ref[8 + at : 9 + at, :]
            passed_row = back_ref[SIDE + at : SIDE + at + 1, :]
            pair = (kept_row, passed_row) if b == 0 else (passed_row, kept_row)
            end = jnp.broadcast_to(jnp.where(first, *pair), (8, LANES))
            edge = edge + jnp.where(row == (0 if b == 0 else 7), end, 0.0)
        return base_ref[k, level, 8 * b : 8 * b + 8, :] + edge

    for k in range(COMP):
        for level in range(1, LEV):
            for b in range(BLOCKS):
                out_ref[k, level, 8 * b : 8 * b + 8, :] = completed(k, level, b)
        ready(k)
    for b in range(BLOCKS):
        rows = slice(8 * b, 8 * b + 8)
        total = regrid(back_ref, 0, 2 - 2 * core, slot_ref, weight_ref, b)
        for k in range(COMP):
            out_ref[k, 0, rows, :] = completed(k, 0, b) + (part_ref[k, rows, :] + total[k])


def middle_kernel(
    sens_ref, base_ref, part_ref, slot_ref, weight_ref, edge_ref, back_ref, dif_ref, vel_ref, sea_ref, dist_ref, send_ref,
    out_ref, give_ref, flux_ref,
):
    core = lax.axis_index("sec")
    finish(core, base_ref, part_ref, slot_ref, weight_ref, edge_ref, back_ref, out_ref, lambda k: None)
    fluxes([out_ref[k, 0] for k in range(COMP)], sens_ref, sea_weight(sea_ref, dist_ref), flux_ref)
    given(core, flux_ref, send_ref, give_ref)
    edges(core != 0, out_ref, dif_ref, vel_ref, give_ref)


def last_kernel(base_ref, part_ref, slot_ref, weight_ref, edge_ref, back_ref, out_hbm, out_ref, sems):
    copies = [
        pltpu.make_async_copy(out_ref.at[k, pl.ds(1, LEV - 1)], out_hbm.at[k, pl.ds(1, LEV - 1)], sems.at[k]) for k in range(COMP)
    ]
    copies += [pltpu.make_async_copy(out_ref.at[k, 0], out_hbm.at[k, 0], sems.at[COMP + k]) for k in range(COMP)]
    finish(
        lax.axis_index("sec"), base_ref, part_ref, slot_ref, weight_ref, edge_ref, back_ref, out_ref, lambda k: copies[k].start()
    )
    for copy in copies[COMP:]:
        copy.start()
    for copy in copies:
        copy.wait()


def call(kernel, arrays, outs, scratch=(), space=pltpu.VMEM, out_space=pltpu.VMEM, cost=1 << 20):
    in_space = pl.BlockSpec(memory_space=space)
    to_space = pl.BlockSpec(memory_space=out_space)
    return pl.pallas_call(
        kernel,
        out_shape=[jax.ShapeDtypeStruct(shape, jnp.float32) for shape in outs],
        in_specs=[in_space] * len(arrays),
        out_specs=[to_space] * len(outs),
        scratch_shapes=list(scratch),
        compiler_params=pltpu.CompilerParams(vmem_limit_bytes=8 << 20),
        cost_estimate=pl.CostEstimate(flops=cost, transcendentals=0, bytes_accessed=cost),
    )(*arrays)


def routes(axis):
    count = lax.axis_size(axis)
    periodic = axis == "lon"
    pairs = []
    for i in range(count):
        if periodic or i + 1 < count:
            pairs.append((i, (i + 1) % count))
        if periodic or i > 0:
            pairs.append((count + i, count + (i - 1) % count))
    return pairs


def step(give, flux, field, dif, vel, send, take):
    near = lax.ppermute(give, "sec", [(0, 1), (1, 0)])
    (keep,) = call(keep_kernel, (field, dif, vel, send, flux), [(KEEP, LANES)])
    lon, lat = call(send_kernel, (keep, near), [(2 * SIDE, LANES), (2 * PLANES, LANES)])
    lon = lax.ppermute(lon, ("sec", "lon"), routes("lon"))
    lat = lax.ppermute(lat, ("sec", "lat"), routes("lat"))
    (base,) = call(inner_kernel, (field, dif, vel, *take, near), [field.shape])
    back, edge = call(turn_kernel, (lon, lat, base), [(KEEP, LANES), (8 + PLANES, LANES)])
    back = lax.ppermute(back, "sec", [(0, 1), (1, 0)])
    (part,) = call(kept_kernel, (*take, lon), [(COMP, ROWS, LANES)])
    return base, part, *take, edge, back


def on_device(
    adjoint,
    diffusivity,
    velocity,
    sensitivity,
    sea_mask,
    coast_distance,
    send_cells,
    recv_slots,
    regrid_weight,
):
    field = adjoint[0]
    sens = sensitivity[0]
    dif, vel = diffusivity[0], velocity[0]
    send = (sea_mask[0], coast_distance[0], send_cells.reshape(8 * PEERS, LANES))
    take = (recv_slots[0], regrid_weight[0])
    messages = [(GIVE, LANES), (COMP, ROWS, LANES)]
    fresh = (sens, field, dif, vel, *send)
    held = [pltpu.VMEM(a.shape, a.dtype) for a in fresh]
    fresh = [pltpu.with_memory_space_constraint(a, pltpu.HBM) for a in fresh]
    sems = pltpu.SemaphoreType.DMA((6 + 2 * COMP,))
    give, flux = call(start_kernel, fresh, messages, [*held, sems], pltpu.HBM)
    state = step(give, flux, field, dif, vel, send[2], take)
    field, give, flux = call(middle_kernel, (sens, *state, dif, vel, *send), [field.shape] + messages)
    state = step(give, flux, field, dif, vel, send[2], take)
    scratch = [pltpu.VMEM(field.shape, jnp.float32), pltpu.SemaphoreType.DMA((2 * COMP,))]
    (field,) = call(last_kernel, state, [field.shape], scratch, out_space=pltpu.HBM)
    return field[None]


def solution(mesh):
    placed = (
        P("sec", None, None, "lat", "lon"),
        P("sec", None, "lat", "lon"),
        P("sec", None, None, "lat", "lon"),
        P("sec", None, None),
        P("sec", "lat", "lon"),
        P("sec", "lat", "lon"),
        P("sec", "lat", "lon", None),
        P("sec", None, "lat", "lon"),
        P("sec", None, "lat", "lon"),
    )
    return jax.shard_map(
        on_device,
        mesh=mesh,
        in_specs=placed,
        out_specs=P("sec", None, None, "lat", "lon"),
        check_vma=False,
    )
```

time: 53.2 us -> 44.7 us (0.84)
  starting transfers between devices: 40.9 us -> 24 us
  waiting for transfers between devices: 3.58 us -> 12 us
    ppermute x2, starting transfers between devices: 19.8 us -> 4.34 us  [step(): back = lax.ppermute(back, 'sec', [(0, 1), (1, 0)])]
    ppermute x2, waiting for transfers between devices: 1.46 us -> 10.1 us  [step(): lat = lax.ppermute(lat, ('sec', 'lat'), routes('lat'))]
    ppermute x2, starting transfers between devices: 7.37 us -> 6.22 us  [step(): lon = lax.ppermute(lon, ('sec', 'lon'), routes('lon'))]
    pallas_call x7 -> x13, Pallas kernels: 7.98 us -> 8.13 us  [call(): pl.pallas_call(kernel, out_shape=[jax.ShapeDtypeStruct(shape, jnp.float32...]
  transfers between devices with their start and end apart: 8 -> 8, of which waited for: 6 -> 6; matrix products, arithmetic and copies ran while one was open for 0% -> 0% of each run, Pallas kernels for 6% -> 8%
where the time goes in v4:
time: 44.7 us; the launch traced here: 44.3 us
  starting transfers between devices  24 us (54%)
  waiting for transfers between devices  12 us (27%)
  Pallas kernels  8.13 us (18%)
    ppermute x2, starting transfers between devices, step(): near = lax.ppermute(give, 'sec', [(0, 1), (1, 0)])  10.8 us
    ppermute x2, waiting for transfers between devices, step(): lat = lax.ppermute(lat, ('sec', 'lat'), routes('lat'))  10.1 us
    pallas_call x13, Pallas kernels, call(): pl.pallas_call(kernel, out_shape=[jax.ShapeDtypeStruct(shape, jnp.float32...  8.13 us
    ppermute x2, starting transfers between devices, step(): lon = lax.ppermute(lon, ('sec', 'lon'), routes('lon'))  6.22 us
    ppermute x2, starting transfers between devices, step(): back = lax.ppermute(back, 'sec', [(0, 1), (1, 0)])  4.34 us
    ppermute x2, starting transfers between devices, step(): lat = lax.ppermute(lat, ('sec', 'lat'), routes('lat'))  2.58 us
    ppermute x2, waiting for transfers between devices, step(): near = lax.ppermute(give, 'sec', [(0, 1), (1, 0)])  1.26 us
  transfers between devices with their start and end apart: 8, of which 6 were waited for; matrix products, arithmetic and copies ran while one was open for 0% of the time, Pallas kernels for 8%

profile of v4, /device:TPU:1, one launch (start us, length us, event | category | flops | bytes accessed | tf_op | source)
XLA Modules:
  0.0 44.3 jit_solution(1339221962981992692)
XLA Ops:
  0.0 0.0 copy-start.1
  0.0 0.0 copy-start
  0.0 0.0 copy-start.2
  0.0 0.0 copy-start.5
  0.0 1.6 %shard_map.91 = (f32[88,128]{1,0:T(8,128)S(1)}, f32[4,32,128]{2,1,0:T(8,128)S(1)}) custom-call(f32[4,4]{1,0:T(4,128)} %bitcast.45, f32[4,4,32,128]{3,2,1,0:T(8,128)} %bitcast.16, f32[4,32,128]{2,1,0:T(8,128)} %bitcast.19, f32[2,4,32,128]{3,2,1,0:T(8,128)} %bitcast.10, s32[32,128]{1,0:T(8,128)} %bitcast.41, s32[32,128]{1,0:T(8,128)} %bitcast.43, ...), custom_call_target="tpu_custom_call" | custom-call | flops 1048576 | bytes 1048576 | tf_op jit(solution)/shard_map/pallas_call | solution.py:234
  1.6 8.8 %collective-permute-start = (f32[88,128]{1,0:T(8,128)S(1)}, f32[88,128]{1,0:T(8,128)S(1)}, u32[]{:S(2)}, u32[]{:S(2)}) collective-permute-start(f32[88,128]{1,0:T(8,128)S(1)} %get-tuple-element.18), channel_id=1, source_target_pairs={{0,256},{256,0},{1,257},{257,1},{2,258},{258,2},{3,259},{259,3},{4... | collective-permute-start | bytes 135176 | tf_op jit(solution)/shard_map/ppermute | solution.py:258
  10.4 0.0 copy-done.1
  10.4 0.0 copy-done
  10.4 0.0 copy-done.2
  10.4 0.0 copy-done.5
  10.5 0.0 copy-start.4
  10.5 0.3 shard_map.93.keep_ref
  10.8 0.0 copy-start.3
  10.8 0.5 %collective-permute-done.near_ref = f32[88,128]{1,0:T(8,128)S(1)} collective-permute-done((f32[88,128]{1,0:T(8,128)S(1)}, f32[88,128]{1,0:T(8,128)S(1)}, u32[]{:S(2)}, u32[]{:S(2)}) %collective-permute-start) | collective-permute-done | bytes 45088 | tf_op jit(solution)/shard_map/ppermute | solution.py:258
  11.3 3.7 %collective-permute-start.1 = (f32[80,128]{1,0:T(8,128)S(1)}, f32[80,128]{1,0:T(8,128)S(1)}, u32[]{:S(2)}, u32[]{:S(2)}) collective-permute-start(f32[80,128]{1,0:T(8,128)S(1)} %get-tuple-element.20), channel_id=1, source_target_pairs={{0,1},{256,319},{1,2},{257,256},{2,3},{258,257},{3,4},{259,258},{4... | collective-permute-start | bytes 122888 | tf_op jit(solution)/shard_map/ppermute | solution.py:261
  15.0 1.3 %collective-permute-start.2 = (f32[32,128]{1,0:T(8,128)S(1)}, f32[32,128]{1,0:T(8,128)S(1)}, u32[]{:S(2)}, u32[]{:S(2)}) collective-permute-start(f32[32,128]{1,0:T(8,128)S(1)} %get-tuple-element.21), channel_id=1, source_target_pairs={{0,64},{64,128},{320,256},{128,192},{384,320},{448,384},{1,65},{65... | collective-permute-start | bytes 49160 | tf_op jit(solution)/shard_map/ppermute | solution.py:262
  16.3 0.0 copy-done.4
  16.3 0.0 copy-done.3
  16.3 0.8 %shard_map.92.base_ref = f32[4,4,32,128]{3,2,1,0:T(8,128)S(1)} custom-call(f32[4,4,32,128]{3,2,1,0:T(8,128)S(1)} %bitcast.18, f32[4,32,128]{2,1,0:T(8,128)S(1)} %bitcast.21, f32[2,4,32,128]{3,2,1,0:T(8,128)S(1)} %bitcast.12, s32[4,32,128]{2,1,0:T(8,128)S(1)} %bitcast.25, f32[4,32,128]{2,1,0:T(8,128)S(1)} %bitcast.31, f32[88,128]{1,0:T(8,128)S(1)} %collective-permute-done.near_ref), custom_call_target="tpu_custom_call" | custom-call | flops 1048576 | bytes 1048576 | tf_op jit(solution)/shard_map/pallas_call | solution.py:234
  17.1 4.8 %collective-permute-done.2.lat_ref = f32[32,128]{1,0:T(8,128)S(1)} collective-permute-done((f32[32,128]{1,0:T(8,128)S(1)}, f32[32,128]{1,0:T(8,128)S(1)}, u32[]{:S(2)}, u32[]{:S(2)}) %collective-permute-start.2) | collective-permute-done | bytes 16416 | tf_op jit(solution)/shard_map/ppermute | solution.py:262
  21.9 0.0 collective-permute-done.1.lon_ref
  22.0 0.0 copy-start.6
  22.0 0.0 copy-start.7
  22.0 2.1 %collective-permute-start.3 = (f32[56,128]{1,0:T(8,128)S(1)}, f32[56,128]{1,0:T(8,128)S(1)}, u32[]{:S(2)}, u32[]{:S(2)}) collective-permute-start(f32[56,128]{1,0:T(8,128)S(1)} %get-tuple-element.23), channel_id=1, source_target_pairs={{0,256},{256,0},{1,257},{257,1},{2,258},{258,2},{3,259},{259,3},{4... | collective-permute-start | bytes 86024 | tf_op jit(solution)/shard_map/ppermute | solution.py:265
  24.0 0.0 copy-start.8
  24.0 0.7 %shard_map.95.part_ref = f32[4,32,128]{2,1,0:T(8,128)S(1)} custom-call(s32[4,32,128]{2,1,0:T(8,128)S(1)} %bitcast.26, f32[4,32,128]{2,1,0:T(8,128)S(1)} %bitcast.32, f32[80,128]{1,0:T(8,128)S(1)} %collective-permute-done.1.lon_ref), custom_call_target="tpu_custom_call" | custom-call | flops 1048576 | bytes 1048576 | tf_op jit(solution)/shard_map/pallas_call | solution.py:234
  24.7 0.5 %collective-permute-done.3.back_ref = f32[56,128]{1,0:T(8,128)S(1)} collective-permute-done((f32[56,128]{1,0:T(8,128)S(1)}, f32[56,128]{1,0:T(8,128)S(1)}, u32[]{:S(2)}, u32[]{:S(2)}) %collective-permute-start.3) | collective-permute-done | bytes 28704 | tf_op jit(solution)/shard_map/ppermute | solution.py:265
  25.2 0.0 copy-done.6
  25.2 0.0 copy-done.7
  25.2 0.0 copy-done.8
  25.2 1.4 %shard_map.97 = (f32[4,4,32,128]{3,2,1,0:T(8,128)S(1)}, f32[88,128]{1,0:T(8,128)S(1)}, f32[4,32,128]{2,1,0:T(8,128)S(1)}) custom-call(f32[4,4]{1,0:T(4,128)S(1)} %bitcast.46, f32[4,4,32,128]{3,2,1,0:T(8,128)S(1)} %shard_map.92.base_ref, f32[4,32,128]{2,1,0:T(8,128)S(1)} %shard_map.95.part_ref, s32[4,32,128]{2,1,0:T(8,128)S(1)} %bitcast.27, ...), custom_call_target="tpu_custom_call" | custom-call | flops 1048576 | bytes 1048576 | tf_op jit(solution)/shard_map/pallas_call | solution.py:234
  26.6 2.1 %collective-permute-start.4 = (f32[88,128]{1,0:T(8,128)S(1)}, f32[88,128]{1,0:T(8,128)S(1)}, u32[]{:S(2)}, u32[]{:S(2)}) collective-permute-start(f32[88,128]{1,0:T(8,128)S(1)} %get-tuple-element.25), channel_id=1, source_target_pairs={{0,256},{256,0},{1,257},{257,1},{2,258},{258,2},{3,259},{259,3},{4... | collective-permute-start | bytes 135176 | tf_op jit(solution)/shard_map/ppermute | solution.py:258
  28.7 0.3 shard_map.99.keep_ref
  29.0 0.8 %collective-permute-done.4.near_ref = f32[88,128]{1,0:T(8,128)S(1)} collective-permute-done((f32[88,128]{1,0:T(8,128)S(1)}, f32[88,128]{1,0:T(8,128)S(1)}, u32[]{:S(2)}, u32[]{:S(2)}) %collective-permute-start.4) | collective-permute-done | bytes 45088 | tf_op jit(solution)/shard_map/ppermute | solution.py:258
  29.7 2.5 %collective-permute-start.5 = (f32[80,128]{1,0:T(8,128)S(1)}, f32[80,128]{1,0:T(8,128)S(1)}, u32[]{:S(2)}, u32[]{:S(2)}) collective-permute-start(f32[80,128]{1,0:T(8,128)S(1)} %get-tuple-element.27), channel_id=1, source_target_pairs={{0,1},{256,319},{1,2},{257,256},{2,3},{258,257},{3,4},{259,258},{4... | collective-permute-start | bytes 122888 | tf_op jit(solution)/shard_map/ppermute | solution.py:261
  32.2 1.3 %collective-permute-start.6 = (f32[32,128]{1,0:T(8,128)S(1)}, f32[32,128]{1,0:T(8,128)S(1)}, u32[]{:S(2)}, u32[]{:S(2)}) collective-permute-start(f32[32,128]{1,0:T(8,128)S(1)} %get-tuple-element.28), channel_id=1, source_target_pairs={{0,64},{64,128},{320,256},{128,192},{384,320},{448,384},{1,65},{65... | collective-permute-start | bytes 49160 | tf_op jit(solution)/shard_map/ppermute | solution.py:262
  33.5 0.8 %shard_map.98.base_ref = f32[4,4,32,128]{3,2,1,0:T(8,128)S(1)} custom-call(f32[4,4,32,128]{3,2,1,0:T(8,128)S(1)} %get-tuple-element.24.field_ref, f32[4,32,128]{2,1,0:T(8,128)S(1)} %bitcast.24, f32[2,4,32,128]{3,2,1,0:T(8,128)S(1)} %bitcast.15, s32[4,32,128]{2,1,0:T(8,128)S(1)} %bitcast.28, f32[4,32,128]{2,1,0:T(8,128)S(1)} %bitcast.34, ...), custom_call_target="tpu_custom_call" | custom-call | flops 1048576 | bytes 1048576 | tf_op jit(solution)/shard_map/pallas_call | solution.py:234
  34.3 5.3 %collective-permute-done.6.lat_ref = f32[32,128]{1,0:T(8,128)S(1)} collective-permute-done((f32[32,128]{1,0:T(8,128)S(1)}, f32[32,128]{1,0:T(8,128)S(1)}, u32[]{:S(2)}, u32[]{:S(2)}) %collective-permute-start.6) | collective-permute-done | bytes 16416 | tf_op jit(solution)/shard_map/ppermute | solution.py:262
  39.6 0.0 collective-permute-done.5.lon_ref
  39.6 2.3 %collective-permute-start.7 = (f32[56,128]{1,0:T(8,128)S(1)}, f32[56,128]{1,0:T(8,128)S(1)}, u32[]{:S(2)}, u32[]{:S(2)}) collective-permute-start(f32[56,128]{1,0:T(8,128)S(1)} %get-tuple-element.30), channel_id=1, source_target_pairs={{0,256},{256,0},{1,257},{257,1},{2,258},{258,2},{3,259},{259,3},{4... | collective-permute-start | bytes 86024 | tf_op jit(solution)/shard_map/ppermute | solution.py:265
  41.9 0.7 %shard_map.101.part_ref = f32[4,32,128]{2,1,0:T(8,128)S(1)} custom-call(s32[4,32,128]{2,1,0:T(8,128)S(1)} %bitcast.29, f32[4,32,128]{2,1,0:T(8,128)S(1)} %bitcast.35, f32[80,128]{1,0:T(8,128)S(1)} %collective-permute-done.5.lon_ref), custom_call_target="tpu_custom_call" | custom-call | flops 1048576 | bytes 1048576 | tf_op jit(solution)/shard_map/pallas_call | solution.py:234
  42.6 0.2 collective-permute-done.7.back_ref
  42.7 1.6 %shard_map.103 = f32[4,4,32,128]{3,2,1,0:T(8,128)} custom-call(f32[4,4,32,128]{3,2,1,0:T(8,128)S(1)} %shard_map.98.base_ref, f32[4,32,128]{2,1,0:T(8,128)S(1)} %shard_map.101.part_ref, s32[4,32,128]{2,1,0:T(8,128)S(1)} %bitcast.30, f32[4,32,128]{2,1,0:T(8,128)S(1)} %bitcast.36, f32[24,128]{1,0:T(8,128)S(1)} %get-tuple-element.29.edge_ref, ...), custom_call_target="tpu_custom_call" | custom-call | flops 1048576 | bytes 1048576 | tf_op jit(solution)/shard_map/pallas_call | solution.py:234
  (4 shorter events, 0.0 us)
Async XLA Ops:
  0.0 10.4 %copy-start.1 = (f32[1,4,4,32,128]{4,3,2,1,0:T(8,128)S(1)}, f32[1,4,4,32,128]{4,3,2,1,0:T(8,128)}, u32[]{:S(2)}) copy-start(f32[1,4,4,32,128]{4,3,2,1,0:T(8,128)} %param.9) | copy-start | bytes 786436
  0.0 10.4 %copy-start = (f32[1,2,4,32,128]{4,3,2,1,0:T(8,128)S(1)}, f32[1,2,4,32,128]{4,3,2,1,0:T(8,128)}, u32[]{:S(2)}) copy-start(f32[1,2,4,32,128]{4,3,2,1,0:T(8,128)} %param.11) | copy-start | bytes 393220
  0.0 10.4 %copy-start.2 = (f32[1,4,32,128]{3,2,1,0:T(8,128)S(1)}, f32[1,4,32,128]{3,2,1,0:T(8,128)}, u32[]{:S(2)}) copy-start(f32[1,4,32,128]{3,2,1,0:T(8,128)} %param.10) | copy-start | bytes 196612
  0.0 10.4 %copy-start.5 = (s32[1,1,3,1024]{3,1,2,0:T(1,128)S(1)}, s32[1,1,3,1024]{3,1,2,0:T(1,128)}, u32[]{:S(2)}) copy-start(s32[1,1,3,1024]{3,1,2,0:T(1,128)} %param.15) | copy-start | bytes 36868
  1.6 9.6 %collective-permute-start = (f32[88,128]{1,0:T(8,128)S(1)}, f32[88,128]{1,0:T(8,128)S(1)}, u32[]{:S(2)}, u32[]{:S(2)}) collective-permute-start(f32[88,128]{1,0:T(8,128)S(1)} %get-tuple-element.18), channel_id=1, source_target_pairs={{0,256},{256,0},{1,257},{257,1},{2,258},{258,2},{3,259},{259,3},{4... | collective-permute-start | bytes 135176 | tf_op jit(solution)/shard_map/ppermute | solution.py:258
  10.5 5.9 %copy-start.4 = (f32[1,4,32,128]{3,2,1,0:T(8,128)S(1)}, f32[1,4,32,128]{3,2,1,0:T(8,128)}, u32[]{:S(2)}) copy-start(f32[1,4,32,128]{3,2,1,0:T(8,128)} %param.17) | copy-start | bytes 196612
  10.8 5.6 %copy-start.3 = (s32[1,4,32,128]{3,2,1,0:T(8,128)S(1)}, s32[1,4,32,128]{3,2,1,0:T(8,128)}, u32[]{:S(2)}) copy-start(s32[1,4,32,128]{3,2,1,0:T(8,128)} %param.16) | copy-start | bytes 196612
  11.3 10.7 %collective-permute-start.1 = (f32[80,128]{1,0:T(8,128)S(1)}, f32[80,128]{1,0:T(8,128)S(1)}, u32[]{:S(2)}, u32[]{:S(2)}) collective-permute-start(f32[80,128]{1,0:T(8,128)S(1)} %get-tuple-element.20), channel_id=1, source_target_pairs={{0,1},{256,319},{1,2},{257,256},{2,3},{258,257},{3,4},{259,258},{4... | collective-permute-start | bytes 122888 | tf_op jit(solution)/shard_map/ppermute | solution.py:261
  15.0 6.9 %collective-permute-start.2 = (f32[32,128]{1,0:T(8,128)S(1)}, f32[32,128]{1,0:T(8,128)S(1)}, u32[]{:S(2)}, u32[]{:S(2)}) collective-permute-start(f32[32,128]{1,0:T(8,128)S(1)} %get-tuple-element.21), channel_id=1, source_target_pairs={{0,64},{64,128},{320,256},{128,192},{384,320},{448,384},{1,65},{65... | collective-permute-start | bytes 49160 | tf_op jit(solution)/shard_map/ppermute | solution.py:262
  22.0 3.2 %copy-start.6 = (s32[1,32,128]{2,1,0:T(8,128)S(1)}, s32[1,32,128]{2,1,0:T(8,128)}, u32[]{:S(2)}) copy-start(s32[1,32,128]{2,1,0:T(8,128)} %param.13) | copy-start | bytes 49156
  22.0 3.2 %copy-start.7 = (s32[1,32,128]{2,1,0:T(8,128)S(1)}, s32[1,32,128]{2,1,0:T(8,128)}, u32[]{:S(2)}) copy-start(s32[1,32,128]{2,1,0:T(8,128)} %param.14) | copy-start | bytes 49156
  22.0 3.2 %collective-permute-start.3 = (f32[56,128]{1,0:T(8,128)S(1)}, f32[56,128]{1,0:T(8,128)S(1)}, u32[]{:S(2)}, u32[]{:S(2)}) collective-permute-start(f32[56,128]{1,0:T(8,128)S(1)} %get-tuple-element.23), channel_id=1, source_target_pairs={{0,256},{256,0},{1,257},{257,1},{2,258},{258,2},{3,259},{259,3},{4... | collective-permute-start | bytes 86024 | tf_op jit(solution)/shard_map/ppermute | solution.py:265
  24.0 1.2 %copy-start.8 = (f32[1,4,4]{2,1,0:T(4,128)S(1)}, f32[1,4,4]{2,1,0:T(4,128)}, u32[]{:S(2)}) copy-start(f32[1,4,4]{2,1,0:T(4,128)} %param.12) | copy-start | bytes 196
  26.6 3.1 %collective-permute-start.4 = (f32[88,128]{1,0:T(8,128)S(1)}, f32[88,128]{1,0:T(8,128)S(1)}, u32[]{:S(2)}, u32[]{:S(2)}) collective-permute-start(f32[88,128]{1,0:T(8,128)S(1)} %get-tuple-element.25), channel_id=1, source_target_pairs={{0,256},{256,0},{1,257},{257,1},{2,258},{258,2},{3,259},{259,3},{4... | collective-permute-start | bytes 135176 | tf_op jit(solution)/shard_map/ppermute | solution.py:258
  29.7 9.9 %collective-permute-start.5 = (f32[80,128]{1,0:T(8,128)S(1)}, f32[80,128]{1,0:T(8,128)S(1)}, u32[]{:S(2)}, u32[]{:S(2)}) collective-permute-start(f32[80,128]{1,0:T(8,128)S(1)} %get-tuple-element.27), channel_id=1, source_target_pairs={{0,1},{256,319},{1,2},{257,256},{2,3},{258,257},{3,4},{259,258},{4... | collective-permute-start | bytes 122888 | tf_op jit(solution)/shard_map/ppermute | solution.py:261
  32.2 7.4 %collective-permute-start.6 = (f32[32,128]{1,0:T(8,128)S(1)}, f32[32,128]{1,0:T(8,128)S(1)}, u32[]{:S(2)}, u32[]{:S(2)}) collective-permute-start(f32[32,128]{1,0:T(8,128)S(1)} %get-tuple-element.28), channel_id=1, source_target_pairs={{0,64},{64,128},{320,256},{128,192},{384,320},{448,384},{1,65},{65... | collective-permute-start | bytes 49160 | tf_op jit(solution)/shard_map/ppermute | solution.py:262
  39.6 3.1 %collective-permute-start.7 = (f32[56,128]{1,0:T(8,128)S(1)}, f32[56,128]{1,0:T(8,128)S(1)}, u32[]{:S(2)}, u32[]{:S(2)}) collective-permute-start(f32[56,128]{1,0:T(8,128)S(1)} %get-tuple-element.30), channel_id=1, source_target_pairs={{0,256},{256,0},{1,257},{257,1},{2,258},{258,2},{3,259},{259,3},{4... | collective-permute-start | bytes 86024 | tf_op jit(solution)/shard_map/ppermute | solution.py:265

commit v5 on v4

v5 whole, which is shorter than its diff:
```python
import jax
import jax.numpy as jnp
from jax import lax
from jax.experimental import pallas as pl
from jax.experimental.pallas import tpu as pltpu
from jax.sharding import PartitionSpec as P

COMP = 4
LEV = 4
TERMS = 4
ROWS = 32
LANES = 128
BLOCKS = ROWS // 8
PEERS = 3
PLANES = COMP * LEV

LIST = 8 * COMP
SIDE = LIST + 8
KEEP = SIDE + PLANES
GIVE = KEEP + LIST
SURFACE = GIVE
COEF = SURFACE + COMP * ROWS
SEA = COEF + 3 * ROWS
SLOT = SEA + ROWS
WEIGHT = SLOT + TERMS * ROWS
CELL = WEIGHT + TERMS * ROWS
SENS = CELL + 8 * PEERS
FIRST = SENS + 8
STRIP = 2 * SIDE + 2 * PLANES
BACK = STRIP + 2 * (8 + PLANES)


def lookup(rows, high, low, first_row):
    found = [jnp.zeros((8, LANES), jnp.float32) for _ in range(COMP)]
    for r in range(len(rows[0])):
        here = high == first_row + r
        for k in range(COMP):
            row = jnp.broadcast_to(rows[k][r](), (8, LANES))
            got = jnp.take_along_axis(row, low, axis=1, mode="promise_in_bounds")
            found[k] = jnp.where(here, got, found[k])
    return found


def regrid(list_ref, offset, source, entries, b):
    slots, weights = entries

    def row_of(k, r):
        at = offset + 8 * k + r
        return lambda: list_ref[at : at + 1, :]

    table = [[row_of(k, r) for r in range(8)] for k in range(COMP)]
    total = None
    for t in range(TERMS):
        slot = slots(t, b)
        found = lookup(table, slot >> 7, slot & (LANES - 1), 8 * source)
        found = [weights(t, b) * entry for entry in found]
        total = found if total is None else [a + b for a, b in zip(total, found)]
    return total


def own_entries(slot_ref, weight_ref):
    return (lambda t, b: slot_ref[t, 8 * b : 8 * b + 8, :]), (lambda t, b: weight_ref[t, 8 * b : 8 * b + 8, :])


def near_entries(near_ref):
    def rows(base, t, b):
        return near_ref[base + ROWS * t + 8 * b : base + ROWS * t + 8 * b + 8, :]

    return (lambda t, b: rows(SLOT, t, b).astype(jnp.int32)), (lambda t, b: rows(WEIGHT, t, b))


def fluxes(surface, sens_ref, weight, flux_ref):
    for k in range(COMP):
        total = sens_ref[k : k + 1, 0:1] * surface[0]
        for j in range(1, COMP):
            total = total + sens_ref[k : k + 1, j : j + 1] * surface[j]
        flux_ref[k] = weight * total


def pick(flux_ref, cell, out_ref, offset):
    def row_of(k, r):
        return lambda: flux_ref[k, r : r + 1, :]

    table = [[row_of(k, r) for r in range(ROWS)] for k in range(COMP)]
    found = lookup(table, cell >> 7, cell & (LANES - 1), 0)
    for k in range(COMP):
        out_ref[offset + 8 * k : offset + 8 * k + 8, :] = found[k]


def direction(upward):
    half = jnp.where(upward, -0.5, 0.5).astype(jnp.float32)
    last = jnp.where(upward, ROWS - 1, 0)
    column = jnp.broadcast_to(jnp.where(upward, LANES - 1, 0), (8, LANES))
    return half, last, column


def pull(value, index):
    return jnp.take_along_axis(value, index, axis=1, mode="promise_in_bounds")


def edges(upward, field_ref, dif_ref, vel_ref, side_ref, side_at, row_ref, row_at):
    half, last, column = direction(upward)
    lane = lax.broadcasted_iota(jnp.int32, (8, LANES), 1)
    side = jnp.zeros((8, LANES), jnp.float32)
    for level in range(LEV):
        across = dif_ref[level] + half * vel_ref[0, level]
        along = dif_ref[level, pl.ds(last, 1), :] + half * vel_ref[1, level, pl.ds(last, 1), :]
        for k in range(COMP):
            at = LEV * k + level
            product = across * field_ref[k, level]
            for b in range(BLOCKS):
                side = jnp.where(lane == PLANES * b + at, pull(product[8 * b : 8 * b + 8], column), side)
            row_ref[row_at + at : row_at + at + 1, :] = along * field_ref[k, level, pl.ds(last, 1), :]
    side_ref[side_at : side_at + 8, :] = side


def given(core, flux_ref, send_ref, give_ref):
    pick(flux_ref, send_ref[pl.ds(pl.multiple_of(16 * core, 8), 8), :], give_ref, 0)
    pick(flux_ref, send_ref[8:16, :], give_ref, KEEP)


def keep_kernel(field_ref, dif_ref, vel_ref, send_ref, flux_ref, keep_ref):
    core = lax.axis_index("sec")
    pick(flux_ref, send_ref[pl.ds(pl.multiple_of(16 - 16 * core, 8), 8), :], keep_ref, 0)
    edges(core == 0, field_ref, dif_ref, vel_ref, keep_ref, LIST, keep_ref, SIDE)


def sea_weight(sea_ref, dist_ref):
    distance = dist_ref[...].astype(jnp.float32)
    blend = (distance + 1.0) / (distance + 9.0)
    return sea_ref[...].astype(jnp.float32) * blend


def start_kernel(
    sens_hbm, field_hbm, dif_hbm, vel_hbm, sea_hbm, dist_hbm, send_hbm, slot_hbm, weight_hbm,
    give_ref, flux_ref, sens_ref, field_ref, dif_ref, vel_ref, sea_ref, dist_ref, send_ref, slot_ref, weight_ref, sems,
):
    early = [(sens_hbm, sens_ref), (send_hbm, send_ref), (sea_hbm, sea_ref), (dist_hbm, dist_ref)]
    early += [(field_hbm.at[:, 0], field_ref.at[:, 0])]
    late = [(dif_hbm, dif_ref), (vel_hbm, vel_ref), (slot_hbm, slot_ref), (weight_hbm, weight_ref)]
    late += [(field_hbm.at[:, pl.ds(1, LEV - 1)], field_ref.at[:, pl.ds(1, LEV - 1)])]
    copies = [pltpu.make_async_copy(a, b, sems.at[i]) for i, (a, b) in enumerate(early + late)]
    for copy in copies:
        copy.start()
    for copy in copies[: len(early)]:
        copy.wait()

    core = lax.axis_index("sec")
    sea = sea_weight(sea_ref, dist_ref)
    fluxes([field_ref[k, 0] for k in range(COMP)], sens_ref, sea, flux_ref)
    given(core, flux_ref, send_ref, give_ref)
    give_ref[SEA:SLOT, :] = sea
    give_ref[CELL:SENS, :] = send_ref[...].astype(jnp.float32)
    give_ref[SENS:, :] = jnp.zeros((8, LANES), jnp.float32)
    give_ref[SENS : SENS + COMP, 0:COMP] = sens_ref[...]
    for copy in copies[len(early) :]:
        copy.wait()
    edges(core != 0, field_ref, dif_ref, vel_ref, give_ref, LIST, give_ref, SIDE)
    for k in range(COMP):
        give_ref[SURFACE + ROWS * k : SURFACE + ROWS * k + ROWS, :] = field_ref[k, 0]
    for i, plane in enumerate((dif_ref[0], vel_ref[0, 0], vel_ref[1, 0])):
        give_ref[COEF + ROWS * i : COEF + ROWS * i + ROWS, :] = plane
    for t in range(TERMS):
        give_ref[SLOT + ROWS * t : SLOT + ROWS * t + ROWS, :] = slot_ref[t].astype(jnp.float32)
        give_ref[WEIGHT + ROWS * t : WEIGHT + ROWS * t + ROWS, :] = weight_ref[t]


def inside(plane, dif, half_u, half_v):
    lane = lax.broadcasted_iota(jnp.int32, (ROWS, LANES), 1)
    row = lax.broadcasted_iota(jnp.int32, (ROWS, LANES), 0)
    east = jnp.where(lane == LANES - 1, 0.0, pltpu.roll((dif + half_u) * plane, LANES - 1, 1))
    west = jnp.where(lane == 0, 0.0, pltpu.roll((dif - half_u) * plane, 1, 1))
    north = jnp.where(row == ROWS - 1, 0.0, pltpu.roll((dif + half_v) * plane, ROWS - 1, 0))
    south = jnp.where(row == 0, 0.0, pltpu.roll((dif - half_v) * plane, 1, 0))
    return plane - 4.0 * (dif * plane) + ((north + south) + (east + west))


def inner(field_ref, dif_ref, vel_ref, entries, list_ref, offset, base_ref):
    for level in range(LEV):
        for k in range(COMP):
            base_ref[k, level] = inside(field_ref[k, level], dif_ref[level], 0.5 * vel_ref[0, level], 0.5 * vel_ref[1, level])
    for b in range(BLOCKS):
        rows = slice(8 * b, 8 * b + 8)
        total = regrid(list_ref, offset, 1, entries, b)
        for k in range(COMP):
            base_ref[k, 0, rows, :] = base_ref[k, 0, rows, :] + total[k]


def first_inner_kernel(field_ref, dif_ref, vel_ref, slot_ref, weight_ref, near_ref, give_ref, base_ref, other_ref, strip_ref):
    inner(field_ref, dif_ref, vel_ref, own_entries(slot_ref, weight_ref), near_ref, KEEP, base_ref)
    dif = near_ref[COEF : COEF + ROWS, :]
    half_u = 0.5 * near_ref[COEF + ROWS : COEF + 2 * ROWS, :]
    half_v = 0.5 * near_ref[COEF + 2 * ROWS : COEF + 3 * ROWS, :]
    for k in range(COMP):
        other_ref[k] = inside(near_ref[SURFACE + ROWS * k : SURFACE + ROWS * k + ROWS, :], dif, half_u, half_v)
    for b in range(BLOCKS):
        rows = slice(8 * b, 8 * b + 8)
        total = regrid(give_ref, KEEP, 1, near_entries(near_ref), b)
        for k in range(COMP):
            other_ref[k, rows, :] = other_ref[k, rows, :] + total[k]

    half, last, column = direction(lax.axis_index("sec") != 0)
    lane = lax.broadcasted_iota(jnp.int32, (8, LANES), 1)
    side = jnp.zeros((8, LANES), jnp.float32)
    factor = jnp.zeros((8, LANES), jnp.float32)
    strip_ref[8 : 8 + PLANES, :] = jnp.zeros((PLANES, LANES), jnp.float32)
    strip_ref[16 + PLANES :, :] = jnp.zeros((PLANES, LANES), jnp.float32)
    for level in range(1, LEV):
        across = dif_ref[level] + half * vel_ref[0, level]
        along = dif_ref[level, pl.ds(last, 1), :] + half * vel_ref[1, level, pl.ds(last, 1), :]
        for b in range(BLOCKS):
            here = ((lane >> 4) == b) & ((lane & (LEV - 1)) == level)
            factor = jnp.where(here, pull(across[8 * b : 8 * b + 8], column), factor)
        for k in range(COMP):
            at = LEV * k + level
            for b in range(BLOCKS):
                side = jnp.where(lane == PLANES * b + at, pull(base_ref[k, level, 8 * b : 8 * b + 8, :], column), side)
            strip_ref[8 + at : 9 + at, :] = base_ref[k, level, pl.ds(last, 1), :]
            strip_ref[16 + PLANES + at : 17 + PLANES + at, :] = along
    strip_ref[:8, :] = side
    strip_ref[8 + PLANES : 16 + PLANES, :] = factor


def second_inner_kernel(field_ref, dif_ref, vel_ref, slot_ref, weight_ref, near_ref, flux_ref, base_ref, list_ref):
    pick(flux_ref, near_ref[CELL + 8 : CELL + 16, :].astype(jnp.int32), list_ref, 0)
    inner(field_ref, dif_ref, vel_ref, own_entries(slot_ref, weight_ref), list_ref, 0, base_ref)


def send_kernel(keep_ref, near_ref, lon_ref, lat_ref):
    lon_ref[:SIDE, :] = keep_ref[:SIDE, :]
    lon_ref[SIDE:, :] = near_ref[:SIDE, :]
    lat_ref[:PLANES, :] = keep_ref[SIDE:, :]
    lat_ref[PLANES : 2 * PLANES, :] = near_ref[SIDE:KEEP, :]


def first_turn_kernel(lon_ref, lat_ref, strip_ref, back_ref):
    back_ref[: 2 * SIDE, :] = lon_ref[...]
    back_ref[2 * SIDE : STRIP, :] = lat_ref[...]
    back_ref[STRIP:, :] = strip_ref[...]


def second_turn_kernel(lon_ref, lat_ref, base_ref, back_ref, edge_ref):
    back_ref[:LIST, :] = lon_ref[:LIST, :]
    back_ref[LIST:SIDE, :] = lon_ref[SIDE + LIST :, :]
    back_ref[SIDE:, :] = lat_ref[PLANES : 2 * PLANES, :]
    edge_ref[:8, :] = lon_ref[LIST:SIDE, :]
    edge_ref[8:, :] = lat_ref[:PLANES, :]


def kept(list_ref, offset, entries, part_ref):
    source = 2 * lax.axis_index("sec")
    for b in range(BLOCKS):
        total = regrid(list_ref, offset, source, entries, b)
        for k in range(COMP):
            part_ref[k, 8 * b : 8 * b + 8, :] = total[k]


def first_kept_kernel(slot_ref, weight_ref, near_ref, lon_ref, part_ref, other_part_ref):
    kept(lon_ref, SIDE, own_entries(slot_ref, weight_ref), part_ref)
    kept(lon_ref, 0, near_entries(near_ref), other_part_ref)


def second_kept_kernel(slot_ref, weight_ref, lon_ref, part_ref):
    kept(lon_ref, SIDE, own_entries(slot_ref, weight_ref), part_ref)


def around(core, kept_side, passed_side, kept_row, passed_row):
    first = core == 0
    from_west = jnp.where(first, kept_side, passed_side)
    from_east = jnp.where(first, passed_side, kept_side)
    lane = lax.broadcasted_iota(jnp.int32, (8, LANES), 1)
    row = lax.broadcasted_iota(jnp.int32, (8, LANES), 0)

    def arrived(k, level, b):
        at = LEV * k + level
        j = PLANES * b + at
        edge_east = jnp.broadcast_to(from_east[:, j : j + 1], (8, LANES))
        edge_west = jnp.broadcast_to(from_west[:, j : j + 1], (8, LANES))
        edge = jnp.where(lane == LANES - 1, edge_east, jnp.where(lane == 0, edge_west, 0.0))
        if b == 0 or b == BLOCKS - 1:
            pair = (kept_row(at), passed_row(at)) if b == 0 else (passed_row(at), kept_row(at))
            end = jnp.broadcast_to(jnp.where(first, *pair), (8, LANES))
            edge = edge + jnp.where(row == (0 if b == 0 else 7), end, 0.0)
        return edge

    return arrived


def finish(core, base_ref, part_ref, entries, arrived, list_ref, out_ref, ready):
    for k in range(COMP):
        for level in range(1, LEV):
            for b in range(BLOCKS):
                rows = slice(8 * b, 8 * b + 8)
                out_ref[k, level, rows, :] = base_ref[k, level, rows, :] + arrived(k, level, b)
    ready()
    for b in range(BLOCKS):
        rows = slice(8 * b, 8 * b + 8)
        total = regrid(list_ref, 0, 2 - 2 * core, entries, b)
        for k in range(COMP):
            out_ref[k, 0, rows, :] = (base_ref[k, 0, rows, :] + arrived(k, 0, b)) + (part_ref[k, rows, :] + total[k])


def other_edges(core, surface_ref, near_ref, lat_ref, lon_ref, back_ref, out_lon_ref, out_lat_ref):
    first = core == 0
    half, last, column = direction(first)
    lane = lax.broadcasted_iota(jnp.int32, (8, LANES), 1)
    row = lax.broadcasted_iota(jnp.int32, (8, LANES), 0)
    passed_side = back_ref[LIST:SIDE, :]
    kept_side = lon_ref[SIDE + LIST :, :]
    from_west = jnp.where(first, kept_side, passed_side)
    from_east = jnp.where(first, passed_side, kept_side)

    corner_north = jnp.zeros((8, LANES), jnp.float32)
    corner_south = jnp.zeros((8, LANES), jnp.float32)
    for i in range(PLANES // 8):
        passed = back_ref[2 * SIDE + 8 * i : 2 * SIDE + 8 * i + 8, :]
        kept_rows = lat_ref[PLANES + 8 * i : PLANES + 8 * i + 8, :]
        south = pull(jnp.where(first, kept_rows, passed), column)
        north = pull(jnp.where(first, passed, kept_rows), column)
        corner_south = corner_south + jnp.where(lane == row + 8 * i, south, 0.0)
        corner_north = corner_north + jnp.where(lane == row + 8 * i + PLANES * (BLOCKS - 1), north, 0.0)
        index = row + 8 * i + jnp.where(first, PLANES * (BLOCKS - 1), 0)
        end_west = jnp.where(first, from_west[7:8], from_west[0:1])
        end_east = jnp.where(first, from_east[7:8], from_east[0:1])
        west = pull(jnp.broadcast_to(end_west, (8, LANES)), index)
        east = pull(jnp.broadcast_to(end_east, (8, LANES)), index)
        ends = jnp.where(lane == LANES - 1, east, jnp.where(lane == 0, west, 0.0))
        at = STRIP + 8 + 8 * i
        line = back_ref[at : at + 8, :] + passed + ends
        factor = back_ref[at + 8 + PLANES : at + 16 + PLANES, :]
        out_lat_ref[PLANES + 8 * i : PLANES + 8 * i + 8, :] = factor * line
    corner_south = jnp.broadcast_to(jnp.sum(corner_south, axis=0, keepdims=True), (8, LANES))
    corner_north = jnp.broadcast_to(jnp.sum(corner_north, axis=0, keepdims=True), (8, LANES))
    corner = jnp.where(row == 0, corner_south, jnp.where(row == 7, corner_north, 0.0))
    factor = back_ref[STRIP + 8 + PLANES : STRIP + 16 + PLANES, :]
    side = factor * (back_ref[STRIP : STRIP + 8, :] + passed_side + corner)

    across = near_ref[COEF : COEF + ROWS, :] + half * near_ref[COEF + ROWS : COEF + 2 * ROWS, :]
    along = near_ref[pl.ds(COEF + last, 1), :] + half * near_ref[pl.ds(COEF + 2 * ROWS + last, 1), :]
    for k in range(COMP):
        at = LEV * k
        product = across * surface_ref[k]
        for b in range(BLOCKS):
            side = jnp.where(lane == PLANES * b + at, pull(product[8 * b : 8 * b + 8], column), side)
        out_lat_ref[PLANES + at : PLANES + at + 1, :] = along * surface_ref[k, pl.ds(last, 1), :]
    out_lon_ref[SIDE + LIST :, :] = side


def middle_kernel(
    sens_ref, base_ref, part_ref, other_base_ref, other_part_ref, slot_ref, weight_ref, near_ref, lon_ref, lat_ref, back_ref,
    dif_ref, vel_ref, sea_ref, dist_ref, send_ref,
    out_ref, out_lon_ref, out_lat_ref, other_flux_ref, flux_ref, surface_ref,
):
    core = lax.axis_index("sec")
    arrived = around(
        core, lon_ref[LIST:SIDE, :], back_ref[SIDE + LIST : 2 * SIDE, :],
        lambda at: lat_ref[at : at + 1, :], lambda at: back_ref[2 * SIDE + PLANES + at : 2 * SIDE + PLANES + at + 1, :],
    )
    finish(core, base_ref, part_ref, own_entries(slot_ref, weight_ref), arrived, back_ref, out_ref, lambda: None)
    arrived = around(
        core, lon_ref[SIDE + LIST :, :], back_ref[LIST:SIDE, :],
        lambda at: lat_ref[PLANES + at : PLANES + at + 1, :], lambda at: back_ref[2 * SIDE + at : 2 * SIDE + at + 1, :],
    )
    for b in range(BLOCKS):
        rows = slice(8 * b, 8 * b + 8)
        total = regrid(back_ref, SIDE, 2 - 2 * core, near_entries(near_ref), b)
        for k in range(COMP):
            surface_ref[k, rows, :] = (other_base_ref[k, rows, :] + arrived(k, 0, b)) + (other_part_ref[k, rows, :] + total[k])
    fluxes([out_ref[k, 0] for k in range(COMP)], sens_ref, sea_weight(sea_ref, dist_ref), flux_ref)
    other_sens = near_ref[SENS : SENS + COMP, :]
    fluxes([surface_ref[k] for k in range(COMP)], other_sens, near_ref[SEA:SLOT, :], other_flux_ref)
    pick(flux_ref, send_ref[pl.ds(pl.multiple_of(16 - 16 * core, 8), 8), :], out_lon_ref, 0)
    cell = near_ref[pl.ds(pl.multiple_of(CELL + 16 - 16 * core, 8), 8), :].astype(jnp.int32)
    pick(other_flux_ref, cell, out_lon_ref, SIDE)
    edges(core == 0, out_ref, dif_ref, vel_ref, out_lon_ref, LIST, out_lat_ref, 0)
    other_edges(core, surface_ref, near_ref, lat_ref, lon_ref, back_ref, out_lon_ref, out_lat_ref)


def last_kernel(base_ref, part_ref, slot_ref, weight_ref, edge_ref, back_ref, out_hbm, out_ref, sems):
    core = lax.axis_index("sec")
    deep = pltpu.make_async_copy(out_ref.at[:, pl.ds(1, LEV - 1)], out_hbm.at[:, pl.ds(1, LEV - 1)], sems.at[0])
    top = pltpu.make_async_copy(out_ref.at[:, 0], out_hbm.at[:, 0], sems.at[1])
    arrived = around(
        core, edge_ref[:8, :], back_ref[LIST:SIDE, :],
        lambda at: edge_ref[8 + at : 9 + at, :], lambda at: back_ref[SIDE + at : SIDE + at + 1, :],
    )
    finish(core, base_ref, part_ref, own_entries(slot_ref, weight_ref), arrived, back_ref, out_ref, deep.start)
    top.start()
    deep.wait()
    top.wait()


def call(kernel, arrays, outs, scratch=(), space=pltpu.VMEM, out_space=pltpu.VMEM, cost=1 << 20):
    in_space = pl.BlockSpec(memory_space=space)
    to_space = pl.BlockSpec(memory_space=out_space)
    return pl.pallas_call(
        kernel,
        out_shape=[jax.ShapeDtypeStruct(shape, jnp.float32) for shape in outs],
        in_specs=[in_space] * len(arrays),
        out_specs=[to_space] * len(outs),
        scratch_shapes=list(scratch),
        compiler_params=pltpu.CompilerParams(vmem_limit_bytes=8 << 20),
        cost_estimate=pl.CostEstimate(flops=cost, transcendentals=0, bytes_accessed=cost),
    )(*arrays)


def routes(axis):
    count = lax.axis_size(axis)
    periodic = axis == "lon"
    pairs = []
    for i in range(count):
        if periodic or i + 1 < count:
            pairs.append((i, (i + 1) % count))
        if periodic or i > 0:
            pairs.append((count + i, count + (i - 1) % count))
    return pairs


def on_device(
    adjoint,
    diffusivity,
    velocity,
    sensitivity,
    sea_mask,
    coast_distance,
    send_cells,
    recv_slots,
    regrid_weight,
):
    field = adjoint[0]
    sens = sensitivity[0]
    dif, vel = diffusivity[0], velocity[0]
    send = (sea_mask[0], coast_distance[0], send_cells.reshape(8 * PEERS, LANES))
    take = (recv_slots[0], regrid_weight[0])
    swap = [(0, 1), (1, 0)]
    surface = (COMP, ROWS, LANES)
    lon_rows, lat_rows = (2 * SIDE, LANES), (2 * PLANES, LANES)
    fresh = (sens, field, dif, vel, *send, *take)
    held = [pltpu.VMEM(a.shape, a.dtype) for a in fresh]
    fresh = [pltpu.with_memory_space_constraint(a, pltpu.HBM) for a in fresh]
    sems = pltpu.SemaphoreType.DMA((10,))
    give, flux = call(start_kernel, fresh, [(FIRST, LANES), surface], [*held, sems], pltpu.HBM)

    near = lax.ppermute(give, "sec", swap)
    (keep,) = call(keep_kernel, (field, dif, vel, send[2], flux), [(KEEP, LANES)])
    lon, lat = call(send_kernel, (keep, near), [lon_rows, lat_rows])
    lon = lax.ppermute(lon, ("sec", "lon"), routes("lon"))
    lat = lax.ppermute(lat, ("sec", "lat"), routes("lat"))
    base, other_base, strip = call(
        first_inner_kernel, (field, dif, vel, *take, near, give), [field.shape, surface, (BACK - STRIP, LANES)]
    )
    (back,) = call(first_turn_kernel, (lon, lat, strip), [(BACK, LANES)])
    back = lax.ppermute(back, "sec", swap)
    part, other_part = call(first_kept_kernel, (*take, near, lon), [surface, surface])

    scratch = [pltpu.VMEM(surface, jnp.float32)] * 2
    field, lon, lat, flux = call(
        middle_kernel,
        (sens, base, part, other_base, other_part, *take, near, lon, lat, back, dif, vel, *send),
        [field.shape, lon_rows, lat_rows, surface],
        scratch,
    )
    lon = lax.ppermute(lon, ("sec", "lon"), routes("lon"))
    lat = lax.ppermute(lat, ("sec", "lat"), routes("lat"))
    scratch = [pltpu.VMEM((LIST, LANES), jnp.float32)]
    (base,) = call(second_inner_kernel, (field, dif, vel, *take, near, flux), [field.shape], scratch)
    back, edge = call(second_turn_kernel, (lon, lat, base), [(KEEP, LANES), (8 + PLANES, LANES)])
    back = lax.ppermute(back, "sec", swap)
    (part,) = call(second_kept_kernel, (*take, lon), [surface])
    scratch = [pltpu.VMEM(field.shape, jnp.float32), pltpu.SemaphoreType.DMA((2,))]
    (field,) = call(last_kernel, (base, part, *take, edge, back), [field.shape], scratch, out_space=pltpu.HBM)
    return field[None]


def solution(mesh):
    placed = (
        P("sec", None, None, "lat", "lon"),
        P("sec", None, "lat", "lon"),
        P("sec", None, None, "lat", "lon"),
        P("sec", None, None),
        P("sec", "lat", "lon"),
        P("sec", "lat", "lon"),
        P("sec", "lat", "lon", None),
        P("sec", None, "lat", "lon"),
        P("sec", None, "lat", "lon"),
    )
    return jax.shard_map(
        on_device,
        mesh=mesh,
        in_specs=placed,
        out_specs=P("sec", None, None, "lat", "lon"),
        check_vma=False,
    )
```

time: 44.7 us -> 43.6 us (0.975)
  waiting for transfers between devices: 12 us -> 10.1 us
  Pallas kernels: 8.13 us -> 10 us
  starting transfers between devices: 24 us -> 22.3 us
  local copies, waits for them, and re-layouts: 0.04 us -> 0.7 us
    pallas_call x13 -> x11, Pallas kernels: 8.13 us -> 10 us  [call(): pl.pallas_call(kernel, out_shape=[jax.ShapeDtypeStruct(shape, jnp.float32...]
    ppermute x8 -> x7, waiting for transfers between devices: 12 us -> 10.1 us  [the longest x2 9.07 us: on_device(): lat = lax.ppermute(lat, ('sec', 'lat'), routes('lat'))]
    ppermute x8 -> x7, starting transfers between devices: 24 us -> 22.3 us  [the longest x1 8.78 us: on_device(): near = lax.ppermute(give, 'sec', swap)]
    unnamed x18, local copies, waits for them, and re-layouts: 0.04 us -> 0.7 us
  transfers between devices with their start and end apart: 8 -> 7, of which waited for: 6 -> 4; matrix products, arithmetic and copies ran while one was open for 0% -> 0% of each run, Pallas kernels for 8% -> 11%
where the time goes in v5:
time: 43.6 us; the launch traced here: 43.3 us
  starting transfers between devices  22.3 us (51%)
  waiting for transfers between devices  10.1 us (23%)
  Pallas kernels  10 us (23%)
  local copies, waits for them, and re-layouts  0.7 us (2%)
    pallas_call x11, Pallas kernels, call(): pl.pallas_call(kernel, out_shape=[jax.ShapeDtypeStruct(shape, jnp.float32...  10 us
    ppermute x2, waiting for transfers between devices, on_device(): lat = lax.ppermute(lat, ('sec', 'lat'), routes('lat'))  9.07 us
    ppermute x1, starting transfers between devices, on_device(): near = lax.ppermute(give, 'sec', swap)  8.78 us
    ppermute x2, starting transfers between devices, on_device(): lon = lax.ppermute(lon, ('sec', 'lon'), routes('lon'))  6.74 us
    ppermute x2, starting transfers between devices, on_device(): back = lax.ppermute(back, 'sec', swap)  4.16 us
    ppermute x2, starting transfers between devices, on_device(): lat = lax.ppermute(lat, ('sec', 'lat'), routes('lat'))  2.58 us
  transfers between devices with their start and end apart: 7, of which 4 were waited for; matrix products, arithmetic and copies ran while one was open for 0% of the time, Pallas kernels for 11%

profile of v5, /device:TPU:1, one launch (start us, length us, event | category | flops | bytes accessed | tf_op | source)
XLA Modules:
  0.0 43.3 jit_solution(18057248115257630652)
XLA Ops:
  0.0 0.0 copy-start
  0.0 0.0 copy-start.3
  0.0 0.0 copy-start.4
  0.0 0.0 copy-start.5
  0.0 1.7 %shard_map.91 = (f32[632,128]{1,0:T(8,128)S(1)}, f32[4,32,128]{2,1,0:T(8,128)S(1)}) custom-call(f32[4,4]{1,0:T(4,128)} %bitcast.44, f32[4,4,32,128]{3,2,1,0:T(8,128)} %bitcast.29, f32[4,32,128]{2,1,0:T(8,128)} %bitcast.32, f32[2,4,32,128]{3,2,1,0:T(8,128)} %bitcast.10, s32[32,128]{1,0:T(8,128)} %bitcast.40, s32[32,128]{1,0:T(8,128)} %bitcast.42, ...), custom_call_target="tpu_custom_call" | custom-call | flops 1048576 | bytes 1048576 | tf_op jit(solution)/shard_map/pallas_call | solution.py:396
  1.7 8.8 %collective-permute-start = (f32[632,128]{1,0:T(8,128)S(1)}, f32[632,128]{1,0:T(8,128)S(1)}, u32[]{:S(2)}, u32[]{:S(2)}) collective-permute-start(f32[632,128]{1,0:T(8,128)S(1)} %get-tuple-element.20.give_ref), channel_id=1, source_target_pairs={{0,256},{256,0},{1,257},{257,1},{2,258},{258,2},{3,259},{259,3},{4... | collective-permute-start | bytes 970760 | tf_op jit(solution)/shard_map/ppermute | solution.py:444
  10.5 0.0 copy-done
  10.5 0.0 copy-done.3
  10.5 0.0 copy-done.4
  10.5 0.0 copy-done.5
  10.5 0.3 shard_map.93.keep_ref
  10.8 0.0 copy-start.1
  10.8 0.0 copy-start.2
  10.8 0.9 %collective-permute-done.near_ref = f32[632,128]{1,0:T(8,128)S(1)} collective-permute-done((f32[632,128]{1,0:T(8,128)S(1)}, f32[632,128]{1,0:T(8,128)S(1)}, u32[]{:S(2)}, u32[]{:S(2)}) %collective-permute-start) | collective-permute-done | bytes 323616 | tf_op jit(solution)/shard_map/ppermute | solution.py:444
  11.7 3.7 %collective-permute-start.1 = (f32[80,128]{1,0:T(8,128)S(1)}, f32[80,128]{1,0:T(8,128)S(1)}, u32[]{:S(2)}, u32[]{:S(2)}) collective-permute-start(f32[80,128]{1,0:T(8,128)S(1)} %get-tuple-element.23), channel_id=1, source_target_pairs={{0,1},{256,319},{1,2},{257,256},{2,3},{258,257},{3,4},{259,258},{4... | collective-permute-start | bytes 122888 | tf_op jit(solution)/shard_map/ppermute | solution.py:447
  15.5 1.3 %collective-permute-start.2 = (f32[32,128]{1,0:T(8,128)S(1)}, f32[32,128]{1,0:T(8,128)S(1)}, u32[]{:S(2)}, u32[]{:S(2)}) collective-permute-start(f32[32,128]{1,0:T(8,128)S(1)} %get-tuple-element.27), channel_id=1, source_target_pairs={{0,64},{64,128},{320,256},{128,192},{384,320},{448,384},{1,65},{65... | collective-permute-start | bytes 49160 | tf_op jit(solution)/shard_map/ppermute | solution.py:448
  16.8 0.0 copy-done.1
  16.8 0.0 copy-done.2
  16.8 1.5 %shard_map.92 = (f32[4,4,32,128]{3,2,1,0:T(8,128)S(1)}, f32[4,32,128]{2,1,0:T(8,128)S(1)}, f32[48,128]{1,0:T(8,128)S(1)}) custom-call(f32[4,4,32,128]{3,2,1,0:T(8,128)S(1)} %bitcast.31, f32[4,32,128]{2,1,0:T(8,128)S(1)} %bitcast.34, f32[2,4,32,128]{3,2,1,0:T(8,128)S(1)} %bitcast.12, s32[4,32,128]{2,1,0:T(8,128)S(1)} %bitcast.16, f32[4,32,128]{2,1,0:T(8,128)S(1)} %bitcast.23, ...), custom_call_target="tpu_custom_call" | custom-call | flops 1048576 | bytes 1048576 | tf_op jit(solution)/shard_map/pallas_call | solution.py:396
  18.3 4.1 %collective-permute-done.2.lat_ref = f32[32,128]{1,0:T(8,128)S(1)} collective-permute-done((f32[32,128]{1,0:T(8,128)S(1)}, f32[32,128]{1,0:T(8,128)S(1)}, u32[]{:S(2)}, u32[]{:S(2)}) %collective-permute-start.2) | collective-permute-done | bytes 16416 | tf_op jit(solution)/shard_map/ppermute | solution.py:448
  22.4 0.0 collective-permute-done.1.lon_ref
  22.4 1.9 %collective-permute-start.3 = (f32[160,128]{1,0:T(8,128)S(1)}, f32[160,128]{1,0:T(8,128)S(1)}, u32[]{:S(2)}, u32[]{:S(2)}) collective-permute-start(f32[160,128]{1,0:T(8,128)S(1)} %shard_map.96), channel_id=1, source_target_pairs={{0,256},{256,0},{1,257},{257,1},{2,258},{258,2},{3,259},{259,3},{4... | collective-permute-start | bytes 245768 | tf_op jit(solution)/shard_map/ppermute | solution.py:453
  24.3 0.0 copy-start.6
  24.3 0.0 copy-start.7
  24.4 1.3 %shard_map.95 = (f32[4,32,128]{2,1,0:T(8,128)S(1)}, f32[4,32,128]{2,1,0:T(8,128)S(1)}) custom-call(s32[4,32,128]{2,1,0:T(8,128)S(1)} %bitcast.17, f32[4,32,128]{2,1,0:T(8,128)S(1)} %bitcast.24, f32[632,128]{1,0:T(8,128)S(1)} %collective-permute-done.near_ref, f32[80,128]{1,0:T(8,128)S(1)} %collective-permute-done.1.lon_ref), custom_call_target="tpu_custom_call" | custom-call | flops 1048576 | bytes 1048576 | tf_op jit(solution)/shard_map/pallas_call | solution.py:396
  25.6 0.0 collective-permute-done.3.back_ref
  25.6 0.0 copy-start.8
  25.6 0.0 copy-done.6
  25.6 0.0 copy-done.7
  25.7 0.7 %copy-done.8 = f32[1,4,4]{2,1,0:T(4,128)S(1)} copy-done((f32[1,4,4]{2,1,0:T(4,128)S(1)}, f32[1,4,4]{2,1,0:T(4,128)}, u32[]{:S(2)}) %copy-start.8) | copy-done | bytes 88
  26.3 2.1 %shard_map.97 = (f32[4,4,32,128]{3,2,1,0:T(8,128)S(1)}, f32[80,128]{1,0:T(8,128)S(1)}, f32[32,128]{1,0:T(8,128)S(1)}, f32[4,32,128]{2,1,0:T(8,128)S(1)}) custom-call(f32[4,4]{1,0:T(4,128)S(1)} %bitcast.45, f32[4,4,32,128]{3,2,1,0:T(8,128)S(1)} %get-tuple-element.21.base_ref, f32[4,32,128]{2,1,0:T(8,128)S(1)} %get-tuple-element.24.part_ref, ...), custom_call_target="tpu_custom_call" | custom-call | flops 1048576 | bytes 1048576 | tf_op jit(solution)/shard_map/pallas_call | solution.py:396
  28.4 3.0 %collective-permute-start.4 = (f32[80,128]{1,0:T(8,128)S(1)}, f32[80,128]{1,0:T(8,128)S(1)}, u32[]{:S(2)}, u32[]{:S(2)}) collective-permute-start(f32[80,128]{1,0:T(8,128)S(1)} %get-tuple-element.31), channel_id=1, source_target_pairs={{0,1},{256,319},{1,2},{257,256},{2,3},{258,257},{3,4},{259,258},{4... | collective-permute-start | bytes 122888 | tf_op jit(solution)/shard_map/ppermute | solution.py:463
  31.4 1.3 %collective-permute-start.5 = (f32[32,128]{1,0:T(8,128)S(1)}, f32[32,128]{1,0:T(8,128)S(1)}, u32[]{:S(2)}, u32[]{:S(2)}) collective-permute-start(f32[32,128]{1,0:T(8,128)S(1)} %get-tuple-element.32), channel_id=1, source_target_pairs={{0,64},{64,128},{320,256},{128,192},{384,320},{448,384},{1,65},{65... | collective-permute-start | bytes 49160 | tf_op jit(solution)/shard_map/ppermute | solution.py:464
  32.7 1.0 %shard_map.98.base_ref = f32[4,4,32,128]{3,2,1,0:T(8,128)S(1)} custom-call(f32[4,4,32,128]{3,2,1,0:T(8,128)S(1)} %get-tuple-element.29.field_ref, f32[4,32,128]{2,1,0:T(8,128)S(1)} %bitcast.36, f32[2,4,32,128]{3,2,1,0:T(8,128)S(1)} %bitcast.14, s32[4,32,128]{2,1,0:T(8,128)S(1)} %bitcast.19, f32[4,32,128]{2,1,0:T(8,128)S(1)} %bitcast.26, ...), custom_call_target="tpu_custom_call" | custom-call | flops 1048576 | bytes 1048576 | tf_op jit(solution)/shard_map/pallas_call | solution.py:396
  33.7 5.0 %collective-permute-done.5.lat_ref = f32[32,128]{1,0:T(8,128)S(1)} collective-permute-done((f32[32,128]{1,0:T(8,128)S(1)}, f32[32,128]{1,0:T(8,128)S(1)}, u32[]{:S(2)}, u32[]{:S(2)}) %collective-permute-start.5) | collective-permute-done | bytes 16416 | tf_op jit(solution)/shard_map/ppermute | solution.py:464
  38.7 0.0 collective-permute-done.4.lon_ref
  38.7 2.2 %collective-permute-start.6 = (f32[56,128]{1,0:T(8,128)S(1)}, f32[56,128]{1,0:T(8,128)S(1)}, u32[]{:S(2)}, u32[]{:S(2)}) collective-permute-start(f32[56,128]{1,0:T(8,128)S(1)} %get-tuple-element.34), channel_id=1, source_target_pairs={{0,256},{256,0},{1,257},{257,1},{2,258},{258,2},{3,259},{259,3},{4... | collective-permute-start | bytes 86024 | tf_op jit(solution)/shard_map/ppermute | solution.py:468
  40.9 0.7 %shard_map.99.part_ref = f32[4,32,128]{2,1,0:T(8,128)S(1)} custom-call(s32[4,32,128]{2,1,0:T(8,128)S(1)} %bitcast.20, f32[4,32,128]{2,1,0:T(8,128)S(1)} %bitcast.27, f32[80,128]{1,0:T(8,128)S(1)} %collective-permute-done.4.lon_ref), custom_call_target="tpu_custom_call" | custom-call | flops 1048576 | bytes 1048576 | tf_op jit(solution)/shard_map/pallas_call | solution.py:396
  41.6 0.2 collective-permute-done.6.back_ref
  41.8 1.5 %shard_map.101 = f32[4,4,32,128]{3,2,1,0:T(8,128)} custom-call(f32[4,4,32,128]{3,2,1,0:T(8,128)S(1)} %shard_map.98.base_ref, f32[4,32,128]{2,1,0:T(8,128)S(1)} %shard_map.99.part_ref, s32[4,32,128]{2,1,0:T(8,128)S(1)} %bitcast.21, f32[4,32,128]{2,1,0:T(8,128)S(1)} %bitcast.28, f32[24,128]{1,0:T(8,128)S(1)} %get-tuple-element.33.edge_ref, ...), custom_call_target="tpu_custom_call" | custom-call | flops 1048576 | bytes 1048576 | tf_op jit(solution)/shard_map/pallas_call | solution.py:396
  (3 shorter events, 0.0 us)
Async XLA Ops:
  0.0 10.5 %copy-start = (f32[1,2,4,32,128]{4,3,2,1,0:T(8,128)S(1)}, f32[1,2,4,32,128]{4,3,2,1,0:T(8,128)}, u32[]{:S(2)}) copy-start(f32[1,2,4,32,128]{4,3,2,1,0:T(8,128)} %param.11) | copy-start | bytes 393220
  0.0 10.5 %copy-start.3 = (f32[1,4,4,32,128]{4,3,2,1,0:T(8,128)S(1)}, f32[1,4,4,32,128]{4,3,2,1,0:T(8,128)}, u32[]{:S(2)}) copy-start(f32[1,4,4,32,128]{4,3,2,1,0:T(8,128)} %param.9) | copy-start | bytes 786436
  0.0 10.5 %copy-start.4 = (f32[1,4,32,128]{3,2,1,0:T(8,128)S(1)}, f32[1,4,32,128]{3,2,1,0:T(8,128)}, u32[]{:S(2)}) copy-start(f32[1,4,32,128]{3,2,1,0:T(8,128)} %param.10) | copy-start | bytes 196612
  0.0 10.5 %copy-start.5 = (s32[1,1,3,1024]{3,1,2,0:T(1,128)S(1)}, s32[1,1,3,1024]{3,1,2,0:T(1,128)}, u32[]{:S(2)}) copy-start(s32[1,1,3,1024]{3,1,2,0:T(1,128)} %param.15) | copy-start | bytes 36868
  1.7 10.0 %collective-permute-start = (f32[632,128]{1,0:T(8,128)S(1)}, f32[632,128]{1,0:T(8,128)S(1)}, u32[]{:S(2)}, u32[]{:S(2)}) collective-permute-start(f32[632,128]{1,0:T(8,128)S(1)} %get-tuple-element.20.give_ref), channel_id=1, source_target_pairs={{0,256},{256,0},{1,257},{257,1},{2,258},{258,2},{3,259},{259,3},{4... | collective-permute-start | bytes 970760 | tf_op jit(solution)/shard_map/ppermute | solution.py:444
  10.8 5.9 %copy-start.1 = (s32[1,4,32,128]{3,2,1,0:T(8,128)S(1)}, s32[1,4,32,128]{3,2,1,0:T(8,128)}, u32[]{:S(2)}) copy-start(s32[1,4,32,128]{3,2,1,0:T(8,128)} %param.16) | copy-start | bytes 196612
  10.8 5.9 %copy-start.2 = (f32[1,4,32,128]{3,2,1,0:T(8,128)S(1)}, f32[1,4,32,128]{3,2,1,0:T(8,128)}, u32[]{:S(2)}) copy-start(f32[1,4,32,128]{3,2,1,0:T(8,128)} %param.17) | copy-start | bytes 196612
  11.7 10.7 %collective-permute-start.1 = (f32[80,128]{1,0:T(8,128)S(1)}, f32[80,128]{1,0:T(8,128)S(1)}, u32[]{:S(2)}, u32[]{:S(2)}) collective-permute-start(f32[80,128]{1,0:T(8,128)S(1)} %get-tuple-element.23), channel_id=1, source_target_pairs={{0,1},{256,319},{1,2},{257,256},{2,3},{258,257},{3,4},{259,258},{4... | collective-permute-start | bytes 122888 | tf_op jit(solution)/shard_map/ppermute | solution.py:447
  15.5 6.9 %collective-permute-start.2 = (f32[32,128]{1,0:T(8,128)S(1)}, f32[32,128]{1,0:T(8,128)S(1)}, u32[]{:S(2)}, u32[]{:S(2)}) collective-permute-start(f32[32,128]{1,0:T(8,128)S(1)} %get-tuple-element.27), channel_id=1, source_target_pairs={{0,64},{64,128},{320,256},{128,192},{384,320},{448,384},{1,65},{65... | collective-permute-start | bytes 49160 | tf_op jit(solution)/shard_map/ppermute | solution.py:448
  22.4 3.2 %collective-permute-start.3 = (f32[160,128]{1,0:T(8,128)S(1)}, f32[160,128]{1,0:T(8,128)S(1)}, u32[]{:S(2)}, u32[]{:S(2)}) collective-permute-start(f32[160,128]{1,0:T(8,128)S(1)} %shard_map.96), channel_id=1, source_target_pairs={{0,256},{256,0},{1,257},{257,1},{2,258},{258,2},{3,259},{259,3},{4... | collective-permute-start | bytes 245768 | tf_op jit(solution)/shard_map/ppermute | solution.py:453
  24.3 1.3 %copy-start.6 = (s32[1,32,128]{2,1,0:T(8,128)S(1)}, s32[1,32,128]{2,1,0:T(8,128)}, u32[]{:S(2)}) copy-start(s32[1,32,128]{2,1,0:T(8,128)} %param.13) | copy-start | bytes 49156
  24.3 1.3 %copy-start.7 = (s32[1,32,128]{2,1,0:T(8,128)S(1)}, s32[1,32,128]{2,1,0:T(8,128)}, u32[]{:S(2)}) copy-start(s32[1,32,128]{2,1,0:T(8,128)} %param.14) | copy-start | bytes 49156
  25.6 0.7 %copy-start.8 = (f32[1,4,4]{2,1,0:T(4,128)S(1)}, f32[1,4,4]{2,1,0:T(4,128)}, u32[]{:S(2)}) copy-start(f32[1,4,4]{2,1,0:T(4,128)} %param.12) | copy-start | bytes 196
  28.4 10.3 %collective-permute-start.4 = (f32[80,128]{1,0:T(8,128)S(1)}, f32[80,128]{1,0:T(8,128)S(1)}, u32[]{:S(2)}, u32[]{:S(2)}) collective-permute-start(f32[80,128]{1,0:T(8,128)S(1)} %get-tuple-element.31), channel_id=1, source_target_pairs={{0,1},{256,319},{1,2},{257,256},{2,3},{258,257},{3,4},{259,258},{4... | collective-permute-start | bytes 122888 | tf_op jit(solution)/shard_map/ppermute | solution.py:463
  31.4 7.3 %collective-permute-start.5 = (f32[32,128]{1,0:T(8,128)S(1)}, f32[32,128]{1,0:T(8,128)S(1)}, u32[]{:S(2)}, u32[]{:S(2)}) collective-permute-start(f32[32,128]{1,0:T(8,128)S(1)} %get-tuple-element.32), channel_id=1, source_target_pairs={{0,64},{64,128},{320,256},{128,192},{384,320},{448,384},{1,65},{65... | collective-permute-start | bytes 49160 | tf_op jit(solution)/shard_map/ppermute | solution.py:464
  38.7 3.1 %collective-permute-start.6 = (f32[56,128]{1,0:T(8,128)S(1)}, f32[56,128]{1,0:T(8,128)S(1)}, u32[]{:S(2)}, u32[]{:S(2)}) collective-permute-start(f32[56,128]{1,0:T(8,128)S(1)} %get-tuple-element.34), channel_id=1, source_target_pairs={{0,256},{256,0},{1,257},{257,1},{2,258},{258,2},{3,259},{259,3},{4... | collective-permute-start | bytes 86024 | tf_op jit(solution)/shard_map/ppermute | solution.py:468

commit v6 on v5

--- a/solution.py
+++ b/solution.py
@@ -58,13 +58,9 @@
     return total
 
 
-def own_entries(slot_ref, weight_ref):
-    return (lambda t, b: slot_ref[t, 8 * b : 8 * b + 8, :]), (lambda t, b: weight_ref[t, 8 * b : 8 * b + 8, :])
-
-
-def near_entries(near_ref):
+def entries_of(message_ref):
     def rows(base, t, b):
-        return near_ref[base + ROWS * t + 8 * b : base + ROWS * t + 8 * b + 8, :]
+        return message_ref[base + ROWS * t + 8 * b : base + ROWS * t + 8 * b + 8, :]
 
     return (lambda t, b: rows(SLOT, t, b).astype(jnp.int32)), (lambda t, b: rows(WEIGHT, t, b))
 
@@ -117,12 +113,6 @@
 def given(core, flux_ref, send_ref, give_ref):
     pick(flux_ref, send_ref[pl.ds(pl.multiple_of(16 * core, 8), 8), :], give_ref, 0)
     pick(flux_ref, send_ref[8:16, :], give_ref, KEEP)
-
-
-def keep_kernel(field_ref, dif_ref, vel_ref, send_ref, flux_ref, keep_ref):
-    core = lax.axis_index("sec")
-    pick(flux_ref, send_ref[pl.ds(pl.multiple_of(16 - 16 * core, 8), 8), :], keep_ref, 0)
-    edges(core == 0, field_ref, dif_ref, vel_ref, keep_ref, LIST, keep_ref, SIDE)
 
 
 def sea_weight(sea_ref, dist_ref):
@@ -175,31 +165,19 @@
     return plane - 4.0 * (dif * plane) + ((north + south) + (east + west))
 
 
-def inner(field_ref, dif_ref, vel_ref, entries, list_ref, offset, base_ref):
+def cells_of(message_ref, d):
+    return message_ref[pl.ds(pl.multiple_of(CELL + 8 * d, 8), 8), :].astype(jnp.int32)
+
+
+def keep_kernel(field_ref, dif_ref, vel_ref, give_ref, flux_ref, keep_ref, base_ref, strip_ref):
+    core = lax.axis_index("sec")
+    pick(flux_ref, cells_of(give_ref, 2 - 2 * core), keep_ref, 0)
+    edges(core == 0, field_ref, dif_ref, vel_ref, keep_ref, LIST, keep_ref, SIDE)
     for level in range(LEV):
         for k in range(COMP):
             base_ref[k, level] = inside(field_ref[k, level], dif_ref[level], 0.5 * vel_ref[0, level], 0.5 * vel_ref[1, level])
-    for b in range(BLOCKS):
-        rows = slice(8 * b, 8 * b + 8)
-        total = regrid(list_ref, offset, 1, entries, b)
-        for k in range(COMP):
-            base_ref[k, 0, rows, :] = base_ref[k, 0, rows, :] + total[k]
-
-
-def first_inner_kernel(field_ref, dif_ref, vel_ref, slot_ref, weight_ref, near_ref, give_ref, base_ref, other_ref, strip_ref):
-    inner(field_ref, dif_ref, vel_ref, own_entries(slot_ref, weight_ref), near_ref, KEEP, base_ref)
-    dif = near_ref[COEF : COEF + ROWS, :]
-    half_u = 0.5 * near_ref[COEF + ROWS : COEF + 2 * ROWS, :]
-    half_v = 0.5 * near_ref[COEF + 2 * ROWS : COEF + 3 * ROWS, :]
-    for k in range(COMP):
-        other_ref[k] = inside(near_ref[SURFACE + ROWS * k : SURFACE + ROWS * k + ROWS, :], dif, half_u, half_v)
-    for b in range(BLOCKS):
-        rows = slice(8 * b, 8 * b + 8)
-        total = regrid(give_ref, KEEP, 1, near_entries(near_ref), b)
-        for k in range(COMP):
-            other_ref[k, rows, :] = other_ref[k, rows, :] + total[k]
-
-    half, last, column = direction(lax.axis_index("sec") != 0)
+
+    half, last, column = direction(core != 0)
     lane = lax.broadcasted_iota(jnp.int32, (8, LANES), 1)
     side = jnp.zeros((8, LANES), jnp.float32)
     factor = jnp.zeros((8, LANES), jnp.float32)
@@ -221,9 +199,29 @@
     strip_ref[8 + PLANES : 16 + PLANES, :] = factor
 
 
-def second_inner_kernel(field_ref, dif_ref, vel_ref, slot_ref, weight_ref, near_ref, flux_ref, base_ref, list_ref):
-    pick(flux_ref, near_ref[CELL + 8 : CELL + 16, :].astype(jnp.int32), list_ref, 0)
-    inner(field_ref, dif_ref, vel_ref, own_entries(slot_ref, weight_ref), list_ref, 0, base_ref)
+def first_inner_kernel(give_ref, near_ref, centre_ref, other_base_ref, other_centre_ref):
+    dif = near_ref[COEF : COEF + ROWS, :]
+    half_u = 0.5 * near_ref[COEF + ROWS : COEF + 2 * ROWS, :]
+    half_v = 0.5 * near_ref[COEF + 2 * ROWS : COEF + 3 * ROWS, :]
+    for k in range(COMP):
+        other_base_ref[k] = inside(near_ref[SURFACE + ROWS * k : SURFACE + ROWS * k + ROWS, :], dif, half_u, half_v)
+    for b in range(BLOCKS):
+        own = regrid(near_ref, KEEP, 1, entries_of(give_ref), b)
+        other = regrid(give_ref, KEEP, 1, entries_of(near_ref), b)
+        for k in range(COMP):
+            centre_ref[k, 8 * b : 8 * b + 8, :] = own[k]
+            other_centre_ref[k, 8 * b : 8 * b + 8, :] = other[k]
+
+
+def second_inner_kernel(field_ref, dif_ref, vel_ref, give_ref, near_ref, flux_ref, base_ref, centre_ref, list_ref):
+    for level in range(LEV):
+        for k in range(COMP):
+            base_ref[k, level] = inside(field_ref[k, level], dif_ref[level], 0.5 * vel_ref[0, level], 0.5 * vel_ref[1, level])
+    pick(flux_ref, cells_of(near_ref, 1), list_ref, 0)
+    for b in range(BLOCKS):
+        total = regrid(list_ref, 0, 1, entries_of(give_ref), b)
+        for k in range(COMP):
+            centre_ref[k, 8 * b : 8 * b + 8, :] = total[k]
 
 
 def send_kernel(keep_ref, near_ref, lon_ref, lat_ref):
@@ -233,7 +231,7 @@
     lat_ref[PLANES : 2 * PLANES, :] = near_ref[SIDE:KEEP, :]
 
 
-def first_turn_kernel(lon_ref, lat_ref, strip_ref, back_ref):
+def first_turn_kernel(lon_ref, lat_ref, strip_ref, centre_ref, back_ref):
     back_ref[: 2 * SIDE, :] = lon_ref[...]
     back_ref[2 * SIDE : STRIP, :] = lat_ref[...]
     back_ref[STRIP:, :] = strip_ref[...]
@@ -247,21 +245,22 @@
     edge_ref[8:, :] = lat_ref[:PLANES, :]
 
 
-def kept(list_ref, offset, entries, part_ref):
+def kept(list_ref, offset, entries, centre_ref, part_ref):
     source = 2 * lax.axis_index("sec")
     for b in range(BLOCKS):
+        rows = slice(8 * b, 8 * b + 8)
         total = regrid(list_ref, offset, source, entries, b)
         for k in range(COMP):
-            part_ref[k, 8 * b : 8 * b + 8, :] = total[k]
-
-
-def first_kept_kernel(slot_ref, weight_ref, near_ref, lon_ref, part_ref, other_part_ref):
-    kept(lon_ref, SIDE, own_entries(slot_ref, weight_ref), part_ref)
-    kept(lon_ref, 0, near_entries(near_ref), other_part_ref)
-
-
-def second_kept_kernel(slot_ref, weight_ref, lon_ref, part_ref):
-    kept(lon_ref, SIDE, own_entries(slot_ref, weight_ref), part_ref)
+            part_ref[k, rows, :] = centre_ref[k, rows, :] + total[k]
+
+
+def first_kept_kernel(give_ref, near_ref, lon_ref, centre_ref, other_centre_ref, part_ref, other_part_ref):
+    kept(lon_ref, SIDE, entries_of(give_ref), centre_ref, part_ref)
+    kept(lon_ref, 0, entries_of(near_ref), other_centre_ref, other_part_ref)
+
+
+def second_kept_kernel(give_ref, lon_ref, centre_ref, part_ref):
+    kept(lon_ref, SIDE, entries_of(give_ref), centre_ref, part_ref)
 
 
 def around(core, kept_side, passed_side, kept_row, passed_row):
@@ -347,8 +346,7 @@
 
 
 def middle_kernel(
-    sens_ref, base_ref, part_ref, other_base_ref, other_part_ref, slot_ref, weight_ref, near_ref, lon_ref, lat_ref, back_ref,
-    dif_ref, vel_ref, sea_ref, dist_ref, send_ref,
+    base_ref, part_ref, other_base_ref, other_part_ref, give_ref, near_ref, lon_ref, lat_ref, back_ref, dif_ref, vel_ref,
     out_ref, out_lon_ref, out_lat_ref, other_flux_ref, flux_ref, surface_ref,
 ):
     core = lax.axis_index("sec")
@@ -356,27 +354,27 @@
         core, lon_ref[LIST:SIDE, :], back_ref[SIDE + LIST : 2 * SIDE, :],
         lambda at: lat_ref[at : at + 1, :], lambda at: back_ref[2 * SIDE + PLANES + at : 2 * SIDE + PLANES + at + 1, :],
     )
-    finish(core, base_ref, part_ref, own_entries(slot_ref, weight_ref), arrived, back_ref, out_ref, lambda: None)
+    finish(core, base_ref, part_ref, entries_of(give_ref), arrived, back_ref, out_ref, lambda: None)
     arrived = around(
         core, lon_ref[SIDE + LIST :, :], back_ref[LIST:SIDE, :],
         lambda at: lat_ref[PLANES + at : PLANES + at + 1, :], lambda at: back_ref[2 * SIDE + at : 2 * SIDE + at + 1, :],
     )
     for b in range(BLOCKS):
         rows = slice(8 * b, 8 * b + 8)
-        total = regrid(back_ref, SIDE, 2 - 2 * core, near_entries(near_ref), b)
+        total = regrid(back_ref, SIDE, 2 - 2 * core, entries_of(near_ref), b)
         for k in range(COMP):
             surface_ref[k, rows, :] = (other_base_ref[k, rows, :] + arrived(k, 0, b)) + (other_part_ref[k, rows, :] + total[k])
-    fluxes([out_ref[k, 0] for k in range(COMP)], sens_ref, sea_weight(sea_ref, dist_ref), flux_ref)
-    other_sens = near_ref[SENS : SENS + COMP, :]
-    fluxes([surface_ref[k] for k in range(COMP)], other_sens, near_ref[SEA:SLOT, :], other_flux_ref)
-    pick(flux_ref, send_ref[pl.ds(pl.multiple_of(16 - 16 * core, 8), 8), :], out_lon_ref, 0)
-    cell = near_ref[pl.ds(pl.multiple_of(CELL + 16 - 16 * core, 8), 8), :].astype(jnp.int32)
-    pick(other_flux_ref, cell, out_lon_ref, SIDE)
+    for message_ref, planes, to_ref, offset in (
+        (give_ref, [out_ref[k, 0] for k in range(COMP)], flux_ref, 0),
+        (near_ref, [surface_ref[k] for k in range(COMP)], other_flux_ref, SIDE),
+    ):
+        fluxes(planes, message_ref[SENS : SENS + COMP, :], message_ref[SEA:SLOT, :], to_ref)
+        pick(to_ref, cells_of(message_ref, 2 - 2 * core), out_lon_ref, offset)
     edges(core == 0, out_ref, dif_ref, vel_ref, out_lon_ref, LIST, out_lat_ref, 0)
     other_edges(core, surface_ref, near_ref, lat_ref, lon_ref, back_ref, out_lon_ref, out_lat_ref)
 
 
-def last_kernel(base_ref, part_ref, slot_ref, weight_ref, edge_ref, back_ref, out_hbm, out_ref, sems):
+def last_kernel(base_ref, part_ref, give_ref, edge_ref, back_ref, out_hbm, out_ref, sems):
     core = lax.axis_index("sec")
     deep = pltpu.make_async_copy(out_ref.at[:, pl.ds(1, LEV - 1)], out_hbm.at[:, pl.ds(1, LEV - 1)], sems.at[0])
     top = pltpu.make_async_copy(out_ref.at[:, 0], out_hbm.at[:, 0], sems.at[1])
@@ -384,7 +382,7 @@
         core, edge_ref[:8, :], back_ref[LIST:SIDE, :],
         lambda at: edge_ref[8 + at : 9 + at, :], lambda at: back_ref[SIDE + at : SIDE + at + 1, :],
     )
-    finish(core, base_ref, part_ref, own_entries(slot_ref, weight_ref), arrived, back_ref, out_ref, deep.start)
+    finish(core, base_ref, part_ref, entries_of(give_ref), arrived, back_ref, out_ref, deep.start)
     top.start()
     deep.wait()
     top.wait()
@@ -442,33 +440,32 @@
     give, flux = call(start_kernel, fresh, [(FIRST, LANES), surface], [*held, sems], pltpu.HBM)
 
     near = lax.ppermute(give, "sec", swap)
-    (keep,) = call(keep_kernel, (field, dif, vel, send[2], flux), [(KEEP, LANES)])
+    strip = (BACK - STRIP, LANES)
+    keep, base, strip = call(keep_kernel, (field, dif, vel, give, flux), [(KEEP, LANES), field.shape, strip])
     lon, lat = call(send_kernel, (keep, near), [lon_rows, lat_rows])
     lon = lax.ppermute(lon, ("sec", "lon"), routes("lon"))
     lat = lax.ppermute(lat, ("sec", "lat"), routes("lat"))
-    base, other_base, strip = call(
-        first_inner_kernel, (field, dif, vel, *take, near, give), [field.shape, surface, (BACK - STRIP, LANES)]
-    )
-    (back,) = call(first_turn_kernel, (lon, lat, strip), [(BACK, LANES)])
+    centre, other_base, other_centre = call(first_inner_kernel, (give, near), [surface] * 3)
+    (back,) = call(first_turn_kernel, (lon, lat, strip, centre), [(BACK, LANES)])
     back = lax.ppermute(back, "sec", swap)
-    part, other_part = call(first_kept_kernel, (*take, near, lon), [surface, surface])
+    part, other_part = call(first_kept_kernel, (give, near, lon, centre, other_centre), [surface] * 2)
 
     scratch = [pltpu.VMEM(surface, jnp.float32)] * 2
     field, lon, lat, flux = call(
         middle_kernel,
-        (sens, base, part, other_base, other_part, *take, near, lon, lat, back, dif, vel, *send),
+        (base, part, other_base, other_part, give, near, lon, lat, back, dif, vel),
         [field.shape, lon_rows, lat_rows, surface],
         scratch,
     )
     lon = lax.ppermute(lon, ("sec", "lon"), routes("lon"))
     lat = lax.ppermute(lat, ("sec", "lat"), routes("lat"))
     scratch = [pltpu.VMEM((LIST, LANES), jnp.float32)]
-    (base,) = call(second_inner_kernel, (field, dif, vel, *take, near, flux), [field.shape], scratch)
+    base, centre = call(second_inner_kernel, (field, dif, vel, give, near, flux), [field.shape, surface], scratch)
     back, edge = call(second_turn_kernel, (lon, lat, base), [(KEEP, LANES), (8 + PLANES, LANES)])
     back = lax.ppermute(back, "sec", swap)
-    (part,) = call(second_kept_kernel, (*take, lon), [surface])
+    (part,) = call(second_kept_kernel, (give, lon, centre), [surface])
     scratch = [pltpu.VMEM(field.shape, jnp.float32), pltpu.SemaphoreType.DMA((2,))]
-    (field,) = call(last_kernel, (base, part, *take, edge, back), [field.shape], scratch, out_space=pltpu.HBM)
+    (field,) = call(last_kernel, (base, part, give, edge, back), [field.shape], scratch, out_space=pltpu.HBM)
     return field[None]
 
 

time: 43.6 us -> 43 us (0.986)
  local copies, waits for them, and re-layouts: 0.7 us -> 0.01 us
    unnamed x18 -> x6, local copies, waits for them, and re-layouts: 0.7 us -> 0.01 us
where the time goes in v6:
time: 43 us; the launch traced here: 42.7 us
  starting transfers between devices  22.2 us (52%)
  Pallas kernels  10.2 us (24%)
  waiting for transfers between devices  10.2 us (24%)
    pallas_call x11, Pallas kernels, call(): pl.pallas_call(kernel, out_shape=[jax.ShapeDtypeStruct(shape, jnp.float32...  10.2 us
    ppermute x2, waiting for transfers between devices, on_device(): lat = lax.ppermute(lat, ('sec', 'lat'), routes('lat'))  9.38 us
    ppermute x1, starting transfers between devices, on_device(): near = lax.ppermute(give, 'sec', swap)  8.79 us
    ppermute x2, starting transfers between devices, on_device(): lon = lax.ppermute(lon, ('sec', 'lon'), routes('lon'))  6.59 us
    ppermute x2, starting transfers between devices, on_device(): back = lax.ppermute(back, 'sec', swap)  4.21 us
    ppermute x2, starting transfers between devices, on_device(): lat = lax.ppermute(lat, ('sec', 'lat'), routes('lat'))  2.58 us
  transfers between devices with their start and end apart: 7, of which 4 were waited for; matrix products, arithmetic and copies ran while one was open for 0% of the time, Pallas kernels for 11%

profile of v6, /device:TPU:1, one launch (start us, length us, event | category | flops | bytes accessed | tf_op | source)
XLA Modules:
  0.0 42.7 jit_solution(2393503798265195374)
XLA Ops:
  0.0 0.0 copy-start
  0.0 0.0 copy-start.1
  0.0 0.0 copy-start.2
  0.0 1.7 %shard_map.91 = (f32[632,128]{1,0:T(8,128)S(1)}, f32[4,32,128]{2,1,0:T(8,128)S(1)}) custom-call(f32[4,4]{1,0:T(4,128)} %bitcast.25, f32[4,4,32,128]{3,2,1,0:T(8,128)} %bitcast.18, f32[4,32,128]{2,1,0:T(8,128)} %bitcast.14, f32[2,4,32,128]{3,2,1,0:T(8,128)} %bitcast.10, s32[32,128]{1,0:T(8,128)} %bitcast.22, s32[32,128]{1,0:T(8,128)} %bitcast.23, ...), custom_call_target="tpu_custom_call" | custom-call | flops 1048576 | bytes 1048576 | tf_op jit(solution)/shard_map/pallas_call | solution.py:394
  1.7 8.8 %collective-permute-start = (f32[632,128]{1,0:T(8,128)S(1)}, f32[632,128]{1,0:T(8,128)S(1)}, u32[]{:S(2)}, u32[]{:S(2)}) collective-permute-start(f32[632,128]{1,0:T(8,128)S(1)} %get-tuple-element.25.give_ref), channel_id=1, source_target_pairs={{0,256},{256,0},{1,257},{257,1},{2,258},{258,2},{3,259},{259,3},{4... | collective-permute-start | bytes 970760 | tf_op jit(solution)/shard_map/ppermute | solution.py:442
  10.5 0.0 copy-done
  10.5 0.0 copy-done.1
  10.5 0.0 copy-done.2
  10.5 0.5 %shard_map.92 = (f32[56,128]{1,0:T(8,128)S(1)}, f32[4,4,32,128]{3,2,1,0:T(8,128)S(1)}, f32[48,128]{1,0:T(8,128)S(1)}) custom-call(f32[4,4,32,128]{3,2,1,0:T(8,128)S(1)} %bitcast.19, f32[4,32,128]{2,1,0:T(8,128)S(1)} %bitcast.15, f32[2,4,32,128]{3,2,1,0:T(8,128)S(1)} %bitcast.11, f32[632,128]{1,0:T(8,128)S(1)} %get-tuple-element.25.give_ref, ...), custom_call_target="tpu_custom_call" | custom-call | flops 1048576 | bytes 1048576 | tf_op jit(solution)/shard_map/pallas_call | solution.py:394
  11.0 0.7 %collective-permute-done.near_ref = f32[632,128]{1,0:T(8,128)S(1)} collective-permute-done((f32[632,128]{1,0:T(8,128)S(1)}, f32[632,128]{1,0:T(8,128)S(1)}, u32[]{:S(2)}, u32[]{:S(2)}) %collective-permute-start) | collective-permute-done | bytes 323616 | tf_op jit(solution)/shard_map/ppermute | solution.py:442
  11.7 3.7 %collective-permute-start.1 = (f32[80,128]{1,0:T(8,128)S(1)}, f32[80,128]{1,0:T(8,128)S(1)}, u32[]{:S(2)}, u32[]{:S(2)}) collective-permute-start(f32[80,128]{1,0:T(8,128)S(1)} %get-tuple-element.29), channel_id=1, source_target_pairs={{0,1},{256,319},{1,2},{257,256},{2,3},{258,257},{3,4},{259,258},{4... | collective-permute-start | bytes 122888 | tf_op jit(solution)/shard_map/ppermute | solution.py:446
  15.4 1.3 %collective-permute-start.2 = (f32[32,128]{1,0:T(8,128)S(1)}, f32[32,128]{1,0:T(8,128)S(1)}, u32[]{:S(2)}, u32[]{:S(2)}) collective-permute-start(f32[32,128]{1,0:T(8,128)S(1)} %get-tuple-element.35), channel_id=1, source_target_pairs={{0,64},{64,128},{320,256},{128,192},{384,320},{448,384},{1,65},{65... | collective-permute-start | bytes 49160 | tf_op jit(solution)/shard_map/ppermute | solution.py:447
  16.7 1.3 %shard_map.94 = (f32[4,32,128]{2,1,0:T(8,128)S(1)}, f32[4,32,128]{2,1,0:T(8,128)S(1)}, f32[4,32,128]{2,1,0:T(8,128)S(1)}) custom-call(f32[632,128]{1,0:T(8,128)S(1)} %get-tuple-element.25.give_ref, f32[632,128]{1,0:T(8,128)S(1)} %collective-permute-done.near_ref), custom_call_target="tpu_custom_call" | custom-call | flops 1048576 | bytes 1048576 | tf_op jit(solution)/shard_map/pallas_call | solution.py:394
  18.0 4.3 %collective-permute-done.2.lat_ref = f32[32,128]{1,0:T(8,128)S(1)} collective-permute-done((f32[32,128]{1,0:T(8,128)S(1)}, f32[32,128]{1,0:T(8,128)S(1)}, u32[]{:S(2)}, u32[]{:S(2)}) %collective-permute-start.2) | collective-permute-done | bytes 16416 | tf_op jit(solution)/shard_map/ppermute | solution.py:447
  22.4 0.0 collective-permute-done.1.lon_ref
  22.4 1.9 %collective-permute-start.3 = (f32[160,128]{1,0:T(8,128)S(1)}, f32[160,128]{1,0:T(8,128)S(1)}, u32[]{:S(2)}, u32[]{:S(2)}) collective-permute-start(f32[160,128]{1,0:T(8,128)S(1)} %shard_map.96), channel_id=1, source_target_pairs={{0,256},{256,0},{1,257},{257,1},{2,258},{258,2},{3,259},{259,3},{4... | collective-permute-start | bytes 245768 | tf_op jit(solution)/shard_map/ppermute | solution.py:450
  24.3 1.3 %shard_map.95 = (f32[4,32,128]{2,1,0:T(8,128)S(1)}, f32[4,32,128]{2,1,0:T(8,128)S(1)}) custom-call(f32[632,128]{1,0:T(8,128)S(1)} %get-tuple-element.25.give_ref, f32[632,128]{1,0:T(8,128)S(1)} %collective-permute-done.near_ref, f32[80,128]{1,0:T(8,128)S(1)} %collective-permute-done.1.lon_ref, f32[4,32,128]{2,1,0:T(8,128)S(1)} %get-tuple-element.30.centre_ref, ...), custom_call_target="tpu_custom_call" | custom-call | flops 1048576 | bytes 1048576 | tf_op jit(solution)/shard_map/pallas_call | solution.py:394
  25.6 0.0 collective-permute-done.3.back_ref
  25.6 2.2 %shard_map.97 = (f32[4,4,32,128]{3,2,1,0:T(8,128)S(1)}, f32[80,128]{1,0:T(8,128)S(1)}, f32[32,128]{1,0:T(8,128)S(1)}, f32[4,32,128]{2,1,0:T(8,128)S(1)}) custom-call(f32[4,4,32,128]{3,2,1,0:T(8,128)S(1)} %get-tuple-element.27.base_ref, f32[4,32,128]{2,1,0:T(8,128)S(1)} %get-tuple-element.32.part_ref, f32[4,32,128]{2,1,0:T(8,128)S(1)} %get-tuple-element.33.other_base_ref, ...), custom_call_target="tpu_custom_call" | custom-call | flops 1048576 | bytes 1048576 | tf_op jit(solution)/shard_map/pallas_call | solution.py:394
  27.8 2.9 %collective-permute-start.4 = (f32[80,128]{1,0:T(8,128)S(1)}, f32[80,128]{1,0:T(8,128)S(1)}, u32[]{:S(2)}, u32[]{:S(2)}) collective-permute-start(f32[80,128]{1,0:T(8,128)S(1)} %get-tuple-element.40), channel_id=1, source_target_pairs={{0,1},{256,319},{1,2},{257,256},{2,3},{258,257},{3,4},{259,258},{4... | collective-permute-start | bytes 122888 | tf_op jit(solution)/shard_map/ppermute | solution.py:460
  30.7 1.3 %collective-permute-start.5 = (f32[32,128]{1,0:T(8,128)S(1)}, f32[32,128]{1,0:T(8,128)S(1)}, u32[]{:S(2)}, u32[]{:S(2)}) collective-permute-start(f32[32,128]{1,0:T(8,128)S(1)} %get-tuple-element.42), channel_id=1, source_target_pairs={{0,64},{64,128},{320,256},{128,192},{384,320},{448,384},{1,65},{65... | collective-permute-start | bytes 49160 | tf_op jit(solution)/shard_map/ppermute | solution.py:461
  32.0 1.0 %shard_map.98 = (f32[4,4,32,128]{3,2,1,0:T(8,128)S(1)}, f32[4,32,128]{2,1,0:T(8,128)S(1)}) custom-call(f32[4,4,32,128]{3,2,1,0:T(8,128)S(1)} %get-tuple-element.37.field_ref, f32[4,32,128]{2,1,0:T(8,128)S(1)} %bitcast.17, f32[2,4,32,128]{3,2,1,0:T(8,128)S(1)} %bitcast.13, f32[632,128]{1,0:T(8,128)S(1)} %get-tuple-element.25.give_ref, ...), custom_call_target="tpu_custom_call" | custom-call | flops 1048576 | bytes 1048576 | tf_op jit(solution)/shard_map/pallas_call | solution.py:394
  33.0 5.0 %collective-permute-done.5.lat_ref = f32[32,128]{1,0:T(8,128)S(1)} collective-permute-done((f32[32,128]{1,0:T(8,128)S(1)}, f32[32,128]{1,0:T(8,128)S(1)}, u32[]{:S(2)}, u32[]{:S(2)}) %collective-permute-start.5) | collective-permute-done | bytes 16416 | tf_op jit(solution)/shard_map/ppermute | solution.py:461
  38.0 0.0 collective-permute-done.4.lon_ref
  38.0 2.3 %collective-permute-start.6 = (f32[56,128]{1,0:T(8,128)S(1)}, f32[56,128]{1,0:T(8,128)S(1)}, u32[]{:S(2)}, u32[]{:S(2)}) collective-permute-start(f32[56,128]{1,0:T(8,128)S(1)} %get-tuple-element.44), channel_id=1, source_target_pairs={{0,256},{256,0},{1,257},{257,1},{2,258},{258,2},{3,259},{259,3},{4... | collective-permute-start | bytes 86024 | tf_op jit(solution)/shard_map/ppermute | solution.py:465
  40.3 0.7 %shard_map.99.part_ref = f32[4,32,128]{2,1,0:T(8,128)S(1)} custom-call(f32[632,128]{1,0:T(8,128)S(1)} %get-tuple-element.25.give_ref, f32[80,128]{1,0:T(8,128)S(1)} %collective-permute-done.4.lon_ref, f32[4,32,128]{2,1,0:T(8,128)S(1)} %get-tuple-element.41.centre_ref), custom_call_target="tpu_custom_call" | custom-call | flops 1048576 | bytes 1048576 | tf_op jit(solution)/shard_map/pallas_call | solution.py:394
  41.0 0.2 collective-permute-done.6.back_ref
  41.2 1.5 %shard_map.101 = f32[4,4,32,128]{3,2,1,0:T(8,128)} custom-call(f32[4,4,32,128]{3,2,1,0:T(8,128)S(1)} %get-tuple-element.39.base_ref, f32[4,32,128]{2,1,0:T(8,128)S(1)} %shard_map.99.part_ref, f32[632,128]{1,0:T(8,128)S(1)} %get-tuple-element.25.give_ref, f32[24,128]{1,0:T(8,128)S(1)} %get-tuple-element.43.edge_ref, f32[56,128]{1,0:T(8,128)S(1)} %collective-permute-done.6.back_ref), custom_call_target="tpu_custom_call" | custom-call | flops 1048576 | bytes 1048576 | tf_op jit(solution)/shard_map/pallas_call | solution.py:394
  (3 shorter events, 0.0 us)
Async XLA Ops:
  0.0 10.5 %copy-start = (f32[1,2,4,32,128]{4,3,2,1,0:T(8,128)S(1)}, f32[1,2,4,32,128]{4,3,2,1,0:T(8,128)}, u32[]{:S(2)}) copy-start(f32[1,2,4,32,128]{4,3,2,1,0:T(8,128)} %param.11) | copy-start | bytes 393220
  0.0 10.5 %copy-start.1 = (f32[1,4,32,128]{3,2,1,0:T(8,128)S(1)}, f32[1,4,32,128]{3,2,1,0:T(8,128)}, u32[]{:S(2)}) copy-start(f32[1,4,32,128]{3,2,1,0:T(8,128)} %param.10) | copy-start | bytes 196612
  0.0 10.5 %copy-start.2 = (f32[1,4,4,32,128]{4,3,2,1,0:T(8,128)S(1)}, f32[1,4,4,32,128]{4,3,2,1,0:T(8,128)}, u32[]{:S(2)}) copy-start(f32[1,4,4,32,128]{4,3,2,1,0:T(8,128)} %param.9) | copy-start | bytes 786436
  1.7 10.0 %collective-permute-start = (f32[632,128]{1,0:T(8,128)S(1)}, f32[632,128]{1,0:T(8,128)S(1)}, u32[]{:S(2)}, u32[]{:S(2)}) collective-permute-start(f32[632,128]{1,0:T(8,128)S(1)} %get-tuple-element.25.give_ref), channel_id=1, source_target_pairs={{0,256},{256,0},{1,257},{257,1},{2,258},{258,2},{3,259},{259,3},{4... | collective-permute-start | bytes 970760 | tf_op jit(solution)/shard_map/ppermute | solution.py:442
  11.7 10.7 %collective-permute-start.1 = (f32[80,128]{1,0:T(8,128)S(1)}, f32[80,128]{1,0:T(8,128)S(1)}, u32[]{:S(2)}, u32[]{:S(2)}) collective-permute-start(f32[80,128]{1,0:T(8,128)S(1)} %get-tuple-element.29), channel_id=1, source_target_pairs={{0,1},{256,319},{1,2},{257,256},{2,3},{258,257},{3,4},{259,258},{4... | collective-permute-start | bytes 122888 | tf_op jit(solution)/shard_map/ppermute | solution.py:446
  15.4 6.9 %collective-permute-start.2 = (f32[32,128]{1,0:T(8,128)S(1)}, f32[32,128]{1,0:T(8,128)S(1)}, u32[]{:S(2)}, u32[]{:S(2)}) collective-permute-start(f32[32,128]{1,0:T(8,128)S(1)} %get-tuple-element.35), channel_id=1, source_target_pairs={{0,64},{64,128},{320,256},{128,192},{384,320},{448,384},{1,65},{65... | collective-permute-start | bytes 49160 | tf_op jit(solution)/shard_map/ppermute | solution.py:447
  22.4 3.2 %collective-permute-start.3 = (f32[160,128]{1,0:T(8,128)S(1)}, f32[160,128]{1,0:T(8,128)S(1)}, u32[]{:S(2)}, u32[]{:S(2)}) collective-permute-start(f32[160,128]{1,0:T(8,128)S(1)} %shard_map.96), channel_id=1, source_target_pairs={{0,256},{256,0},{1,257},{257,1},{2,258},{258,2},{3,259},{259,3},{4... | collective-permute-start | bytes 245768 | tf_op jit(solution)/shard_map/ppermute | solution.py:450
  27.8 10.2 %collective-permute-start.4 = (f32[80,128]{1,0:T(8,128)S(1)}, f32[80,128]{1,0:T(8,128)S(1)}, u32[]{:S(2)}, u32[]{:S(2)}) collective-permute-start(f32[80,128]{1,0:T(8,128)S(1)} %get-tuple-element.40), channel_id=1, source_target_pairs={{0,1},{256,319},{1,2},{257,256},{2,3},{258,257},{3,4},{259,258},{4... | collective-permute-start | bytes 122888 | tf_op jit(solution)/shard_map/ppermute | solution.py:460
  30.7 7.4 %collective-permute-start.5 = (f32[32,128]{1,0:T(8,128)S(1)}, f32[32,128]{1,0:T(8,128)S(1)}, u32[]{:S(2)}, u32[]{:S(2)}) collective-permute-start(f32[32,128]{1,0:T(8,128)S(1)} %get-tuple-element.42), channel_id=1, source_target_pairs={{0,64},{64,128},{320,256},{128,192},{384,320},{448,384},{1,65},{65... | collective-permute-start | bytes 49160 | tf_op jit(solution)/shard_map/ppermute | solution.py:461
  38.0 3.1 %collective-permute-start.6 = (f32[56,128]{1,0:T(8,128)S(1)}, f32[56,128]{1,0:T(8,128)S(1)}, u32[]{:S(2)}, u32[]{:S(2)}) collective-permute-start(f32[56,128]{1,0:T(8,128)S(1)} %get-tuple-element.44), channel_id=1, source_target_pairs={{0,256},{256,0},{1,257},{257,1},{2,258},{258,2},{3,259},{259,3},{4... | collective-permute-start | bytes 86024 | tf_op jit(solution)/shard_map/ppermute | solution.py:465

commit v7 on v6

--- a/solution.py
+++ b/solution.py
@@ -169,15 +169,8 @@
     return message_ref[pl.ds(pl.multiple_of(CELL + 8 * d, 8), 8), :].astype(jnp.int32)
 
 
-def keep_kernel(field_ref, dif_ref, vel_ref, give_ref, flux_ref, keep_ref, base_ref, strip_ref):
-    core = lax.axis_index("sec")
-    pick(flux_ref, cells_of(give_ref, 2 - 2 * core), keep_ref, 0)
-    edges(core == 0, field_ref, dif_ref, vel_ref, keep_ref, LIST, keep_ref, SIDE)
-    for level in range(LEV):
-        for k in range(COMP):
-            base_ref[k, level] = inside(field_ref[k, level], dif_ref[level], 0.5 * vel_ref[0, level], 0.5 * vel_ref[1, level])
-
-    half, last, column = direction(core != 0)
+def strip_of(upward, base_ref, dif_ref, vel_ref, strip_ref):
+    half, last, column = direction(upward)
     lane = lax.broadcasted_iota(jnp.int32, (8, LANES), 1)
     side = jnp.zeros((8, LANES), jnp.float32)
     factor = jnp.zeros((8, LANES), jnp.float32)
@@ -199,6 +192,18 @@
     strip_ref[8 + PLANES : 16 + PLANES, :] = factor
 
 
+def keep_kernel(field_ref, dif_ref, vel_ref, give_ref, flux_ref, keep_ref, base_ref, own_strip_ref, strip_ref):
+    core = lax.axis_index("sec")
+    pick(flux_ref, cells_of(give_ref, 2 - 2 * core), keep_ref, 0)
+    edges(core == 0, field_ref, dif_ref, vel_ref, keep_ref, LIST, keep_ref, SIDE)
+    for level in range(LEV):
+        for k in range(COMP):
+            base_ref[k, level] = inside(field_ref[k, level], dif_ref[level], 0.5 * vel_ref[0, level], 0.5 * vel_ref[1, level])
+
+    strip_of(core == 0, base_ref, dif_ref, vel_ref, own_strip_ref)
+    strip_of(core != 0, base_ref, dif_ref, vel_ref, strip_ref)
+
+
 def first_inner_kernel(give_ref, near_ref, centre_ref, other_base_ref, other_centre_ref):
     dif = near_ref[COEF : COEF + ROWS, :]
     half_u = 0.5 * near_ref[COEF + ROWS : COEF + 2 * ROWS, :]
@@ -213,10 +218,23 @@
             other_centre_ref[k, 8 * b : 8 * b + 8, :] = other[k]
 
 
-def second_inner_kernel(field_ref, dif_ref, vel_ref, give_ref, near_ref, flux_ref, base_ref, centre_ref, list_ref):
+def second_inner_kernel(
+    before_ref, surface_ref, dif_ref, vel_ref, give_ref, near_ref, flux_ref, lon_ref, lat_ref, back_ref, base_ref, centre_ref,
+    field_ref, list_ref,
+):
+    arrived = around(
+        lax.axis_index("sec"), lon_ref[LIST:SIDE, :], back_ref[SIDE + LIST : 2 * SIDE, :],
+        lambda at: lat_ref[at : at + 1, :], lambda at: back_ref[2 * SIDE + PLANES + at : 2 * SIDE + PLANES + at + 1, :],
+    )
+    for k in range(COMP):
+        for level in range(1, LEV):
+            for b in range(BLOCKS):
+                rows = slice(8 * b, 8 * b + 8)
+                field_ref[k, level, rows, :] = before_ref[k, level, rows, :] + arrived(k, level, b)
     for level in range(LEV):
         for k in range(COMP):
-            base_ref[k, level] = inside(field_ref[k, level], dif_ref[level], 0.5 * vel_ref[0, level], 0.5 * vel_ref[1, level])
+            plane = surface_ref[k] if level == 0 else field_ref[k, level]
+            base_ref[k, level] = inside(plane, dif_ref[level], 0.5 * vel_ref[0, level], 0.5 * vel_ref[1, level])
     pick(flux_ref, cells_of(near_ref, 1), list_ref, 0)
     for b in range(BLOCKS):
         total = regrid(list_ref, 0, 1, entries_of(give_ref), b)
@@ -299,21 +317,22 @@
             out_ref[k, 0, rows, :] = (base_ref[k, 0, rows, :] + arrived(k, 0, b)) + (part_ref[k, rows, :] + total[k])
 
 
-def other_edges(core, surface_ref, near_ref, lat_ref, lon_ref, back_ref, out_lon_ref, out_lat_ref):
+def surface_edges(
+    core, surface_ref, message_ref, kept_side, passed_side, kept_rows_of, passed_rows_of, strip_rows_of,
+    out_lon_ref, lon_at, out_lat_ref, lat_at,
+):
     first = core == 0
     half, last, column = direction(first)
     lane = lax.broadcasted_iota(jnp.int32, (8, LANES), 1)
     row = lax.broadcasted_iota(jnp.int32, (8, LANES), 0)
-    passed_side = back_ref[LIST:SIDE, :]
-    kept_side = lon_ref[SIDE + LIST :, :]
     from_west = jnp.where(first, kept_side, passed_side)
     from_east = jnp.where(first, passed_side, kept_side)
 
     corner_north = jnp.zeros((8, LANES), jnp.float32)
     corner_south = jnp.zeros((8, LANES), jnp.float32)
     for i in range(PLANES // 8):
-        passed = back_ref[2 * SIDE + 8 * i : 2 * SIDE + 8 * i + 8, :]
-        kept_rows = lat_ref[PLANES + 8 * i : PLANES + 8 * i + 8, :]
+        passed = passed_rows_of(8 * i, 8)
+        kept_rows = kept_rows_of(8 * i, 8)
         south = pull(jnp.where(first, kept_rows, passed), column)
         north = pull(jnp.where(first, passed, kept_rows), column)
         corner_south = corner_south + jnp.where(lane == row + 8 * i, south, 0.0)
@@ -324,54 +343,60 @@
         west = pull(jnp.broadcast_to(end_west, (8, LANES)), index)
         east = pull(jnp.broadcast_to(end_east, (8, LANES)), index)
         ends = jnp.where(lane == LANES - 1, east, jnp.where(lane == 0, west, 0.0))
-        at = STRIP + 8 + 8 * i
-        line = back_ref[at : at + 8, :] + passed + ends
-        factor = back_ref[at + 8 + PLANES : at + 16 + PLANES, :]
-        out_lat_ref[PLANES + 8 * i : PLANES + 8 * i + 8, :] = factor * line
+        line = strip_rows_of(8 + 8 * i, 8) + passed + ends
+        factor = strip_rows_of(16 + PLANES + 8 * i, 8)
+        out_lat_ref[lat_at + 8 * i : lat_at + 8 * i + 8, :] = factor * line
     corner_south = jnp.broadcast_to(jnp.sum(corner_south, axis=0, keepdims=True), (8, LANES))
     corner_north = jnp.broadcast_to(jnp.sum(corner_north, axis=0, keepdims=True), (8, LANES))
     corner = jnp.where(row == 0, corner_south, jnp.where(row == 7, corner_north, 0.0))
-    factor = back_ref[STRIP + 8 + PLANES : STRIP + 16 + PLANES, :]
-    side = factor * (back_ref[STRIP : STRIP + 8, :] + passed_side + corner)
-
-    across = near_ref[COEF : COEF + ROWS, :] + half * near_ref[COEF + ROWS : COEF + 2 * ROWS, :]
-    along = near_ref[pl.ds(COEF + last, 1), :] + half * near_ref[pl.ds(COEF + 2 * ROWS + last, 1), :]
+    side = strip_rows_of(8 + PLANES, 8) * (strip_rows_of(0, 8) + passed_side + corner)
+
+    across = message_ref[COEF : COEF + ROWS, :] + half * message_ref[COEF + ROWS : COEF + 2 * ROWS, :]
+    along = message_ref[pl.ds(COEF + last, 1), :] + half * message_ref[pl.ds(COEF + 2 * ROWS + last, 1), :]
     for k in range(COMP):
         at = LEV * k
         product = across * surface_ref[k]
         for b in range(BLOCKS):
             side = jnp.where(lane == PLANES * b + at, pull(product[8 * b : 8 * b + 8], column), side)
-        out_lat_ref[PLANES + at : PLANES + at + 1, :] = along * surface_ref[k, pl.ds(last, 1), :]
-    out_lon_ref[SIDE + LIST :, :] = side
+        out_lat_ref[lat_at + at : lat_at + at + 1, :] = along * surface_ref[k, pl.ds(last, 1), :]
+    out_lon_ref[lon_at : lon_at + 8, :] = side
+
+
+def rows_from(ref, offset):
+    return lambda at, count=1: ref[offset + at : offset + at + count, :]
 
 
 def middle_kernel(
-    base_ref, part_ref, other_base_ref, other_part_ref, give_ref, near_ref, lon_ref, lat_ref, back_ref, dif_ref, vel_ref,
-    out_ref, out_lon_ref, out_lat_ref, other_flux_ref, flux_ref, surface_ref,
+    base_ref, part_ref, other_base_ref, other_part_ref, own_strip_ref, give_ref, near_ref, lon_ref, lat_ref, back_ref,
+    surface_ref, out_lon_ref, out_lat_ref, other_flux_ref, flux_ref, other_surface_ref,
 ):
     core = lax.axis_index("sec")
-    arrived = around(
-        core, lon_ref[LIST:SIDE, :], back_ref[SIDE + LIST : 2 * SIDE, :],
-        lambda at: lat_ref[at : at + 1, :], lambda at: back_ref[2 * SIDE + PLANES + at : 2 * SIDE + PLANES + at + 1, :],
-    )
-    finish(core, base_ref, part_ref, entries_of(give_ref), arrived, back_ref, out_ref, lambda: None)
-    arrived = around(
-        core, lon_ref[SIDE + LIST :, :], back_ref[LIST:SIDE, :],
-        lambda at: lat_ref[PLANES + at : PLANES + at + 1, :], lambda at: back_ref[2 * SIDE + at : 2 * SIDE + at + 1, :],
-    )
-    for b in range(BLOCKS):
-        rows = slice(8 * b, 8 * b + 8)
-        total = regrid(back_ref, SIDE, 2 - 2 * core, entries_of(near_ref), b)
-        for k in range(COMP):
-            surface_ref[k, rows, :] = (other_base_ref[k, rows, :] + arrived(k, 0, b)) + (other_part_ref[k, rows, :] + total[k])
-    for message_ref, planes, to_ref, offset in (
-        (give_ref, [out_ref[k, 0] for k in range(COMP)], flux_ref, 0),
-        (near_ref, [surface_ref[k] for k in range(COMP)], other_flux_ref, SIDE),
-    ):
-        fluxes(planes, message_ref[SENS : SENS + COMP, :], message_ref[SEA:SLOT, :], to_ref)
-        pick(to_ref, cells_of(message_ref, 2 - 2 * core), out_lon_ref, offset)
-    edges(core == 0, out_ref, dif_ref, vel_ref, out_lon_ref, LIST, out_lat_ref, 0)
-    other_edges(core, surface_ref, near_ref, lat_ref, lon_ref, back_ref, out_lon_ref, out_lat_ref)
+    sections = (
+        (
+            lambda k, b: base_ref[k, 0, 8 * b : 8 * b + 8, :], part_ref, give_ref, 0, lon_ref[LIST:SIDE, :],
+            back_ref[SIDE + LIST : 2 * SIDE, :], rows_from(lat_ref, 0), rows_from(back_ref, 2 * SIDE + PLANES),
+            rows_from(own_strip_ref, 0), surface_ref, flux_ref,
+        ),
+        (
+            lambda k, b: other_base_ref[k, 8 * b : 8 * b + 8, :], other_part_ref, near_ref, 1, lon_ref[SIDE + LIST :, :],
+            back_ref[LIST:SIDE, :], rows_from(lat_ref, PLANES), rows_from(back_ref, 2 * SIDE),
+            rows_from(back_ref, STRIP), other_surface_ref, other_flux_ref,
+        ),
+    )
+    for base, part, message_ref, at, kept_side, passed_side, kept_rows, passed_rows, strip, to_ref, to_flux_ref in sections:
+        arrived = around(core, kept_side, passed_side, kept_rows, passed_rows)
+        for b in range(BLOCKS):
+            rows = slice(8 * b, 8 * b + 8)
+            total = regrid(back_ref, SIDE * at, 2 - 2 * core, entries_of(message_ref), b)
+            for k in range(COMP):
+                to_ref[k, rows, :] = (base(k, b) + arrived(k, 0, b)) + (part[k, rows, :] + total[k])
+        planes = [to_ref[k] for k in range(COMP)]
+        fluxes(planes, message_ref[SENS : SENS + COMP, :], message_ref[SEA:SLOT, :], to_flux_ref)
+        pick(to_flux_ref, cells_of(message_ref, 2 - 2 * core), out_lon_ref, SIDE * at)
+        surface_edges(
+            core, to_ref, message_ref, kept_side, passed_side, kept_rows, passed_rows, strip,
+            out_lon_ref, SIDE * at + LIST, out_lat_ref, PLANES * at,
+        )
 
 
 def last_kernel(base_ref, part_ref, give_ref, edge_ref, back_ref, out_hbm, out_ref, sems):
@@ -441,7 +466,9 @@
 
     near = lax.ppermute(give, "sec", swap)
     strip = (BACK - STRIP, LANES)
-    keep, base, strip = call(keep_kernel, (field, dif, vel, give, flux), [(KEEP, LANES), field.shape, strip])
+    keep, base, own_strip, strip = call(
+        keep_kernel, (field, dif, vel, give, flux), [(KEEP, LANES), field.shape, strip, strip]
+    )
     lon, lat = call(send_kernel, (keep, near), [lon_rows, lat_rows])
     lon = lax.ppermute(lon, ("sec", "lon"), routes("lon"))
     lat = lax.ppermute(lat, ("sec", "lat"), routes("lat"))
@@ -451,16 +478,19 @@
     part, other_part = call(first_kept_kernel, (give, near, lon, centre, other_centre), [surface] * 2)
 
     scratch = [pltpu.VMEM(surface, jnp.float32)] * 2
-    field, lon, lat, flux = call(
+    arrived = (lon, lat, back)
+    top, lon, lat, flux = call(
         middle_kernel,
-        (base, part, other_base, other_part, give, near, lon, lat, back, dif, vel),
-        [field.shape, lon_rows, lat_rows, surface],
+        (base, part, other_base, other_part, own_strip, give, near, *arrived),
+        [surface, lon_rows, lat_rows, surface],
         scratch,
     )
     lon = lax.ppermute(lon, ("sec", "lon"), routes("lon"))
     lat = lax.ppermute(lat, ("sec", "lat"), routes("lat"))
-    scratch = [pltpu.VMEM((LIST, LANES), jnp.float32)]
-    base, centre = call(second_inner_kernel, (field, dif, vel, give, near, flux), [field.shape, surface], scratch)
+    scratch = [pltpu.VMEM(field.shape, jnp.float32), pltpu.VMEM((LIST, LANES), jnp.float32)]
+    base, centre = call(
+        second_inner_kernel, (base, top, dif, vel, give, near, flux, *arrived), [field.shape, surface], scratch
+    )
     back, edge = call(second_turn_kernel, (lon, lat, base), [(KEEP, LANES), (8 + PLANES, LANES)])
     back = lax.ppermute(back, "sec", swap)
     (part,) = call(second_kept_kernel, (give, lon, centre), [surface])

time: 43 us -> 42.8 us (level)
  transfers between devices with their start and end apart: 7 -> 7, of which waited for: 4 -> 4; matrix products, arithmetic and copies ran while one was open for 0% -> 0% of each run, Pallas kernels for 11% -> 12%
where the time goes in v7:
time: 42.8 us; the launch traced here: 42.5 us
  starting transfers between devices  22.2 us (52%)
  Pallas kernels  10.2 us (24%)
  waiting for transfers between devices  9.98 us (23%)
    pallas_call x11, Pallas kernels, call(): pl.pallas_call(kernel, out_shape=[jax.ShapeDtypeStruct(shape, jnp.float32...  10.2 us
    ppermute x2, waiting for transfers between devices, on_device(): lat = lax.ppermute(lat, ('sec', 'lat'), routes('lat'))  9.2 us
    ppermute x1, starting transfers between devices, on_device(): near = lax.ppermute(give, 'sec', swap)  8.79 us
    ppermute x2, starting transfers between devices, on_device(): lon = lax.ppermute(lon, ('sec', 'lon'), routes('lon'))  6.59 us
    ppermute x2, starting transfers between devices, on_device(): back = lax.ppermute(back, 'sec', swap)  4.21 us
    ppermute x2, starting transfers between devices, on_device(): lat = lax.ppermute(lat, ('sec', 'lat'), routes('lat'))  2.58 us
  transfers between devices with their start and end apart: 7, of which 4 were waited for; matrix products, arithmetic and copies ran while one was open for 0% of the time, Pallas kernels for 12%

profile of v7, /device:TPU:1, one launch (start us, length us, event | category | flops | bytes accessed | tf_op | source)
XLA Modules:
  0.0 42.5 jit_solution(5221601130407699558)
XLA Ops:
  0.0 0.0 copy-start
  0.0 0.0 copy-start.1
  0.0 0.0 copy-start.2
  0.0 1.7 %shard_map.91 = (f32[632,128]{1,0:T(8,128)S(1)}, f32[4,32,128]{2,1,0:T(8,128)S(1)}) custom-call(f32[4,4]{1,0:T(4,128)} %bitcast.23, f32[4,4,32,128]{3,2,1,0:T(8,128)} %bitcast.13, f32[4,32,128]{2,1,0:T(8,128)} %bitcast.15, f32[2,4,32,128]{3,2,1,0:T(8,128)} %bitcast.10, s32[32,128]{1,0:T(8,128)} %bitcast.20, s32[32,128]{1,0:T(8,128)} %bitcast.21, ...), custom_call_target="tpu_custom_call" | custom-call | flops 1048576 | bytes 1048576 | tf_op jit(solution)/shard_map/pallas_call | solution.py:419
  1.7 8.8 %collective-permute-start = (f32[632,128]{1,0:T(8,128)S(1)}, f32[632,128]{1,0:T(8,128)S(1)}, u32[]{:S(2)}, u32[]{:S(2)}) collective-permute-start(f32[632,128]{1,0:T(8,128)S(1)} %get-tuple-element.26.give_ref), channel_id=1, source_target_pairs={{0,256},{256,0},{1,257},{257,1},{2,258},{258,2},{3,259},{259,3},{4... | collective-permute-start | bytes 970760 | tf_op jit(solution)/shard_map/ppermute | solution.py:467
  10.5 0.0 copy-done
  10.5 0.0 copy-done.1
  10.5 0.0 copy-done.2
  10.5 0.6 %shard_map.92 = (f32[56,128]{1,0:T(8,128)S(1)}, f32[4,4,32,128]{3,2,1,0:T(8,128)S(1)}, f32[48,128]{1,0:T(8,128)S(1)}, f32[48,128]{1,0:T(8,128)S(1)}) custom-call(f32[4,4,32,128]{3,2,1,0:T(8,128)S(1)} %bitcast.14, f32[4,32,128]{2,1,0:T(8,128)S(1)} %bitcast.16, f32[2,4,32,128]{3,2,1,0:T(8,128)S(1)} %bitcast.11, f32[632,128]{1,0:T(8,128)S(1)} %get-tuple-element.26.give_ref, ...), custom_call_target="tpu_custom_call" | custom-call | flops 1048576 | bytes 1048576 | tf_op jit(solution)/shard_map/pallas_call | solution.py:419
  11.1 0.6 %collective-permute-done.near_ref = f32[632,128]{1,0:T(8,128)S(1)} collective-permute-done((f32[632,128]{1,0:T(8,128)S(1)}, f32[632,128]{1,0:T(8,128)S(1)}, u32[]{:S(2)}, u32[]{:S(2)}) %collective-permute-start) | collective-permute-done | bytes 323616 | tf_op jit(solution)/shard_map/ppermute | solution.py:467
  11.7 3.7 %collective-permute-start.1 = (f32[80,128]{1,0:T(8,128)S(1)}, f32[80,128]{1,0:T(8,128)S(1)}, u32[]{:S(2)}, u32[]{:S(2)}) collective-permute-start(f32[80,128]{1,0:T(8,128)S(1)} %get-tuple-element.30), channel_id=1, source_target_pairs={{0,1},{256,319},{1,2},{257,256},{2,3},{258,257},{3,4},{259,258},{4... | collective-permute-start | bytes 122888 | tf_op jit(solution)/shard_map/ppermute | solution.py:473
  15.4 1.3 %collective-permute-start.2 = (f32[32,128]{1,0:T(8,128)S(1)}, f32[32,128]{1,0:T(8,128)S(1)}, u32[]{:S(2)}, u32[]{:S(2)}) collective-permute-start(f32[32,128]{1,0:T(8,128)S(1)} %get-tuple-element.37), channel_id=1, source_target_pairs={{0,64},{64,128},{320,256},{128,192},{384,320},{448,384},{1,65},{65... | collective-permute-start | bytes 49160 | tf_op jit(solution)/shard_map/ppermute | solution.py:474
  16.7 1.3 %shard_map.94 = (f32[4,32,128]{2,1,0:T(8,128)S(1)}, f32[4,32,128]{2,1,0:T(8,128)S(1)}, f32[4,32,128]{2,1,0:T(8,128)S(1)}) custom-call(f32[632,128]{1,0:T(8,128)S(1)} %get-tuple-element.26.give_ref, f32[632,128]{1,0:T(8,128)S(1)} %collective-permute-done.near_ref), custom_call_target="tpu_custom_call" | custom-call | flops 1048576 | bytes 1048576 | tf_op jit(solution)/shard_map/pallas_call | solution.py:419
  18.0 4.3 %collective-permute-done.2.lat_ref = f32[32,128]{1,0:T(8,128)S(1)} collective-permute-done((f32[32,128]{1,0:T(8,128)S(1)}, f32[32,128]{1,0:T(8,128)S(1)}, u32[]{:S(2)}, u32[]{:S(2)}) %collective-permute-start.2) | collective-permute-done | bytes 16416 | tf_op jit(solution)/shard_map/ppermute | solution.py:474
  22.4 0.0 collective-permute-done.1.lon_ref
  22.4 1.9 %collective-permute-start.3 = (f32[160,128]{1,0:T(8,128)S(1)}, f32[160,128]{1,0:T(8,128)S(1)}, u32[]{:S(2)}, u32[]{:S(2)}) collective-permute-start(f32[160,128]{1,0:T(8,128)S(1)} %shard_map.96), channel_id=1, source_target_pairs={{0,256},{256,0},{1,257},{257,1},{2,258},{258,2},{3,259},{259,3},{4... | collective-permute-start | bytes 245768 | tf_op jit(solution)/shard_map/ppermute | solution.py:477
  24.3 1.3 %shard_map.95 = (f32[4,32,128]{2,1,0:T(8,128)S(1)}, f32[4,32,128]{2,1,0:T(8,128)S(1)}) custom-call(f32[632,128]{1,0:T(8,128)S(1)} %get-tuple-element.26.give_ref, f32[632,128]{1,0:T(8,128)S(1)} %collective-permute-done.near_ref, f32[80,128]{1,0:T(8,128)S(1)} %collective-permute-done.1.lon_ref, f32[4,32,128]{2,1,0:T(8,128)S(1)} %get-tuple-element.31.centre_ref, ...), custom_call_target="tpu_custom_call" | custom-call | flops 1048576 | bytes 1048576 | tf_op jit(solution)/shard_map/pallas_call | solution.py:419
  25.6 0.0 collective-permute-done.3.back_ref
  25.6 2.0 %shard_map.97 = (f32[4,32,128]{2,1,0:T(8,128)S(1)}, f32[80,128]{1,0:T(8,128)S(1)}, f32[32,128]{1,0:T(8,128)S(1)}, f32[4,32,128]{2,1,0:T(8,128)S(1)}) custom-call(f32[4,4,32,128]{3,2,1,0:T(8,128)S(1)} %get-tuple-element.28.base_ref.before_ref, f32[4,32,128]{2,1,0:T(8,128)S(1)} %get-tuple-element.33.part_ref, ...), custom_call_target="tpu_custom_call" | custom-call | flops 1048576 | bytes 1048576 | tf_op jit(solution)/shard_map/pallas_call | solution.py:419
  27.6 2.9 %collective-permute-start.4 = (f32[80,128]{1,0:T(8,128)S(1)}, f32[80,128]{1,0:T(8,128)S(1)}, u32[]{:S(2)}, u32[]{:S(2)}) collective-permute-start(f32[80,128]{1,0:T(8,128)S(1)} %get-tuple-element.42), channel_id=1, source_target_pairs={{0,1},{256,319},{1,2},{257,256},{2,3},{258,257},{3,4},{259,258},{4... | collective-permute-start | bytes 122888 | tf_op jit(solution)/shard_map/ppermute | solution.py:488
  30.5 1.3 %collective-permute-start.5 = (f32[32,128]{1,0:T(8,128)S(1)}, f32[32,128]{1,0:T(8,128)S(1)}, u32[]{:S(2)}, u32[]{:S(2)}) collective-permute-start(f32[32,128]{1,0:T(8,128)S(1)} %get-tuple-element.44), channel_id=1, source_target_pairs={{0,64},{64,128},{320,256},{128,192},{384,320},{448,384},{1,65},{65... | collective-permute-start | bytes 49160 | tf_op jit(solution)/shard_map/ppermute | solution.py:489
  31.8 1.2 %shard_map.98 = (f32[4,4,32,128]{3,2,1,0:T(8,128)S(1)}, f32[4,32,128]{2,1,0:T(8,128)S(1)}) custom-call(f32[4,4,32,128]{3,2,1,0:T(8,128)S(1)} %get-tuple-element.28.base_ref.before_ref, f32[4,32,128]{2,1,0:T(8,128)S(1)} %get-tuple-element.39.surface_ref, f32[4,32,128]{2,1,0:T(8,128)S(1)} %bitcast.17, f32[2,4,32,128]{3,2,1,0:T(8,128)S(1)} %bitcast.12, ...), custom_call_target="tpu_custom_call" | custom-call | flops 1048576 | bytes 1048576 | tf_op jit(solution)/shard_map/pallas_call | solution.py:419
  32.9 4.9 %collective-permute-done.5.lat_ref = f32[32,128]{1,0:T(8,128)S(1)} collective-permute-done((f32[32,128]{1,0:T(8,128)S(1)}, f32[32,128]{1,0:T(8,128)S(1)}, u32[]{:S(2)}, u32[]{:S(2)}) %collective-permute-start.5) | collective-permute-done | bytes 16416 | tf_op jit(solution)/shard_map/ppermute | solution.py:489
  37.8 0.0 collective-permute-done.4.lon_ref
  37.8 2.3 %collective-permute-start.6 = (f32[56,128]{1,0:T(8,128)S(1)}, f32[56,128]{1,0:T(8,128)S(1)}, u32[]{:S(2)}, u32[]{:S(2)}) collective-permute-start(f32[56,128]{1,0:T(8,128)S(1)} %get-tuple-element.46), channel_id=1, source_target_pairs={{0,256},{256,0},{1,257},{257,1},{2,258},{258,2},{3,259},{259,3},{4... | collective-permute-start | bytes 86024 | tf_op jit(solution)/shard_map/ppermute | solution.py:495
  40.1 0.7 %shard_map.99.part_ref = f32[4,32,128]{2,1,0:T(8,128)S(1)} custom-call(f32[632,128]{1,0:T(8,128)S(1)} %get-tuple-element.26.give_ref, f32[80,128]{1,0:T(8,128)S(1)} %collective-permute-done.4.lon_ref, f32[4,32,128]{2,1,0:T(8,128)S(1)} %get-tuple-element.43.centre_ref), custom_call_target="tpu_custom_call" | custom-call | flops 1048576 | bytes 1048576 | tf_op jit(solution)/shard_map/pallas_call | solution.py:419
  40.8 0.2 collective-permute-done.6.back_ref
  40.9 1.5 %shard_map.101 = f32[4,4,32,128]{3,2,1,0:T(8,128)} custom-call(f32[4,4,32,128]{3,2,1,0:T(8,128)S(1)} %get-tuple-element.41.base_ref, f32[4,32,128]{2,1,0:T(8,128)S(1)} %shard_map.99.part_ref, f32[632,128]{1,0:T(8,128)S(1)} %get-tuple-element.26.give_ref, f32[24,128]{1,0:T(8,128)S(1)} %get-tuple-element.45.edge_ref, f32[56,128]{1,0:T(8,128)S(1)} %collective-permute-done.6.back_ref), custom_call_target="tpu_custom_call" | custom-call | flops 1048576 | bytes 1048576 | tf_op jit(solution)/shard_map/pallas_call | solution.py:419
  (3 shorter events, 0.0 us)
Async XLA Ops:
  0.0 10.5 %copy-start = (f32[1,2,4,32,128]{4,3,2,1,0:T(8,128)S(1)}, f32[1,2,4,32,128]{4,3,2,1,0:T(8,128)}, u32[]{:S(2)}) copy-start(f32[1,2,4,32,128]{4,3,2,1,0:T(8,128)} %param.11) | copy-start | bytes 393220
  0.0 10.5 %copy-start.1 = (f32[1,4,4,32,128]{4,3,2,1,0:T(8,128)S(1)}, f32[1,4,4,32,128]{4,3,2,1,0:T(8,128)}, u32[]{:S(2)}) copy-start(f32[1,4,4,32,128]{4,3,2,1,0:T(8,128)} %param.9) | copy-start | bytes 786436
  0.0 10.5 %copy-start.2 = (f32[1,4,32,128]{3,2,1,0:T(8,128)S(1)}, f32[1,4,32,128]{3,2,1,0:T(8,128)}, u32[]{:S(2)}) copy-start(f32[1,4,32,128]{3,2,1,0:T(8,128)} %param.10) | copy-start | bytes 196612
  1.7 10.0 %collective-permute-start = (f32[632,128]{1,0:T(8,128)S(1)}, f32[632,128]{1,0:T(8,128)S(1)}, u32[]{:S(2)}, u32[]{:S(2)}) collective-permute-start(f32[632,128]{1,0:T(8,128)S(1)} %get-tuple-element.26.give_ref), channel_id=1, source_target_pairs={{0,256},{256,0},{1,257},{257,1},{2,258},{258,2},{3,259},{259,3},{4... | collective-permute-start | bytes 970760 | tf_op jit(solution)/shard_map/ppermute | solution.py:467
  11.7 10.7 %collective-permute-start.1 = (f32[80,128]{1,0:T(8,128)S(1)}, f32[80,128]{1,0:T(8,128)S(1)}, u32[]{:S(2)}, u32[]{:S(2)}) collective-permute-start(f32[80,128]{1,0:T(8,128)S(1)} %get-tuple-element.30), channel_id=1, source_target_pairs={{0,1},{256,319},{1,2},{257,256},{2,3},{258,257},{3,4},{259,258},{4... | collective-permute-start | bytes 122888 | tf_op jit(solution)/shard_map/ppermute | solution.py:473
  15.4 6.9 %collective-permute-start.2 = (f32[32,128]{1,0:T(8,128)S(1)}, f32[32,128]{1,0:T(8,128)S(1)}, u32[]{:S(2)}, u32[]{:S(2)}) collective-permute-start(f32[32,128]{1,0:T(8,128)S(1)} %get-tuple-element.37), channel_id=1, source_target_pairs={{0,64},{64,128},{320,256},{128,192},{384,320},{448,384},{1,65},{65... | collective-permute-start | bytes 49160 | tf_op jit(solution)/shard_map/ppermute | solution.py:474
  22.4 3.2 %collective-permute-start.3 = (f32[160,128]{1,0:T(8,128)S(1)}, f32[160,128]{1,0:T(8,128)S(1)}, u32[]{:S(2)}, u32[]{:S(2)}) collective-permute-start(f32[160,128]{1,0:T(8,128)S(1)} %shard_map.96), channel_id=1, source_target_pairs={{0,256},{256,0},{1,257},{257,1},{2,258},{258,2},{3,259},{259,3},{4... | collective-permute-start | bytes 245768 | tf_op jit(solution)/shard_map/ppermute | solution.py:477
  27.6 10.2 %collective-permute-start.4 = (f32[80,128]{1,0:T(8,128)S(1)}, f32[80,128]{1,0:T(8,128)S(1)}, u32[]{:S(2)}, u32[]{:S(2)}) collective-permute-start(f32[80,128]{1,0:T(8,128)S(1)} %get-tuple-element.42), channel_id=1, source_target_pairs={{0,1},{256,319},{1,2},{257,256},{2,3},{258,257},{3,4},{259,258},{4... | collective-permute-start | bytes 122888 | tf_op jit(solution)/shard_map/ppermute | solution.py:488
  30.5 7.3 %collective-permute-start.5 = (f32[32,128]{1,0:T(8,128)S(1)}, f32[32,128]{1,0:T(8,128)S(1)}, u32[]{:S(2)}, u32[]{:S(2)}) collective-permute-start(f32[32,128]{1,0:T(8,128)S(1)} %get-tuple-element.44), channel_id=1, source_target_pairs={{0,64},{64,128},{320,256},{128,192},{384,320},{448,384},{1,65},{65... | collective-permute-start | bytes 49160 | tf_op jit(solution)/shard_map/ppermute | solution.py:489
  37.8 3.1 %collective-permute-start.6 = (f32[56,128]{1,0:T(8,128)S(1)}, f32[56,128]{1,0:T(8,128)S(1)}, u32[]{:S(2)}, u32[]{:S(2)}) collective-permute-start(f32[56,128]{1,0:T(8,128)S(1)} %get-tuple-element.46), channel_id=1, source_target_pairs={{0,256},{256,0},{1,257},{257,1},{2,258},{258,2},{3,259},{259,3},{4... | collective-permute-start | bytes 86024 | tf_op jit(solution)/shard_map/ppermute | solution.py:495

commit v8 on v7

--- a/solution.py
+++ b/solution.py
@@ -28,6 +28,7 @@
 FIRST = SENS + 8
 STRIP = 2 * SIDE + 2 * PLANES
 BACK = STRIP + 2 * (8 + PLANES)
+SUMS = COMP * ROWS
 
 
 def lookup(rows, high, low, first_row):
@@ -255,10 +256,19 @@
     back_ref[STRIP:, :] = strip_ref[...]
 
 
-def second_turn_kernel(lon_ref, lat_ref, base_ref, back_ref, edge_ref):
-    back_ref[:LIST, :] = lon_ref[:LIST, :]
-    back_ref[LIST:SIDE, :] = lon_ref[SIDE + LIST :, :]
-    back_ref[SIDE:, :] = lat_ref[PLANES : 2 * PLANES, :]
+def passed_kernel(near_ref, lon_ref, sum_ref):
+    source = 2 * lax.axis_index("sec")
+    for b in range(BLOCKS):
+        total = regrid(lon_ref, 0, source, entries_of(near_ref), b)
+        for k in range(COMP):
+            at = ROWS * k + 8 * b
+            sum_ref[at : at + 8, :] = total[k]
+    sum_ref[SUMS:, :] = lon_ref[SIDE + LIST :, :]
+
+
+def second_turn_kernel(sum_ref, lon_ref, lat_ref, base_ref, back_ref, edge_ref):
+    back_ref[: SUMS + 8, :] = sum_ref[...]
+    back_ref[SUMS + 8 :, :] = lat_ref[PLANES : 2 * PLANES, :]
     edge_ref[:8, :] = lon_ref[LIST:SIDE, :]
     edge_ref[8:, :] = lat_ref[:PLANES, :]
 
@@ -301,20 +311,6 @@
         return edge
 
     return arrived
-
-
-def finish(core, base_ref, part_ref, entries, arrived, list_ref, out_ref, ready):
-    for k in range(COMP):
-        for level in range(1, LEV):
-            for b in range(BLOCKS):
-                rows = slice(8 * b, 8 * b + 8)
-                out_ref[k, level, rows, :] = base_ref[k, level, rows, :] + arrived(k, level, b)
-    ready()
-    for b in range(BLOCKS):
-        rows = slice(8 * b, 8 * b + 8)
-        total = regrid(list_ref, 0, 2 - 2 * core, entries, b)
-        for k in range(COMP):
-            out_ref[k, 0, rows, :] = (base_ref[k, 0, rows, :] + arrived(k, 0, b)) + (part_ref[k, rows, :] + total[k])
 
 
 def surface_edges(
@@ -399,18 +395,25 @@
         )
 
 
-def last_kernel(base_ref, part_ref, give_ref, edge_ref, back_ref, out_hbm, out_ref, sems):
+def last_kernel(base_ref, part_ref, edge_ref, back_ref, out_hbm, out_ref, sems):
     core = lax.axis_index("sec")
-    deep = pltpu.make_async_copy(out_ref.at[:, pl.ds(1, LEV - 1)], out_hbm.at[:, pl.ds(1, LEV - 1)], sems.at[0])
-    top = pltpu.make_async_copy(out_ref.at[:, 0], out_hbm.at[:, 0], sems.at[1])
     arrived = around(
-        core, edge_ref[:8, :], back_ref[LIST:SIDE, :],
-        lambda at: edge_ref[8 + at : 9 + at, :], lambda at: back_ref[SIDE + at : SIDE + at + 1, :],
-    )
-    finish(core, base_ref, part_ref, entries_of(give_ref), arrived, back_ref, out_ref, deep.start)
-    top.start()
-    deep.wait()
-    top.wait()
+        core, edge_ref[:8, :], back_ref[SUMS : SUMS + 8, :],
+        lambda at: edge_ref[8 + at : 9 + at, :], lambda at: back_ref[SUMS + 8 + at : SUMS + 9 + at, :],
+    )
+    copies = [pltpu.make_async_copy(out_ref.at[k], out_hbm.at[k], sems.at[k]) for k in range(COMP)]
+    for k in range(COMP):
+        for level in range(LEV):
+            for b in range(BLOCKS):
+                rows = slice(8 * b, 8 * b + 8)
+                value = base_ref[k, level, rows, :] + arrived(k, level, b)
+                if level == 0:
+                    at = ROWS * k + 8 * b
+                    value = value + (part_ref[k, rows, :] + back_ref[at : at + 8, :])
+                out_ref[k, level, rows, :] = value
+        copies[k].start()
+    for copy in copies:
+        copy.wait()
 
 
 def call(kernel, arrays, outs, scratch=(), space=pltpu.VMEM, out_space=pltpu.VMEM, cost=1 << 20):
@@ -491,11 +494,12 @@
     base, centre = call(
         second_inner_kernel, (base, top, dif, vel, give, near, flux, *arrived), [field.shape, surface], scratch
     )
-    back, edge = call(second_turn_kernel, (lon, lat, base), [(KEEP, LANES), (8 + PLANES, LANES)])
+    (sums,) = call(passed_kernel, (near, lon), [(SUMS + 8, LANES)])
+    back, edge = call(second_turn_kernel, (sums, lon, lat, base), [(SUMS + 8 + PLANES, LANES), (8 + PLANES, LANES)])
     back = lax.ppermute(back, "sec", swap)
     (part,) = call(second_kept_kernel, (give, lon, centre), [surface])
-    scratch = [pltpu.VMEM(field.shape, jnp.float32), pltpu.SemaphoreType.DMA((2,))]
-    (field,) = call(last_kernel, (base, part, give, edge, back), [field.shape], scratch, out_space=pltpu.HBM)
+    scratch = [pltpu.VMEM(field.shape, jnp.float32), pltpu.SemaphoreType.DMA((COMP,))]
+    (field,) = call(last_kernel, (base, part, edge, back), [field.shape], scratch, out_space=pltpu.HBM)
     return field[None]
 
 

time: 42.8 us -> 42.9 us (level)
  starting transfers between devices: 22.2 us -> 22.9 us
  waiting for transfers between devices: 9.98 us -> 9.37 us
    ppermute x2, starting transfers between devices: 4.21 us -> 4.9 us  [on_device(): back = lax.ppermute(back, 'sec', swap)]
    ppermute x2, waiting for transfers between devices: 9.2 us -> 8.52 us  [on_device(): lat = lax.ppermute(lat, ('sec', 'lat'), routes('lat'))]
    pallas_call x11 -> x12, Pallas kernels: 10.2 us -> 10.3 us  [call(): pl.pallas_call(kernel, out_shape=[jax.ShapeDtypeStruct(shape, jnp.float32...]
  transfers between devices with their start and end apart: 7 -> 7, of which waited for: 4 -> 4; matrix products, arithmetic and copies ran while one was open for 0% -> 0% of each run, Pallas kernels for 12% -> 13%
where the time goes in v8:
time: 42.9 us; the launch traced here: 42.7 us
  starting transfers between devices  22.9 us (53%)
  Pallas kernels  10.3 us (24%)
  waiting for transfers between devices  9.37 us (22%)
    pallas_call x12, Pallas kernels, call(): pl.pallas_call(kernel, out_shape=[jax.ShapeDtypeStruct(shape, jnp.float32...  10.3 us
    ppermute x1, starting transfers between devices, on_device(): near = lax.ppermute(give, 'sec', swap)  8.79 us
    ppermute x2, waiting for transfers between devices, on_device(): lat = lax.ppermute(lat, ('sec', 'lat'), routes('lat'))  8.52 us
    ppermute x2, starting transfers between devices, on_device(): lon = lax.ppermute(lon, ('sec', 'lon'), routes('lon'))  6.59 us
    ppermute x2, starting transfers between devices, on_device(): back = lax.ppermute(back, 'sec', swap)  4.9 us
    ppermute x2, starting transfers between devices, on_device(): lat = lax.ppermute(lat, ('sec', 'lat'), routes('lat'))  2.58 us
  transfers between devices with their start and end apart: 7, of which 4 were waited for; matrix products, arithmetic and copies ran while one was open for 0% of the time, Pallas kernels for 13%

profile of v8, /device:TPU:1, one launch (start us, length us, event | category | flops | bytes accessed | tf_op | source)
XLA Modules:
  0.0 42.7 jit_solution(11364100465635146013)
XLA Ops:
  0.0 0.0 copy-start
  0.0 0.0 copy-start.1
  0.0 0.0 copy-start.2
  0.0 1.7 %shard_map.91 = (f32[632,128]{1,0:T(8,128)S(1)}, f32[4,32,128]{2,1,0:T(8,128)S(1)}) custom-call(f32[4,4]{1,0:T(4,128)} %bitcast.23, f32[4,4,32,128]{3,2,1,0:T(8,128)} %bitcast.13, f32[4,32,128]{2,1,0:T(8,128)} %bitcast.15, f32[2,4,32,128]{3,2,1,0:T(8,128)} %bitcast.10, s32[32,128]{1,0:T(8,128)} %bitcast.20, s32[32,128]{1,0:T(8,128)} %bitcast.21, ...), custom_call_target="tpu_custom_call" | custom-call | flops 1048576 | bytes 1048576 | tf_op jit(solution)/shard_map/pallas_call | solution.py:422
  1.7 8.8 %collective-permute-start = (f32[632,128]{1,0:T(8,128)S(1)}, f32[632,128]{1,0:T(8,128)S(1)}, u32[]{:S(2)}, u32[]{:S(2)}) collective-permute-start(f32[632,128]{1,0:T(8,128)S(1)} %get-tuple-element.26.give_ref), channel_id=1, source_target_pairs={{0,256},{256,0},{1,257},{257,1},{2,258},{258,2},{3,259},{259,3},{4... | collective-permute-start | bytes 970760 | tf_op jit(solution)/shard_map/ppermute | solution.py:470
  10.5 0.0 copy-done
  10.5 0.0 copy-done.1
  10.5 0.0 copy-done.2
  10.5 0.6 %shard_map.92 = (f32[56,128]{1,0:T(8,128)S(1)}, f32[4,4,32,128]{3,2,1,0:T(8,128)S(1)}, f32[48,128]{1,0:T(8,128)S(1)}, f32[48,128]{1,0:T(8,128)S(1)}) custom-call(f32[4,4,32,128]{3,2,1,0:T(8,128)S(1)} %bitcast.14, f32[4,32,128]{2,1,0:T(8,128)S(1)} %bitcast.16, f32[2,4,32,128]{3,2,1,0:T(8,128)S(1)} %bitcast.11, f32[632,128]{1,0:T(8,128)S(1)} %get-tuple-element.26.give_ref, ...), custom_call_target="tpu_custom_call" | custom-call | flops 1048576 | bytes 1048576 | tf_op jit(solution)/shard_map/pallas_call | solution.py:422
  11.1 0.6 %collective-permute-done.near_ref = f32[632,128]{1,0:T(8,128)S(1)} collective-permute-done((f32[632,128]{1,0:T(8,128)S(1)}, f32[632,128]{1,0:T(8,128)S(1)}, u32[]{:S(2)}, u32[]{:S(2)}) %collective-permute-start) | collective-permute-done | bytes 323616 | tf_op jit(solution)/shard_map/ppermute | solution.py:470
  11.7 3.7 %collective-permute-start.1 = (f32[80,128]{1,0:T(8,128)S(1)}, f32[80,128]{1,0:T(8,128)S(1)}, u32[]{:S(2)}, u32[]{:S(2)}) collective-permute-start(f32[80,128]{1,0:T(8,128)S(1)} %get-tuple-element.30), channel_id=1, source_target_pairs={{0,1},{256,319},{1,2},{257,256},{2,3},{258,257},{3,4},{259,258},{4... | collective-permute-start | bytes 122888 | tf_op jit(solution)/shard_map/ppermute | solution.py:476
  15.4 1.3 %collective-permute-start.2 = (f32[32,128]{1,0:T(8,128)S(1)}, f32[32,128]{1,0:T(8,128)S(1)}, u32[]{:S(2)}, u32[]{:S(2)}) collective-permute-start(f32[32,128]{1,0:T(8,128)S(1)} %get-tuple-element.37), channel_id=1, source_target_pairs={{0,64},{64,128},{320,256},{128,192},{384,320},{448,384},{1,65},{65... | collective-permute-start | bytes 49160 | tf_op jit(solution)/shard_map/ppermute | solution.py:477
  16.7 1.3 %shard_map.94 = (f32[4,32,128]{2,1,0:T(8,128)S(1)}, f32[4,32,128]{2,1,0:T(8,128)S(1)}, f32[4,32,128]{2,1,0:T(8,128)S(1)}) custom-call(f32[632,128]{1,0:T(8,128)S(1)} %get-tuple-element.26.give_ref, f32[632,128]{1,0:T(8,128)S(1)} %collective-permute-done.near_ref), custom_call_target="tpu_custom_call" | custom-call | flops 1048576 | bytes 1048576 | tf_op jit(solution)/shard_map/pallas_call | solution.py:422
  18.0 4.3 %collective-permute-done.2.lat_ref = f32[32,128]{1,0:T(8,128)S(1)} collective-permute-done((f32[32,128]{1,0:T(8,128)S(1)}, f32[32,128]{1,0:T(8,128)S(1)}, u32[]{:S(2)}, u32[]{:S(2)}) %collective-permute-start.2) | collective-permute-done | bytes 16416 | tf_op jit(solution)/shard_map/ppermute | solution.py:477
  22.4 0.0 collective-permute-done.1.lon_ref
  22.4 1.9 %collective-permute-start.3 = (f32[160,128]{1,0:T(8,128)S(1)}, f32[160,128]{1,0:T(8,128)S(1)}, u32[]{:S(2)}, u32[]{:S(2)}) collective-permute-start(f32[160,128]{1,0:T(8,128)S(1)} %shard_map.96), channel_id=1, source_target_pairs={{0,256},{256,0},{1,257},{257,1},{2,258},{258,2},{3,259},{259,3},{4... | collective-permute-start | bytes 245768 | tf_op jit(solution)/shard_map/ppermute | solution.py:480
  24.3 1.3 %shard_map.95 = (f32[4,32,128]{2,1,0:T(8,128)S(1)}, f32[4,32,128]{2,1,0:T(8,128)S(1)}) custom-call(f32[632,128]{1,0:T(8,128)S(1)} %get-tuple-element.26.give_ref, f32[632,128]{1,0:T(8,128)S(1)} %collective-permute-done.near_ref, f32[80,128]{1,0:T(8,128)S(1)} %collective-permute-done.1.lon_ref, f32[4,32,128]{2,1,0:T(8,128)S(1)} %get-tuple-element.31.centre_ref, ...), custom_call_target="tpu_custom_call" | custom-call | flops 1048576 | bytes 1048576 | tf_op jit(solution)/shard_map/pallas_call | solution.py:422
  25.6 0.0 collective-permute-done.3.back_ref
  25.6 2.0 %shard_map.97 = (f32[4,32,128]{2,1,0:T(8,128)S(1)}, f32[80,128]{1,0:T(8,128)S(1)}, f32[32,128]{1,0:T(8,128)S(1)}, f32[4,32,128]{2,1,0:T(8,128)S(1)}) custom-call(f32[4,4,32,128]{3,2,1,0:T(8,128)S(1)} %get-tuple-element.28.base_ref.before_ref, f32[4,32,128]{2,1,0:T(8,128)S(1)} %get-tuple-element.33.part_ref, ...), custom_call_target="tpu_custom_call" | custom-call | flops 1048576 | bytes 1048576 | tf_op jit(solution)/shard_map/pallas_call | solution.py:422
  27.6 2.9 %collective-permute-start.4 = (f32[80,128]{1,0:T(8,128)S(1)}, f32[80,128]{1,0:T(8,128)S(1)}, u32[]{:S(2)}, u32[]{:S(2)}) collective-permute-start(f32[80,128]{1,0:T(8,128)S(1)} %get-tuple-element.42), channel_id=1, source_target_pairs={{0,1},{256,319},{1,2},{257,256},{2,3},{258,257},{3,4},{259,258},{4... | collective-permute-start | bytes 122888 | tf_op jit(solution)/shard_map/ppermute | solution.py:491
  30.5 1.3 %collective-permute-start.5 = (f32[32,128]{1,0:T(8,128)S(1)}, f32[32,128]{1,0:T(8,128)S(1)}, u32[]{:S(2)}, u32[]{:S(2)}) collective-permute-start(f32[32,128]{1,0:T(8,128)S(1)} %get-tuple-element.44), channel_id=1, source_target_pairs={{0,64},{64,128},{320,256},{128,192},{384,320},{448,384},{1,65},{65... | collective-permute-start | bytes 49160 | tf_op jit(solution)/shard_map/ppermute | solution.py:492
  31.8 1.2 %shard_map.98 = (f32[4,4,32,128]{3,2,1,0:T(8,128)S(1)}, f32[4,32,128]{2,1,0:T(8,128)S(1)}) custom-call(f32[4,4,32,128]{3,2,1,0:T(8,128)S(1)} %get-tuple-element.28.base_ref.before_ref, f32[4,32,128]{2,1,0:T(8,128)S(1)} %get-tuple-element.39.surface_ref, f32[4,32,128]{2,1,0:T(8,128)S(1)} %bitcast.17, f32[2,4,32,128]{3,2,1,0:T(8,128)S(1)} %bitcast.12, ...), custom_call_target="tpu_custom_call" | custom-call | flops 1048576 | bytes 1048576 | tf_op jit(solution)/shard_map/pallas_call | solution.py:422
  32.9 0.0 collective-permute-done.4.lon_ref
  33.0 0.7 %shard_map.100.sum_ref = f32[136,128]{1,0:T(8,128)S(1)} custom-call(f32[632,128]{1,0:T(8,128)S(1)} %collective-permute-done.near_ref, f32[80,128]{1,0:T(8,128)S(1)} %collective-permute-done.4.lon_ref), custom_call_target="tpu_custom_call" | custom-call | flops 1048576 | bytes 1048576 | tf_op jit(solution)/shard_map/pallas_call | solution.py:422
  33.6 4.2 %collective-permute-done.5.lat_ref = f32[32,128]{1,0:T(8,128)S(1)} collective-permute-done((f32[32,128]{1,0:T(8,128)S(1)}, f32[32,128]{1,0:T(8,128)S(1)}, u32[]{:S(2)}, u32[]{:S(2)}) %collective-permute-start.5) | collective-permute-done | bytes 16416 | tf_op jit(solution)/shard_map/ppermute | solution.py:492
  37.8 3.0 %collective-permute-start.6 = (f32[152,128]{1,0:T(8,128)S(1)}, f32[152,128]{1,0:T(8,128)S(1)}, u32[]{:S(2)}, u32[]{:S(2)}) collective-permute-start(f32[152,128]{1,0:T(8,128)S(1)} %get-tuple-element.46), channel_id=1, source_target_pairs={{0,256},{256,0},{1,257},{257,1},{2,258},{258,2},{3,259},{259,3},{4... | collective-permute-start | bytes 233480 | tf_op jit(solution)/shard_map/ppermute | solution.py:499
  40.8 0.7 %shard_map.99.part_ref = f32[4,32,128]{2,1,0:T(8,128)S(1)} custom-call(f32[632,128]{1,0:T(8,128)S(1)} %get-tuple-element.26.give_ref, f32[80,128]{1,0:T(8,128)S(1)} %collective-permute-done.4.lon_ref, f32[4,32,128]{2,1,0:T(8,128)S(1)} %get-tuple-element.43.centre_ref), custom_call_target="tpu_custom_call" | custom-call | flops 1048576 | bytes 1048576 | tf_op jit(solution)/shard_map/pallas_call | solution.py:422
  41.5 0.2 collective-permute-done.6.back_ref
  41.7 1.0 %shard_map.102 = f32[4,4,32,128]{3,2,1,0:T(8,128)} custom-call(f32[4,4,32,128]{3,2,1,0:T(8,128)S(1)} %get-tuple-element.41.base_ref, f32[4,32,128]{2,1,0:T(8,128)S(1)} %shard_map.99.part_ref, f32[24,128]{1,0:T(8,128)S(1)} %get-tuple-element.45.edge_ref, f32[152,128]{1,0:T(8,128)S(1)} %collective-permute-done.6.back_ref), custom_call_target="tpu_custom_call" | custom-call | flops 1048576 | bytes 1048576 | tf_op jit(solution)/shard_map/pallas_call | solution.py:422
  (3 shorter events, 0.0 us)
Async XLA Ops:
  0.0 10.5 %copy-start = (f32[1,2,4,32,128]{4,3,2,1,0:T(8,128)S(1)}, f32[1,2,4,32,128]{4,3,2,1,0:T(8,128)}, u32[]{:S(2)}) copy-start(f32[1,2,4,32,128]{4,3,2,1,0:T(8,128)} %param.11) | copy-start | bytes 393220
  0.0 10.5 %copy-start.1 = (f32[1,4,4,32,128]{4,3,2,1,0:T(8,128)S(1)}, f32[1,4,4,32,128]{4,3,2,1,0:T(8,128)}, u32[]{:S(2)}) copy-start(f32[1,4,4,32,128]{4,3,2,1,0:T(8,128)} %param.9) | copy-start | bytes 786436
  0.0 10.5 %copy-start.2 = (f32[1,4,32,128]{3,2,1,0:T(8,128)S(1)}, f32[1,4,32,128]{3,2,1,0:T(8,128)}, u32[]{:S(2)}) copy-start(f32[1,4,32,128]{3,2,1,0:T(8,128)} %param.10) | copy-start | bytes 196612
  1.7 10.0 %collective-permute-start = (f32[632,128]{1,0:T(8,128)S(1)}, f32[632,128]{1,0:T(8,128)S(1)}, u32[]{:S(2)}, u32[]{:S(2)}) collective-permute-start(f32[632,128]{1,0:T(8,128)S(1)} %get-tuple-element.26.give_ref), channel_id=1, source_target_pairs={{0,256},{256,0},{1,257},{257,1},{2,258},{258,2},{3,259},{259,3},{4... | collective-permute-start | bytes 970760 | tf_op jit(solution)/shard_map/ppermute | solution.py:470
  11.7 10.7 %collective-permute-start.1 = (f32[80,128]{1,0:T(8,128)S(1)}, f32[80,128]{1,0:T(8,128)S(1)}, u32[]{:S(2)}, u32[]{:S(2)}) collective-permute-start(f32[80,128]{1,0:T(8,128)S(1)} %get-tuple-element.30), channel_id=1, source_target_pairs={{0,1},{256,319},{1,2},{257,256},{2,3},{258,257},{3,4},{259,258},{4... | collective-permute-start | bytes 122888 | tf_op jit(solution)/shard_map/ppermute | solution.py:476
  15.4 6.9 %collective-permute-start.2 = (f32[32,128]{1,0:T(8,128)S(1)}, f32[32,128]{1,0:T(8,128)S(1)}, u32[]{:S(2)}, u32[]{:S(2)}) collective-permute-start(f32[32,128]{1,0:T(8,128)S(1)} %get-tuple-element.37), channel_id=1, source_target_pairs={{0,64},{64,128},{320,256},{128,192},{384,320},{448,384},{1,65},{65... | collective-permute-start | bytes 49160 | tf_op jit(solution)/shard_map/ppermute | solution.py:477
  22.4 3.2 %collective-permute-start.3 = (f32[160,128]{1,0:T(8,128)S(1)}, f32[160,128]{1,0:T(8,128)S(1)}, u32[]{:S(2)}, u32[]{:S(2)}) collective-permute-start(f32[160,128]{1,0:T(8,128)S(1)} %shard_map.96), channel_id=1, source_target_pairs={{0,256},{256,0},{1,257},{257,1},{2,258},{258,2},{3,259},{259,3},{4... | collective-permute-start | bytes 245768 | tf_op jit(solution)/shard_map/ppermute | solution.py:480
  27.6 5.4 %collective-permute-start.4 = (f32[80,128]{1,0:T(8,128)S(1)}, f32[80,128]{1,0:T(8,128)S(1)}, u32[]{:S(2)}, u32[]{:S(2)}) collective-permute-start(f32[80,128]{1,0:T(8,128)S(1)} %get-tuple-element.42), channel_id=1, source_target_pairs={{0,1},{256,319},{1,2},{257,256},{2,3},{258,257},{3,4},{259,258},{4... | collective-permute-start | bytes 122888 | tf_op jit(solution)/shard_map/ppermute | solution.py:491
  30.5 7.3 %collective-permute-start.5 = (f32[32,128]{1,0:T(8,128)S(1)}, f32[32,128]{1,0:T(8,128)S(1)}, u32[]{:S(2)}, u32[]{:S(2)}) collective-permute-start(f32[32,128]{1,0:T(8,128)S(1)} %get-tuple-element.44), channel_id=1, source_target_pairs={{0,64},{64,128},{320,256},{128,192},{384,320},{448,384},{1,65},{65... | collective-permute-start | bytes 49160 | tf_op jit(solution)/shard_map/ppermute | solution.py:492
  37.8 3.9 %collective-permute-start.6 = (f32[152,128]{1,0:T(8,128)S(1)}, f32[152,128]{1,0:T(8,128)S(1)}, u32[]{:S(2)}, u32[]{:S(2)}) collective-permute-start(f32[152,128]{1,0:T(8,128)S(1)} %get-tuple-element.46), channel_id=1, source_target_pairs={{0,256},{256,0},{1,257},{257,1},{2,258},{258,2},{3,259},{259,3},{4... | collective-permute-start | bytes 233480 | tf_op jit(solution)/shard_map/ppermute | solution.py:499
